TPU v7x, 256 devices: a whole 4x4x8 slice. The times are simulated.
256 devices in a mesh: dom: 128 (over x, y, z), feat: 2 (over core).
Axes of the slice: x: 4, y: 4, z: 8, core: 2. Of those that a mesh axis runs over, the one named last changes fastest.
Arguments:
- grad_out: bfloat16 [65536, 512], P('dom', 'feat'), may hold values from -6 to 6
- preact: bfloat16 [65536, 512], P('dom', 'feat'), may hold values from -6 to 6
- aggregated: bfloat16 [65536, 512], P('dom', 'feat'), may hold values from -6 to 6
- weight: bfloat16 [512, 512], P(None, 'feat'), may hold values from -0.1875 to 0.1875
- tiles: bfloat16 [8192, 128, 128], P('dom'), may hold values from -0.25 to 0.25
- in_block: int32 [8192], P('dom'), may hold values from 0 to 11
- out_block: int32 [8192], P('dom'), may hold values from 0 to 3
- tile_count: int32 [128], P('dom'), may hold values from 4 to 64, as said below
- send_rows: int32 [128, 128, 8], P('dom'), may hold values from 0 to 511
Outputs:
- adjoint: bfloat16 [65536, 512], P('dom', 'feat')
- grad_weight: float32 [512, 512], P(None, 'feat')
Inputs may be any that keep to these rules, and one draw needn't show every extreme that they name: Partition d uses its first tile_count[d] tile slots; some partition uses all 64.
All inputs are finite; a program needn't handle non-finite values.
Results may differ from a plain program's by a relative error of at most 0.014.
Values may be sent and summed in bfloat16 or wider, within the bound.
No kernel may reach another device: no remote copies, remote signals or barrier semaphores. Data moves between devices by JAX's collectives and lax.ppermute only.
A program may use at most 64 MiB of HBM per device.

v0:
```python
import math

import jax
import jax.numpy as jnp
from jax import lax
from jax.sharding import PartitionSpec as P

ITERS = 3


def tile_terms(tiles_part, inputs_part, outputs_part, live_part, ext_blocks, block_count):
    picked = jnp.take(ext_blocks, inputs_part, axis=0)
    product = jnp.einsum("tij,tjf->tif", tiles_part, picked, preferred_element_type=jnp.float32)
    product = product * live_part[:, None, None]
    start_blocks = jnp.zeros((block_count,) + product.shape[1:], jnp.float32)
    return start_blocks.at[outputs_part].add(product)


def shards(grad_out, preact, aggregated, weight, tiles, in_block, out_block, tile_count, send_rows):
    row_count, half_cols = grad_out.shape
    tile_size = tiles.shape[1]
    block_count = row_count // tile_size
    slot_count = tiles.shape[0]
    peer_count = lax.axis_size("dom")
    sent_rows = send_rows[0].reshape(-1)
    ghost_blocks = sent_rows.shape[0] // tile_size
    hyperbolic = jnp.tanh(preact.astype(jnp.float32))
    slope = 1.0 - hyperbolic * hyperbolic
    source = grad_out.astype(jnp.float32)
    count_here = tile_count[0]
    adjoint_state = source
    for iteration in range(ITERS):
        scaled = (slope * adjoint_state).astype(jnp.bfloat16)
        partial_sum = lax.dot_general(
            scaled, weight, (((1,), (1,)), ((), ())), preferred_element_type=jnp.float32
        )
        mixed_sum = lax.psum_scatter(
            partial_sum.astype(jnp.bfloat16), "feat", scatter_dimension=1, tiled=True
        )
        outgoing = jnp.take(mixed_sum, sent_rows, axis=0)
        ghosts = lax.all_to_all(outgoing, "dom", split_axis=0, concat_axis=0, tiled=True)
        ext_blocks = jnp.concatenate([mixed_sum, ghosts], 0).reshape(
            block_count + ghost_blocks, tile_size, half_cols
        )
        live_all = (jnp.arange(slot_count, dtype=jnp.int32) < count_here).astype(jnp.float32)
        gathered_sum = tile_terms(tiles, in_block, out_block, live_all, ext_blocks, block_count)
        adjoint_state = gathered_sum.reshape(row_count, half_cols) + source
    adjoint = adjoint_state.astype(jnp.bfloat16)
    pre_grad = (slope * adjoint_state).astype(jnp.bfloat16)
    local_grad = lax.dot_general(
        lax.all_gather(aggregated, "feat", axis=1, tiled=True),
        pre_grad,
        (((0,), (0,)), ((), ())),
        preferred_element_type=jnp.float32,
    )
    total_grad = lax.psum(local_grad, "dom")
    grad_weight = total_grad * jnp.float32(1.0 / math.sqrt(peer_count * row_count))
    return (adjoint, grad_weight)


def solution(mesh):
    placed = (
        P("dom", "feat"),
        P("dom", "feat"),
        P("dom", "feat"),
        P(None, "feat"),
        P("dom", None, None),
        P("dom"),
        P("dom"),
        P("dom"),
        P("dom", None, None),
    )
    return jax.shard_map(
        shards,
        mesh=mesh,
        in_specs=placed,
        out_specs=(P("dom", "feat"), P(None, "feat")),
        check_vma=False,
    )
```

profile of v0, /device:TPU:8, one launch (start us, length us, event | category | flops | bytes accessed | tf_op | source)
XLA Modules:
  0.0 487.6 jit_solution(859854375395738001)
XLA Ops:
  7.2 2.4 convolution_convert_fusion.2
  10.6 16.6 %reduce-scatter.4.cloned.1.call-done = bf16[512,256]{1,0:T(8,128)(2,1)} async-done(((bf16[512,512]{1,0:T(8,128)(2,1)}), bf16[512,256]{1,0:T(8,128)(2,1)}) %reduce-scatter.4.cloned.1.call-update) | async-done | bytes 262160 | tf_op jit(solution)/shard_map/reduce_scatter | solution.py:37
  27.2 4.5 gather_fusion
  32.7 13.7 %all-to-all-start = ((bf16[128,8,256]{2,1,0:T(8,128)(2,1)}), bf16[128,8,256]{2,1,0:T(8,128)(2,1)S(1)}, u32[]{:S(2)}, u32[]{:S(2)}) async-start(bf16[128,8,256]{2,1,0:T(8,128)(2,1)} %select_bitcast_fusion.2), calls=%async_computation.1 | async-start | bytes 1048576 | tf_op jit(solution)/shard_map/all_to_all | solution.py:41
  47.3 17.8 %all-to-all-done = bf16[128,8,256]{2,1,0:T(8,128)(2,1)S(1)} async-done(((bf16[128,8,256]{2,1,0:T(8,128)(2,1)}), bf16[128,8,256]{2,1,0:T(8,128)(2,1)S(1)}, u32[]{:S(2)}, u32[]{:S(2)}) %all-to-all-start) | async-done | bytes 524320 | tf_op jit(solution)/shard_map/all_to_all | solution.py:41
  65.9 1.1 pad_maximum_fusion
  67.0 2.8 gather_fusion.1
  69.8 7.3 %multiply_bitcast_fusion.2 = f32[64,128,256]{1,2,0:T(8,128)} fusion(f32[64]{0:T(128)S(1)} %get-tuple-element.11, bf16[64,128,128]{2,1,0:T(8,128)(2,1)S(1)} %copy-done, bf16[64,128,256]{2,1,0:T(8,128)(2,1)} %gather_fusion.1, pred[64]{0:T(512)(128)(4,1)S(1)} %get-tuple-element.10), kind=kOutput, calls=%fused_computation.11 | convolution fusion | flops 541065216 | bytes 14680384 | tf_op jit(solution)/shard_map/tij,tjf->tif/dot_general | solution.py:13
  77.0 9.0 %copy.17 = f32[64,128,256]{2,1,0:T(8,128)} copy(f32[64,128,256]{1,2,0:T(8,128)} %multiply_bitcast_fusion.2) | data formatting | bytes 16777216 | tf_op jit(solution)/shard_map/mul | solution.py:14
  86.1 12.3 %scatter_fusion = f32[4,128,256]{2,1,0:T(8,128)S(1)} fusion(f32[4,128,256]{2,1,0:T(8,128)S(1)} %broadcast.22.clone.1, s32[64]{0:T(128)S(1)} %compare_select_fusion.2, f32[64,128,256]{2,1,0:T(8,128)} %copy.17), kind=kCustom, calls=%fused_computation.6 | custom fusion | flops 2097152 | bytes 25166080 | tf_op jit(solution)/shard_map/scatter-add | solution.py:16
  98.6 1.1 convolution_convert_fusion.1
  99.8 9.1 %reduce-scatter.6.cloned.1.call-done = bf16[512,256]{1,0:T(8,128)(2,1)} async-done(((bf16[512,512]{1,0:T(8,128)(2,1)}), bf16[512,256]{1,0:T(8,128)(2,1)}) %reduce-scatter.6.cloned.1.call-update) | async-done | bytes 262160 | tf_op jit(solution)/shard_map/reduce_scatter | solution.py:37
  108.9 5.7 %gather_fusion.2 = bf16[1024,256]{1,0:T(8,128)(2,1)} fusion(bf16[512,256]{1,0:T(8,128)(2,1)} %reduce-scatter.6.cloned.1.call-done, s32[1024]{0:T(1024)S(1)} %fusion.26), kind=kCustom, calls=%fused_computation.2.clone | custom fusion | bytes 1052672 | tf_op jit(solution)/shard_map/jit(_take)/gather | solution.py:40
  114.5 1.2 select_bitcast_fusion.1
  115.8 32.2 %all_to_all.36 = bf16[128,8,256]{2,1,0:T(8,128)(2,1)S(1)} all-to-all(bf16[128,8,256]{2,1,0:T(8,128)(2,1)S(1)} %select_bitcast_fusion.1), channel_id=1, replica_groups=mesh['dom'=128,'feat'=2] {'dom'}, dimensions={0} | all-to-all | bytes 1048576 | tf_op jit(solution)/shard_map/all_to_all | solution.py:41
  148.0 2.8 gather_fusion.3
  150.8 7.3 %multiply_bitcast_fusion.1 = f32[64,128,256]{1,2,0:T(8,128)} fusion(f32[64]{0:T(128)S(1)} %get-tuple-element.11, bf16[64,128,128]{2,1,0:T(8,128)(2,1)S(1)} %copy-done, bf16[64,128,256]{2,1,0:T(8,128)(2,1)} %gather_fusion.3, pred[64]{0:T(512)(128)(4,1)S(1)} %get-tuple-element.10), kind=kOutput, calls=%fused_computation.10 | convolution fusion | flops 541065216 | bytes 14680384 | tf_op jit(solution)/shard_map/tij,tjf->tif/dot_general | solution.py:13
  158.1 9.0 %copy.19 = f32[64,128,256]{2,1,0:T(8,128)} copy(f32[64,128,256]{1,2,0:T(8,128)} %multiply_bitcast_fusion.1) | data formatting | bytes 16777216 | tf_op jit(solution)/shard_map/mul | solution.py:14
  167.1 12.3 %scatter_fusion.1 = f32[4,128,256]{2,1,0:T(8,128)S(1)} fusion(f32[4,128,256]{2,1,0:T(8,128)S(1)} %broadcast.22.clone, s32[64]{0:T(128)S(1)} %compare_select_fusion.2, f32[64,128,256]{2,1,0:T(8,128)} %copy.19), kind=kCustom, calls=%fused_computation.7 | custom fusion | flops 2097152 | bytes 25166080 | tf_op jit(solution)/shard_map/scatter-add | solution.py:16
  179.6 1.1 convolution_convert_fusion
  180.8 9.2 %reduce-scatter.8.cloned.1.call-done = bf16[512,256]{1,0:T(8,128)(2,1)} async-done(((bf16[512,512]{1,0:T(8,128)(2,1)}), bf16[512,256]{1,0:T(8,128)(2,1)}) %reduce-scatter.8.cloned.1.call-update) | async-done | bytes 262160 | tf_op jit(solution)/shard_map/reduce_scatter | solution.py:37
  189.9 4.5 gather_fusion.4
  195.5 13.7 %all-to-all-start.2 = ((bf16[128,8,256]{2,1,0:T(8,128)(2,1)}), bf16[128,8,256]{2,1,0:T(8,128)(2,1)S(1)}, u32[]{:S(2)}, u32[]{:S(2)}) async-start(bf16[128,8,256]{2,1,0:T(8,128)(2,1)} %select_bitcast_fusion), calls=%async_computation.5 | async-start | bytes 1048576 | tf_op jit(solution)/shard_map/all_to_all | solution.py:41
  209.3 2.3 all_gather.3
  211.6 16.2 %all-to-all-done.2 = bf16[128,8,256]{2,1,0:T(8,128)(2,1)S(1)} async-done(((bf16[128,8,256]{2,1,0:T(8,128)(2,1)}), bf16[128,8,256]{2,1,0:T(8,128)(2,1)S(1)}, u32[]{:S(2)}, u32[]{:S(2)}) %all-to-all-start.2) | async-done | bytes 524320 | tf_op jit(solution)/shard_map/all_to_all | solution.py:41
  228.6 1.1 pad_maximum_fusion.2
  229.7 2.8 gather_fusion.5
  232.5 7.3 %multiply_bitcast_fusion = f32[64,128,256]{1,2,0:T(8,128)} fusion(f32[64]{0:T(128)S(1)} %get-tuple-element.11, bf16[64,128,128]{2,1,0:T(8,128)(2,1)S(1)} %copy-done, bf16[64,128,256]{2,1,0:T(8,128)(2,1)} %gather_fusion.5, pred[64]{0:T(512)(128)(4,1)S(1)} %get-tuple-element.10), kind=kOutput, calls=%fused_computation.9 | convolution fusion | flops 541065216 | bytes 14680384 | tf_op jit(solution)/shard_map/tij,tjf->tif/dot_general | solution.py:13
  239.8 9.0 %copy.21 = f32[64,128,256]{2,1,0:T(8,128)} copy(f32[64,128,256]{1,2,0:T(8,128)} %multiply_bitcast_fusion) | data formatting | bytes 16777216 | tf_op jit(solution)/shard_map/mul | solution.py:14
  248.8 12.3 %scatter_fusion.2 = f32[4,128,256]{2,1,0:T(8,128)S(1)} fusion(f32[4,128,256]{2,1,0:T(8,128)S(1)} %broadcast.22, s32[64]{0:T(128)S(1)} %compare_select_fusion.2, f32[64,128,256]{2,1,0:T(8,128)} %copy.21), kind=kCustom, calls=%fused_computation.8 | custom fusion | flops 2097152 | bytes 25166080 | tf_op jit(solution)/shard_map/scatter-add | solution.py:16
  261.9 2.2 convolution_bitcast_fusion
  264.1 214.8 %all-reduce.2.cloned.1.call-done = f32[512,256]{0,1:T(8,128)} async-done(((f32[512,256]{0,1:T(8,128)}), f32[512,256]{0,1:T(8,128)}) %all-reduce.2.cloned.1.call-update) | async-done | bytes 524304 | tf_op jit(solution)/shard_map/psum | solution.py:56
  (57 shorter events, 8.1 us)
Async XLA Ops:
  7.2 62.6 %copy-start = (bf16[64,128,128]{2,1,0:T(8,128)(2,1)S(1)}, bf16[64,128,128]{2,1,0:T(8,128)(2,1)}, u32[]{:S(2)}) copy-start(bf16[64,128,128]{2,1,0:T(8,128)(2,1)} %param.17) | copy-start | bytes 6291460
  7.2 40.0 %copy-start.13 = (s32[64]{0:T(128)S(1)}, s32[64]{0:T(128)}, u32[]{:S(2)}) copy-start(s32[64]{0:T(128)} %param.18) | copy-start | bytes 772
  7.2 40.0 %copy-start.14 = (s32[64]{0:T(128)S(1)}, s32[64]{0:T(128)}, u32[]{:S(2)}) copy-start(s32[64]{0:T(128)} %param.19) | copy-start | bytes 772
  7.2 20.0 %reduce-scatter.4.cloned.1.call-start = ((), (), s32[]{:S(2)}) async-start(), calls=%async_computation.6 | async-start | bytes 786432 | tf_op jit(solution)/shard_map/reduce_scatter | solution.py:37
  27.2 38.7 %copy-start.1 = (bf16[512,256]{1,0:T(8,128)(2,1)S(1)}, bf16[512,256]{1,0:T(8,128)(2,1)}, u32[]{:S(2)}) copy-start(bf16[512,256]{1,0:T(8,128)(2,1)} %reduce-scatter.4.cloned.1.call-done) | copy-start | bytes 786436
  32.7 32.4 %all-to-all-start = ((bf16[128,8,256]{2,1,0:T(8,128)(2,1)}), bf16[128,8,256]{2,1,0:T(8,128)(2,1)S(1)}, u32[]{:S(2)}, u32[]{:S(2)}) async-start(bf16[128,8,256]{2,1,0:T(8,128)(2,1)} %select_bitcast_fusion.2), calls=%async_computation.1 | async-start | bytes 1048576 | tf_op jit(solution)/shard_map/all_to_all | solution.py:41
  46.5 62.4 %reduce-scatter.6.cloned.1.call-start = ((), (), s32[]{:S(2)}) async-start(), calls=%async_computation.7 | async-start | bytes 786432 | tf_op jit(solution)/shard_map/reduce_scatter | solution.py:37
  65.1 0.8 copy-start.10
  86.1 12.4 %copy-start.4 = (bf16[512,256]{1,0:T(8,128)(2,1)S(1)}, bf16[512,256]{1,0:T(8,128)(2,1)}, u32[]{:S(2)}) copy-start(bf16[512,256]{1,0:T(8,128)(2,1)} %param.14) | copy-start | bytes 786436
  86.1 12.4 %copy-start.5 = (bf16[512,256]{1,0:T(8,128)(2,1)S(1)}, bf16[512,256]{1,0:T(8,128)(2,1)}, u32[]{:S(2)}) copy-start(bf16[512,256]{1,0:T(8,128)(2,1)} %param.13) | copy-start | bytes 786436
  86.1 12.5 %copy-start.8 = (bf16[512,256]{1,0:T(8,128)(2,1)S(1)}, bf16[512,256]{1,0:T(8,128)(2,1)}, u32[]{:S(2)}) copy-start(bf16[512,256]{1,0:T(8,128)(2,1)} %param.16) | copy-start | bytes 786436
  99.7 90.2 %reduce-scatter.8.cloned.1.call-start = ((), (), s32[]{:S(2)}) async-start(), calls=%async_computation.8 | async-start | bytes 786432 | tf_op jit(solution)/shard_map/reduce_scatter | solution.py:37
  108.9 39.1 %copy-start.3 = (bf16[512,256]{1,0:T(8,128)(2,1)S(1)}, bf16[512,256]{1,0:T(8,128)(2,1)}, u32[]{:S(2)}) copy-start(bf16[512,256]{1,0:T(8,128)(2,1)} %reduce-scatter.6.cloned.1.call-done) | copy-start | bytes 786436
  167.1 12.3 %copy-start.6 = (bf16[512,256]{1,0:T(8,128)(2,1)S(1)}, bf16[512,256]{1,0:T(8,128)(2,1)}, u32[]{:S(2)}) copy-start(bf16[512,256]{1,0:T(8,128)(2,1)} %param.13) | copy-start | bytes 786436
  167.1 12.5 %copy-start.9 = (bf16[512,256]{1,0:T(8,128)(2,1)S(1)}, bf16[512,256]{1,0:T(8,128)(2,1)}, u32[]{:S(2)}) copy-start(bf16[512,256]{1,0:T(8,128)(2,1)} %param.16) | copy-start | bytes 786436
  180.7 28.5 %copy-start.12 = (bf16[512,256]{1,0:T(8,128)(2,1)S(1)}, bf16[512,256]{1,0:T(8,128)(2,1)}, u32[]{:S(2)}) copy-start(bf16[512,256]{1,0:T(8,128)(2,1)} %param.15) | copy-start | bytes 786436
  189.9 38.7 %copy-start.2 = (bf16[512,256]{1,0:T(8,128)(2,1)S(1)}, bf16[512,256]{1,0:T(8,128)(2,1)}, u32[]{:S(2)}) copy-start(bf16[512,256]{1,0:T(8,128)(2,1)} %reduce-scatter.8.cloned.1.call-done) | copy-start | bytes 786436
  195.5 32.4 %all-to-all-start.2 = ((bf16[128,8,256]{2,1,0:T(8,128)(2,1)}), bf16[128,8,256]{2,1,0:T(8,128)(2,1)S(1)}, u32[]{:S(2)}, u32[]{:S(2)}) async-start(bf16[128,8,256]{2,1,0:T(8,128)(2,1)} %select_bitcast_fusion), calls=%async_computation.5 | async-start | bytes 1048576 | tf_op jit(solution)/shard_map/all_to_all | solution.py:41
  209.2 269.8 %all-reduce.2.cloned.1.call-start = ((), (), s32[]{:S(2)}) async-start(), calls=%async_computation.9 | async-start | bytes 1048576 | tf_op jit(solution)/shard_map/psum | solution.py:56
  227.8 0.8 copy-start.11
  248.8 12.3 %copy-start.7 = (bf16[512,256]{1,0:T(8,128)(2,1)S(1)}, bf16[512,256]{1,0:T(8,128)(2,1)}, u32[]{:S(2)}) copy-start(bf16[512,256]{1,0:T(8,128)(2,1)} %param.13) | copy-start | bytes 786436
Sparse Core Ops, SparseCore 0:
  11.1 16.0 reduce-scatter.3
  99.9 8.9 reduce-scatter.5
  180.9 9.0 reduce-scatter.7
  264.2 214.6 all-reduce.1
where the time goes:
time: 489 us; the launch traced here: 488 us
  waiting for transfers between devices  284 us (58%)
  local copies, waits for them, and re-layouts  53.6 us (11%)
  other arithmetic  44.6 us (9%)
  blocking collectives  34.5 us (7%)
  matrix products  28.6 us (6%)
  starting transfers between devices  27.6 us (6%)
  between operations  14.7 us (3%)
    psum x1, waiting for transfers between devices, shards(): total_grad = lax.psum(local_grad, 'dom')  215 us
    scatter-add x3, other arithmetic, tile_terms(): return start_blocks.at[outputs_part].add(product)  36.9 us
    reduce_scatter x3, waiting for transfers between devices, shards(): lax.psum_scatter(partial_sum.astype(jnp.bfloat16), 'feat', scatter_dimens...  34.9 us
    all_to_all x2, waiting for transfers between devices, shards(): lax.all_to_all(outgoing, 'dom', split_axis=0, concat_axis=0, tiled=True)  34.1 us
    all_to_all x1, blocking collectives, shards(): lax.all_to_all(outgoing, 'dom', split_axis=0, concat_axis=0, tiled=True)  32.2 us
    all_to_all x2, starting transfers between devices, shards(): lax.all_to_all(outgoing, 'dom', split_axis=0, concat_axis=0, tiled=True)  27.5 us
    mul x3, local copies, waits for them, and re-layouts, tile_terms(): product = product * live_part[:, None, None]  26.9 us
    dot_general x3, matrix products, tile_terms(): jnp.einsum('tij,tjf->tif', tiles_part, picked, preferred_element_type=jnp...  21.8 us
  transfers between devices with their start and end apart: 6, of which 6 were waited for; matrix products, arithmetic and copies ran while one was open for 0% of the time, Pallas kernels for 0%

commit v1 on v0

v1 whole, which is shorter than its diff:
```python
import math

import jax
import jax.numpy as jnp
from jax import lax
from jax.experimental import pallas as pl
from jax.experimental.pallas import tpu as pltpu
from jax.sharding import PartitionSpec as P

ITERS = 3
BF16 = jnp.bfloat16
F32 = jnp.float32
VMEM = pl.BlockSpec(memory_space=pltpu.VMEM)
SMEM = pl.BlockSpec(memory_space=pltpu.SMEM)
SWAP = ((0, 1), (1, 0))


def params(mib):
    return pltpu.CompilerParams(vmem_limit_bytes=mib << 20)


def dot(a, b, dims=((1,), (0,))):
    return lax.dot_general(a, b, (dims, ((), ())), preferred_element_type=F32)


def densify_kernel(count, inputs, outputs, tiles, dense, total):
    in_blocks = dense.shape[1] // tiles.shape[1]
    out_blocks = dense.shape[0] // tiles.shape[1]
    size = tiles.shape[1]
    total[...] = jnp.zeros_like(total)

    def step(slot, carry):
        place = outputs[slot] * in_blocks + inputs[slot]
        total[place] += tiles[slot].astype(F32)
        return carry

    lax.fori_loop(0, count[0], step, 0)
    for out in range(out_blocks):
        for inp in range(in_blocks):
            dense[out * size:(out + 1) * size, inp * size:(inp + 1) * size] = total[
                out * in_blocks + inp
            ].astype(BF16)


def densify(count, inputs, outputs, tiles, out_blocks, in_blocks):
    size = tiles.shape[1]
    return pl.pallas_call(
        densify_kernel,
        out_shape=jax.ShapeDtypeStruct((out_blocks * size, in_blocks * size), BF16),
        in_specs=[SMEM, SMEM, SMEM, VMEM],
        out_specs=VMEM,
        scratch_shapes=[pltpu.VMEM((out_blocks * in_blocks, size, size), F32)],
        compiler_params=params(16),
        cost_estimate=pl.CostEstimate(flops=1 << 22, bytes_accessed=4 << 20, transcendentals=0),
        name="densify",
    )(count, inputs, outputs, tiles)


def mix_kernel(own, other, own_w, other_w, pick, mixed, outgoing):
    value = dot(own[...], own_w[...], ((1,), (1,))) + dot(other[...], other_w[...], ((1,), (1,)))
    value = value.astype(BF16)
    mixed[...] = value
    outgoing[...] = dot(pick[...], value).astype(BF16)


def mix(own, other, own_w, other_w, pick):
    rows, cols = own.shape
    return pl.pallas_call(
        mix_kernel,
        out_shape=(
            jax.ShapeDtypeStruct((rows, cols), BF16),
            jax.ShapeDtypeStruct((pick.shape[0], cols), BF16),
        ),
        in_specs=[VMEM] * 5,
        out_specs=(VMEM, VMEM),
        compiler_params=params(16),
        name="mix",
    )(own, other, own_w, other_w, pick)


def sweep_kernel(dense, mixed, ghosts, slope, source, scaled):
    rows = mixed.shape[0]
    state = dot(dense[:, :rows], mixed[...]) + dot(dense[:, rows:], ghosts[...])
    state = state + source[...].astype(F32)
    scaled[...] = (slope[...] * state).astype(BF16)


def sweep(dense, mixed, ghosts, slope, source):
    return pl.pallas_call(
        sweep_kernel,
        out_shape=jax.ShapeDtypeStruct(mixed.shape, BF16),
        in_specs=[VMEM] * 5,
        out_specs=VMEM,
        compiler_params=params(16),
        name="sweep",
    )(dense, mixed, ghosts, slope, source)


def last_kernel(half, dense, mixed, ghosts, slope, source, own, other, adjoint, pieces):
    rows, cols = mixed.shape
    state = dot(dense[:, :rows], mixed[...]) + dot(dense[:, rows:], ghosts[...])
    state = state + source[...].astype(F32)
    adjoint[...] = state.astype(BF16)
    pre_grad = (slope[...] * state).astype(BF16)
    count = pieces.shape[0] // 2
    for features, place in ((own, half[0]), (other, 1 - half[0])):
        part = dot(features[...], pre_grad, ((0,), (0,))).astype(BF16)
        for group in range(cols // 8):
            for side in range(cols // 128):
                pieces[place * count + group * (cols // 128) + side] = part[
                    group * 8:group * 8 + 8, side * 128:side * 128 + 128
                ]


def last(half, dense, mixed, ghosts, slope, source, own, other):
    rows, cols = mixed.shape
    return pl.pallas_call(
        last_kernel,
        out_shape=(
            jax.ShapeDtypeStruct((rows, cols), BF16),
            jax.ShapeDtypeStruct((2 * cols * cols // 1024, 8, 128), BF16),
        ),
        in_specs=[SMEM] + [VMEM] * 7,
        out_specs=(VMEM, VMEM),
        compiler_params=params(24),
        name="last",
    )(half, dense, mixed, ghosts, slope, source, own, other)


def total_kernel(scale, terms, spread):
    value = jnp.sum(terms[...].astype(F32), axis=0) * scale
    spread[...] = jnp.broadcast_to(value.astype(BF16)[None], spread.shape)


def unpack_kernel(pieces, grad):
    sides = grad.shape[1] // 128
    for piece in range(pieces.shape[0]):
        group, side = divmod(piece, sides)
        grad[group * 8:group * 8 + 8, side * 128:side * 128 + 128] = pieces[piece].astype(F32)


def shards(grad_out, preact, aggregated, weight, tiles, in_block, out_block, tile_count, send_rows):
    rows, cols = grad_out.shape
    tile_size = tiles.shape[1]
    peers = lax.axis_size("dom")
    sent_rows = send_rows[0].reshape(-1)
    sent = sent_rows.shape[0]
    half = lax.axis_index("feat")
    own_w = lax.dynamic_slice_in_dim(weight, half * cols, cols, 0)
    away_w = lax.dynamic_slice_in_dim(weight, (1 - half) * cols, cols, 0)
    other_w = lax.ppermute(away_w, "feat", SWAP)
    pick = (sent_rows[:, None] == jnp.arange(rows, dtype=jnp.int32)[None, :]).astype(BF16)
    hyperbolic = jnp.tanh(preact.astype(F32))
    slope = 1.0 - hyperbolic * hyperbolic
    scaled = (slope * grad_out.astype(F32)).astype(BF16)
    dense = None
    for iteration in range(ITERS):
        other = lax.ppermute(scaled, "feat", SWAP)
        mixed, outgoing = mix(scaled, other, own_w, other_w, pick)
        ghosts = lax.all_to_all(
            outgoing.reshape(peers, sent // peers, cols), "dom", split_axis=0, concat_axis=0, tiled=True
        ).reshape(sent, cols)
        if dense is None:
            dense = densify(
                tile_count, in_block, out_block, tiles, rows // tile_size, (rows + sent) // tile_size
            )
        if iteration < ITERS - 1:
            scaled = sweep(dense, mixed, ghosts, slope, grad_out)
    other_agg = lax.ppermute(aggregated, "feat", SWAP)
    adjoint, pieces = last(
        half.reshape(1), dense, mixed, ghosts, slope, grad_out, aggregated, other_agg
    )
    terms = lax.all_to_all(pieces, "dom", split_axis=0, concat_axis=0, tiled=True)
    spread = pl.pallas_call(
        lambda *refs: total_kernel(1.0 / math.sqrt(peers * rows), *refs),
        out_shape=jax.ShapeDtypeStruct(pieces.shape, BF16),
        in_specs=[VMEM],
        out_specs=VMEM,
        compiler_params=params(16),
        name="total",
    )(terms)
    gathered = lax.all_to_all(spread, "dom", split_axis=0, concat_axis=0, tiled=True)
    grad_weight = pl.pallas_call(
        unpack_kernel,
        out_shape=jax.ShapeDtypeStruct((2 * cols, cols), F32),
        in_specs=[VMEM],
        out_specs=VMEM,
        compiler_params=params(16),
        name="unpack",
    )(gathered)
    return adjoint, grad_weight


def solution(mesh):
    placed = (
        P("dom", "feat"),
        P("dom", "feat"),
        P("dom", "feat"),
        P(None, "feat"),
        P("dom", None, None),
        P("dom"),
        P("dom"),
        P("dom"),
        P("dom", None, None),
    )
    return jax.shard_map(
        shards,
        mesh=mesh,
        in_specs=placed,
        out_specs=(P("dom", "feat"), P(None, "feat")),
        check_vma=False,
    )
```

time: 489 us -> 151 us (0.31)
  waiting for transfers between devices: 284 us -> 36.1 us
  local copies, waits for them, and re-layouts: 53.6 us -> 7.86 us
  other arithmetic: 44.6 us -> 1.39 us
  blocking collectives: 34.5 us -> 67.5 us
  matrix products: 28.6 us -> 0 us
  between operations: 14.7 us -> 1.53 us
  Pallas kernels: 0 us -> 9.38 us
    psum x1 -> x0, waiting for transfers between devices: 215 us -> none  [shards(): total_grad = lax.psum(local_grad, 'dom')]
    scatter-add x3 -> x0, other arithmetic: 36.9 us -> none  [tile_terms(): return start_blocks.at[outputs_part].add(product)]
    all_to_all x1 -> x3, blocking collectives: 32.2 us -> 67.5 us  [the longest x1 26.6 us: shards(): lax.all_to_all(outgoing.reshape(peers, sent // peers, cols), 'dom', split...]
    reduce_scatter x3 -> x0, waiting for transfers between devices: 34.9 us -> none  [shards(): lax.psum_scatter(partial_sum.astype(jnp.bfloat16), 'feat', scatter_dimens...]
    dot_general x7 -> x0, matrix products: 28.6 us -> none  [the longest x3 21.8 us: tile_terms(): jnp.einsum('tij,tjf->tif', tiles_part, picked, preferred_element_type=jnp...]
    mul x3 -> x0, local copies, waits for them, and re-layouts: 26.9 us -> none  [tile_terms(): product = product * live_part[:, None, None]]
    gather x6 -> x0, local copies, waits for them, and re-layouts: 23 us -> none  [the longest x3 14.7 us: shards(): outgoing = jnp.take(mixed_sum, sent_rows, axis=0)]
    pallas_call x0 -> x9, Pallas kernels: none -> 9.38 us  [the longest x3 3.58 us: mix(): pl.pallas_call(mix_kernel, out_shape=(jax.ShapeDtypeStruct((rows, cols),...]
  transfers between devices with their start and end apart: 6 -> 7, of which waited for: 6 -> 5; matrix products, arithmetic and copies ran while one was open for 0% -> 1% of each run, Pallas kernels for 0% -> 1%
where the time goes in v1:
time: 151 us; the launch traced here: 150 us
  blocking collectives  67.5 us (45%)
  waiting for transfers between devices  36.1 us (24%)
  starting transfers between devices  25.7 us (17%)
  Pallas kernels  9.38 us (6%)
  local copies, waits for them, and re-layouts  7.86 us (5%)
  between operations  1.53 us (1%)
    all_to_all x2, waiting for transfers between devices, shards(): lax.all_to_all(outgoing.reshape(peers, sent // peers, cols), 'dom', split...  31.4 us
    all_to_all x1, blocking collectives, shards(): lax.all_to_all(outgoing.reshape(peers, sent // peers, cols), 'dom', split...  26.6 us
    all_to_all x2, starting transfers between devices, shards(): lax.all_to_all(outgoing.reshape(peers, sent // peers, cols), 'dom', split...  24.6 us
    all_to_all x1, blocking collectives, shards(): lax.all_to_all(pieces, 'dom', split_axis=0, concat_axis=0, tiled=True)  21 us
    all_to_all x1, blocking collectives, shards(): lax.all_to_all(spread, 'dom', split_axis=0, concat_axis=0, tiled=True)  19.9 us
    unnamed x25, local copies, waits for them, and re-layouts  6.78 us
    pallas_call x3, Pallas kernels, mix(): pl.pallas_call(mix_kernel, out_shape=(jax.ShapeDtypeStruct((rows, cols),...  3.58 us
    ppermute x3, waiting for transfers between devices, shards(): other = lax.ppermute(scaled, 'feat', SWAP)  3.05 us
  transfers between devices with their start and end apart: 7, of which 5 were waited for; matrix products, arithmetic and copies ran while one was open for 1% of the time, Pallas kernels for 1%

profile of v1, /device:TPU:8, one launch (start us, length us, event | category | flops | bytes accessed | tf_op | source)
XLA Modules:
  0.0 149.5 jit_solution(15754094843991179785)
XLA Ops:
  0.6 1.2 multiply_subtract_fusion
  1.9 1.0 constant_dynamic-slice_fusion
  2.9 0.6 collective-permute-start.1
  3.5 0.8 copy.11
  4.4 0.2 fusion.pick
  4.6 1.7 %mix.3 = (bf16[512,256]{1,0:T(8,128)(2,1)S(1)}, bf16[1024,256]{1,0:T(8,128)(2,1)}) custom-call(bf16[512,256]{1,0:T(8,128)(2,1)S(1)} %get-tuple-element.19.own, bf16[512,256]{1,0:T(8,128)(2,1)S(1)} %collective-permute-done.other, bf16[256,256]{1,0:T(8,128)(2,1)S(1)} %get-tuple-element.21.own_w, bf16[256,256]{1,0:T(8,128)(2,1)S(1)} %collective-permute-done.1.other_w, ...), custom_call_target="tpu_custom_call" | custom-call | tf_op jit(solution)/shard_map/mix/pallas_call | solution.py:68
  6.4 15.8 %all-to-all-start = ((bf16[128,8,256]{2,1,0:T(8,128)(2,1)}), bf16[128,8,256]{2,1,0:T(8,128)(2,1)}, u32[]{:S(2)}, u32[]{:S(2)}) async-start(bf16[128,8,256]{2,1,0:T(8,128)(2,1)} %bitcast.1), calls=%async_computation | async-start | bytes 1048576 | tf_op jit(solution)/shard_map/all_to_all | solution.py:160
  22.9 1.6 %copy-done.1 = bf16[64,128,128]{2,1,0:T(8,128)(2,1)S(1)} copy-done((bf16[64,128,128]{2,1,0:T(8,128)(2,1)S(1)}, bf16[64,128,128]{2,1,0:T(8,128)(2,1)}, u32[]{:S(2)}) %copy-start.1) | copy-done | bytes 2097176
  24.5 1.2 densify.1.dense
  25.7 14.7 %all-to-all-done = bf16[128,8,256]{2,1,0:T(8,128)(2,1)} async-done(((bf16[128,8,256]{2,1,0:T(8,128)(2,1)}), bf16[128,8,256]{2,1,0:T(8,128)(2,1)}, u32[]{:S(2)}, u32[]{:S(2)}) %all-to-all-start) | async-done | bytes 524320 | tf_op jit(solution)/shard_map/all_to_all | solution.py:160
  40.5 1.0 copy-done.9
  41.4 1.6 %sweep.2.own = bf16[512,256]{1,0:T(8,128)(2,1)S(1)} custom-call(bf16[512,1536]{1,0:T(8,128)(2,1)S(1)} %densify.1.dense, bf16[512,256]{1,0:T(8,128)(2,1)S(1)} %copy-done.9, bf16[1024,256]{1,0:T(8,128)(2,1)} %bitcast.2.ghosts, f32[512,256]{1,0:T(8,128)S(1)} %get-tuple-element.18.slope, bf16[512,256]{1,0:T(8,128)(2,1)S(1)} %copy-done), custom_call_target="tpu_custom_call" | custom-call | tf_op jit(solution)/shard_map/sweep/pallas_call | solution.py:89
  43.1 0.1 collective-permute-start.2
  43.2 1.5 %collective-permute-done.2.other = bf16[512,256]{1,0:T(8,128)(2,1)S(1)} collective-permute-done((bf16[512,256]{1,0:T(8,128)(2,1)S(1)}, bf16[512,256]{1,0:T(8,128)(2,1)S(1)}, u32[]{:S(2)}, u32[]{:S(2)}) %collective-permute-start.2) | collective-permute-done | bytes 262176 | tf_op jit(solution)/shard_map/ppermute | solution.py:158
  44.7 0.9 mix.4
  45.6 26.6 %all_to_all.25 = bf16[128,8,256]{2,1,0:T(8,128)(2,1)S(1)} all-to-all(bf16[128,8,256]{2,1,0:T(8,128)(2,1)S(1)} %bitcast.10), channel_id=1, replica_groups=mesh['dom'=128,'feat'=2] {'dom'}, dimensions={0} | all-to-all | bytes 1048576 | tf_op jit(solution)/shard_map/all_to_all | solution.py:160
  72.2 0.6 sweep.3.own
  72.9 1.5 %collective-permute-done.3.other = bf16[512,256]{1,0:T(8,128)(2,1)S(1)} collective-permute-done((bf16[512,256]{1,0:T(8,128)(2,1)S(1)}, bf16[512,256]{1,0:T(8,128)(2,1)S(1)}, u32[]{:S(2)}, u32[]{:S(2)}) %collective-permute-start.3) | collective-permute-done | bytes 262176 | tf_op jit(solution)/shard_map/ppermute | solution.py:158
  74.4 0.9 mix.5
  75.3 0.8 copy-done.4
  76.1 0.7 copy-done.6
  76.8 8.8 %all-to-all-start.2 = ((bf16[128,8,256]{2,1,0:T(8,128)(2,1)}), bf16[128,8,256]{2,1,0:T(8,128)(2,1)S(1)}, u32[]{:S(2)}, u32[]{:S(2)}) async-start(bf16[128,8,256]{2,1,0:T(8,128)(2,1)} %bitcast.9), calls=%async_computation.2 | async-start | bytes 1048576 | tf_op jit(solution)/shard_map/all_to_all | solution.py:160
  85.6 0.3 collective-permute-start.4
  85.9 1.7 %collective-permute-done.4.other = bf16[512,256]{1,0:T(8,128)(2,1)S(1)} collective-permute-done((bf16[512,256]{1,0:T(8,128)(2,1)}, bf16[512,256]{1,0:T(8,128)(2,1)S(1)}, u32[]{:S(2)}, u32[]{:S(2)}) %collective-permute-start.4) | collective-permute-done | bytes 262176 | tf_op jit(solution)/shard_map/ppermute | solution.py:169
  87.6 16.7 %all-to-all-done.2 = bf16[128,8,256]{2,1,0:T(8,128)(2,1)S(1)} async-done(((bf16[128,8,256]{2,1,0:T(8,128)(2,1)}), bf16[128,8,256]{2,1,0:T(8,128)(2,1)S(1)}, u32[]{:S(2)}, u32[]{:S(2)}) %all-to-all-start.2) | async-done | bytes 524320 | tf_op jit(solution)/shard_map/all_to_all | solution.py:160
  104.3 0.9 copy-done.5
  105.2 0.9 copy-done.7
  106.2 1.4 last.1
  107.6 21.0 %all_to_all.26.refs_0_ = bf16[128,8,128]{2,1,0:T(8,128)(2,1)S(1)} all-to-all(bf16[128,8,128]{2,1,0:T(8,128)(2,1)S(1)} %get-tuple-element.17), channel_id=1, replica_groups=mesh['dom'=128,'feat'=2] {'dom'}, dimensions={0} | all-to-all | bytes 524288 | tf_op jit(solution)/shard_map/all_to_all | solution.py:173
  128.6 0.2 total.1
  128.8 19.9 %all_to_all.27.pieces = bf16[128,8,128]{2,1,0:T(8,128)(2,1)S(1)} all-to-all(bf16[128,8,128]{2,1,0:T(8,128)(2,1)S(1)} %total.1), channel_id=1, replica_groups=mesh['dom'=128,'feat'=2] {'dom'}, dimensions={0} | all-to-all | bytes 524288 | tf_op jit(solution)/shard_map/all_to_all | solution.py:182
  148.7 0.8 unpack.1
  (23 shorter events, 0.3 us)
Async XLA Ops:
  1.8 2.8 %collective-permute-start = (bf16[512,256]{1,0:T(8,128)(2,1)S(1)}, bf16[512,256]{1,0:T(8,128)(2,1)S(1)}, u32[]{:S(2)}, u32[]{:S(2)}) collective-permute-start(bf16[512,256]{1,0:T(8,128)(2,1)S(1)} %get-tuple-element.19.own), channel_id=1, source_target_pairs={{0,1},{1,0},{2,3},{3,2},{4,5},{5,4},{6,7},{7,6},{8,9},{9,8},{10,11... | collective-permute-start | bytes 786440 | tf_op jit(solution)/shard_map/ppermute | solution.py:158
  2.9 20.0 %copy-start.10 = (s32[64]{0:T(128)S(1)}, s32[64]{0:T(128)}, u32[]{:S(2)}) copy-start(s32[64]{0:T(128)} %inputs.1) | copy-start | bytes 772
  2.9 20.0 %copy-start.11 = (s32[64]{0:T(128)S(1)}, s32[64]{0:T(128)}, u32[]{:S(2)}) copy-start(s32[64]{0:T(128)} %outputs.1) | copy-start | bytes 772
  2.9 1.7 %collective-permute-start.1 = (bf16[256,256]{1,0:T(8,128)(2,1)S(1)}, bf16[256,256]{1,0:T(8,128)(2,1)S(1)}, u32[]{:S(2)}, u32[]{:S(2)}) collective-permute-start(bf16[256,256]{1,0:T(8,128)(2,1)S(1)} %get-tuple-element.20), channel_id=1, source_target_pairs={{0,1},{1,0},{2,3},{3,2},{4,5},{5,4},{6,7},{7,6},{8,9},{9,8},{10,11... | collective-permute-start | bytes 393224 | tf_op jit(solution)/shard_map/ppermute | solution.py:151
  4.6 1.8 %copy-start.2 = (bf16[256,256]{1,0:T(8,128)(2,1)}, bf16[256,256]{1,0:T(8,128)(2,1)S(1)}, u32[]{:S(2)}) copy-start(bf16[256,256]{1,0:T(8,128)(2,1)S(1)} %collective-permute-done.1.other_w) | copy-start | bytes 393220
  6.4 15.8 %copy-start.8 = (bf16[512,256]{1,0:T(8,128)(2,1)}, bf16[512,256]{1,0:T(8,128)(2,1)S(1)}, u32[]{:S(2)}) copy-start(bf16[512,256]{1,0:T(8,128)(2,1)S(1)} %get-tuple-element.10.mixed) | copy-start | bytes 786436
  6.4 34.1 %all-to-all-start = ((bf16[128,8,256]{2,1,0:T(8,128)(2,1)}), bf16[128,8,256]{2,1,0:T(8,128)(2,1)}, u32[]{:S(2)}, u32[]{:S(2)}) async-start(bf16[128,8,256]{2,1,0:T(8,128)(2,1)} %bitcast.1), calls=%async_computation | async-start | bytes 1048576 | tf_op jit(solution)/shard_map/all_to_all | solution.py:160
  22.2 18.3 %copy-start = (bf16[512,256]{1,0:T(8,128)(2,1)S(1)}, bf16[512,256]{1,0:T(8,128)(2,1)}, u32[]{:S(2)}) copy-start(bf16[512,256]{1,0:T(8,128)(2,1)} %source.5) | copy-start | bytes 786436
  22.9 1.6 %copy-start.1 = (bf16[64,128,128]{2,1,0:T(8,128)(2,1)S(1)}, bf16[64,128,128]{2,1,0:T(8,128)(2,1)}, u32[]{:S(2)}) copy-start(bf16[64,128,128]{2,1,0:T(8,128)(2,1)} %tiles.1) | copy-start | bytes 6291460
  40.5 4.2 %copy-start.3 = (bf16[256,256]{1,0:T(8,128)(2,1)S(1)}, bf16[256,256]{1,0:T(8,128)(2,1)}, u32[]{:S(2)}) copy-start(bf16[256,256]{1,0:T(8,128)(2,1)} %copy-done.2) | copy-start | bytes 393220
  40.5 1.0 copy-start.9
  43.1 1.6 %collective-permute-start.2 = (bf16[512,256]{1,0:T(8,128)(2,1)S(1)}, bf16[512,256]{1,0:T(8,128)(2,1)S(1)}, u32[]{:S(2)}, u32[]{:S(2)}) collective-permute-start(bf16[512,256]{1,0:T(8,128)(2,1)S(1)} %sweep.2.own), channel_id=1, source_target_pairs={{0,1},{1,0},{2,3},{3,2},{4,5},{5,4},{6,7},{7,6},{8,9},{9,8},{10,11... | collective-permute-start | bytes 786440 | tf_op jit(solution)/shard_map/ppermute | solution.py:158
  72.8 1.6 %collective-permute-start.3 = (bf16[512,256]{1,0:T(8,128)(2,1)S(1)}, bf16[512,256]{1,0:T(8,128)(2,1)S(1)}, u32[]{:S(2)}, u32[]{:S(2)}) collective-permute-start(bf16[512,256]{1,0:T(8,128)(2,1)S(1)} %sweep.3.own), channel_id=1, source_target_pairs={{0,1},{1,0},{2,3},{3,2},{4,5},{5,4},{6,7},{7,6},{8,9},{9,8},{10,11... | collective-permute-start | bytes 786440 | tf_op jit(solution)/shard_map/ppermute | solution.py:158
  75.3 0.8 copy-start.4
  76.1 0.7 copy-start.6
  76.8 27.4 %all-to-all-start.2 = ((bf16[128,8,256]{2,1,0:T(8,128)(2,1)}), bf16[128,8,256]{2,1,0:T(8,128)(2,1)S(1)}, u32[]{:S(2)}, u32[]{:S(2)}) async-start(bf16[128,8,256]{2,1,0:T(8,128)(2,1)} %bitcast.9), calls=%async_computation.2 | async-start | bytes 1048576 | tf_op jit(solution)/shard_map/all_to_all | solution.py:160
  85.6 2.0 %collective-permute-start.4 = (bf16[512,256]{1,0:T(8,128)(2,1)}, bf16[512,256]{1,0:T(8,128)(2,1)S(1)}, u32[]{:S(2)}, u32[]{:S(2)}) collective-permute-start(bf16[512,256]{1,0:T(8,128)(2,1)} %own.1), channel_id=1, source_target_pairs={{0,1},{1,0},{2,3},{3,2},{4,5},{5,4},{6,7},{7,6},{8,9},{9,8},{10,11... | collective-permute-start | bytes 786440 | tf_op jit(solution)/shard_map/ppermute | solution.py:169
  104.3 1.0 copy-start.5
  105.2 0.9 copy-start.7

commit v2 on v1

v2 whole, which is shorter than its diff:
```python
import math

import jax
import jax.numpy as jnp
from jax import lax
from jax.experimental import pallas as pl
from jax.experimental.pallas import tpu as pltpu
from jax.sharding import PartitionSpec as P

ITERS = 3
RING = 8
BF16 = jnp.bfloat16
F32 = jnp.float32
VMEM = pl.BlockSpec(memory_space=pltpu.VMEM)
SMEM = pl.BlockSpec(memory_space=pltpu.SMEM)
HBM = pl.BlockSpec(memory_space=pltpu.HBM)
SWAP = ((0, 1), (1, 0))


def params(mib):
    return pltpu.CompilerParams(vmem_limit_bytes=mib << 20)


def dot(a, b, dims=((1,), (0,))):
    return lax.dot_general(a, b, (dims, ((), ())), preferred_element_type=F32)


def densify_kernel(count, inputs, outputs, tiles, dense, total, here, sems):
    size = tiles.shape[1]
    in_blocks = dense.shape[1] // size
    out_blocks = dense.shape[0] // size
    runs = here.shape[0]
    run = here.shape[1]
    fetches = [
        pltpu.make_async_copy(tiles.at[pl.ds(part * run, run)], here.at[part], sems.at[part])
        for part in range(runs)
    ]
    for part in range(runs):

        @pl.when(part * run < count[0])
        def _():
            fetches[part].start()

    total[...] = jnp.zeros_like(total)
    for part in range(runs):

        @pl.when(part * run < count[0])
        def _():
            fetches[part].wait()

            def step(slot, carry):
                place = outputs[part * run + slot] * in_blocks + inputs[part * run + slot]
                total[place] += here[part, slot].astype(F32)
                return carry

            lax.fori_loop(0, jnp.minimum(count[0] - part * run, run), step, 0)

    for out in range(out_blocks):
        for inp in range(in_blocks):
            dense[out * size:(out + 1) * size, inp * size:(inp + 1) * size] = total[
                out * in_blocks + inp
            ].astype(BF16)


def densify(count, inputs, outputs, tiles, out_blocks, in_blocks):
    size = tiles.shape[1]
    runs = 8
    return pl.pallas_call(
        densify_kernel,
        out_shape=jax.ShapeDtypeStruct((out_blocks * size, in_blocks * size), BF16),
        in_specs=[SMEM, SMEM, SMEM, HBM],
        out_specs=VMEM,
        scratch_shapes=[
            pltpu.VMEM((out_blocks * in_blocks, size, size), F32),
            pltpu.VMEM((runs, tiles.shape[0] // runs, size, size), BF16),
            pltpu.SemaphoreType.DMA((runs,)),
        ],
        compiler_params=params(60),
        cost_estimate=pl.CostEstimate(flops=1 << 22, bytes_accessed=4 << 20, transcendentals=0),
        name="densify",
    )(count, inputs, outputs, tiles)


def mix_kernel(half, own, other, own_w, other_w, pick, mixed, outgoing):
    cols = own.shape[1]
    mine = pl.ds(pl.multiple_of(half[0] * cols, cols), cols)
    value = dot(own[...], own_w[mine, :], ((1,), (1,)))
    value = value + dot(other[...], other_w[mine, :], ((1,), (1,)))
    value = value.astype(BF16)
    mixed[...] = value
    outgoing[...] = dot(pick[...], value).astype(BF16)


def mix(half, own, other, own_w, other_w, pick):
    rows, cols = own.shape
    return pl.pallas_call(
        mix_kernel,
        out_shape=(
            jax.ShapeDtypeStruct((rows, cols), BF16),
            jax.ShapeDtypeStruct((pick.shape[0], cols), BF16),
        ),
        in_specs=[SMEM] + [VMEM] * 5,
        out_specs=(VMEM, VMEM),
        compiler_params=params(16),
        name="mix",
    )(half, own, other, own_w, other_w, pick)


def sweep_kernel(dense, mixed, ghosts, slope, source, scaled):
    rows = mixed.shape[0]
    state = dot(dense[:, :rows], mixed[...]) + dot(dense[:, rows:], ghosts[...])
    state = state + source[...].astype(F32)
    scaled[...] = (slope[...] * state).astype(BF16)


def sweep(dense, mixed, ghosts, slope, source):
    return pl.pallas_call(
        sweep_kernel,
        out_shape=jax.ShapeDtypeStruct(mixed.shape, BF16),
        in_specs=[VMEM] * 5,
        out_specs=VMEM,
        compiler_params=params(16),
        name="sweep",
    )(dense, mixed, ghosts, slope, source)


def last_kernel(
    half, dense, mixed, ghosts, slope, source, own, other, adjoint, pieces, own_here, other_here, sems
):
    rows, cols = mixed.shape
    fetches = [
        pltpu.make_async_copy(own, own_here, sems.at[0]),
        pltpu.make_async_copy(other, other_here, sems.at[1]),
    ]
    for fetch in fetches:
        fetch.start()
    state = dot(dense[:, :rows], mixed[...]) + dot(dense[:, rows:], ghosts[...])
    state = state + source[...].astype(F32)
    adjoint[...] = state.astype(BF16)
    pre_grad = (slope[...] * state).astype(BF16)
    count = pieces.shape[0] // 2
    sides = cols // 128
    for fetch, features, place in (
        (fetches[0], own_here, half[0]),
        (fetches[1], other_here, 1 - half[0]),
    ):
        fetch.wait()
        part = dot(features[...], pre_grad, ((0,), (0,))).astype(BF16)
        for group in range(cols // 8):
            for side in range(sides):
                pieces[place * count + group * sides + side] = part[
                    group * 8:group * 8 + 8, side * 128:side * 128 + 128
                ]


def last(half, dense, mixed, ghosts, slope, source, own, other):
    rows, cols = mixed.shape
    return pl.pallas_call(
        last_kernel,
        out_shape=(
            jax.ShapeDtypeStruct((rows, cols), BF16),
            jax.ShapeDtypeStruct((2 * cols * cols // 1024, 8, 128), BF16),
        ),
        in_specs=[SMEM] + [VMEM] * 5 + [HBM] * 2,
        out_specs=(VMEM, VMEM),
        scratch_shapes=[
            pltpu.VMEM(own.shape, BF16),
            pltpu.VMEM(own.shape, BF16),
            pltpu.SemaphoreType.DMA((2,)),
        ],
        compiler_params=params(24),
        name="last",
    )(half, dense, mixed, ghosts, slope, source, own, other)


def total_kernel(terms_count, scale, terms, spread):
    value = terms[0].astype(F32)
    for term in range(1, terms_count):
        value = value + terms[term].astype(F32)
    value = (value * scale).astype(BF16)
    for copy in range(spread.shape[0]):
        spread[copy] = value


def total(terms, terms_count, copies, scale):
    blocks = terms.shape[0] // terms_count
    out = pl.pallas_call(
        lambda *refs: total_kernel(terms_count, scale, *refs),
        out_shape=jax.ShapeDtypeStruct((copies, blocks) + terms.shape[1:], BF16),
        in_specs=[VMEM],
        out_specs=VMEM,
        compiler_params=params(16),
        name="total",
    )(terms.reshape((terms_count, blocks) + terms.shape[1:]))
    return out.reshape((copies * blocks,) + terms.shape[1:])


def unpack_kernel(pieces, grad):
    sides = grad.shape[1] // 128
    for piece in range(pieces.shape[0]):
        group, side = divmod(piece, sides)
        grad[group * 8:group * 8 + 8, side * 128:side * 128 + 128] = pieces[piece].astype(F32)


def shards(grad_out, preact, aggregated, weight, tiles, in_block, out_block, tile_count, send_rows):
    rows, cols = grad_out.shape
    tile_size = tiles.shape[1]
    peers = lax.axis_size("dom")
    sent_rows = send_rows[0].reshape(-1)
    sent = sent_rows.shape[0]
    half = lax.axis_index("feat")
    half = half.reshape(1)
    other_weight = lax.ppermute(weight, "feat", SWAP)
    other_agg = lax.ppermute(aggregated, "feat", SWAP)
    pick = (sent_rows[:, None] == jnp.arange(rows, dtype=jnp.int32)[None, :]).astype(BF16)
    hyperbolic = jnp.tanh(preact.astype(F32))
    slope = 1.0 - hyperbolic * hyperbolic
    scaled = (slope * grad_out.astype(F32)).astype(BF16)
    dense = densify(
        tile_count, in_block, out_block, tiles, rows // tile_size, (rows + sent) // tile_size
    )
    for iteration in range(ITERS):
        other = lax.ppermute(scaled, "feat", SWAP)
        mixed, outgoing = mix(half, scaled, other, weight, other_weight, pick)
        if iteration == 0:
            outgoing, dense, other_agg = lax.optimization_barrier((outgoing, dense, other_agg))
        ghosts = lax.all_to_all(
            outgoing.reshape(peers, sent // peers, cols), "dom", split_axis=0, concat_axis=0, tiled=True
        ).reshape(sent, cols)
        if iteration < ITERS - 1:
            scaled = sweep(dense, mixed, ghosts, slope, grad_out)
    adjoint, pieces = last(half, dense, mixed, ghosts, slope, grad_out, aggregated, other_agg)
    lines = peers // RING
    across = [[line * RING + place for line in range(lines)] for place in range(RING)]
    along = [[line * RING + place for place in range(RING)] for line in range(lines)]

    def exchange(blocks, groups):
        return lax.all_to_all(
            blocks, "dom", split_axis=0, concat_axis=0, tiled=True, axis_index_groups=groups
        )

    terms = total(exchange(pieces, across), lines, RING, 1.0)
    spread = total(exchange(terms, along), RING, lines, 1.0 / math.sqrt(peers * rows))
    gathered = exchange(spread, across)
    grad_weight = pl.pallas_call(
        unpack_kernel,
        out_shape=jax.ShapeDtypeStruct((2 * cols, cols), F32),
        in_specs=[VMEM],
        out_specs=VMEM,
        compiler_params=params(16),
        name="unpack",
    )(gathered)
    return adjoint, grad_weight


def solution(mesh):
    placed = (
        P("dom", "feat"),
        P("dom", "feat"),
        P("dom", "feat"),
        P(None, "feat"),
        P("dom", None, None),
        P("dom"),
        P("dom"),
        P("dom"),
        P("dom", None, None),
    )
    return jax.shard_map(
        shards,
        mesh=mesh,
        in_specs=placed,
        out_specs=(P("dom", "feat"), P(None, "feat")),
        check_vma=False,
    )
```

time: 151 us -> 142 us (0.940)
  blocking collectives: 67.5 us -> 124 us
  waiting for transfers between devices: 36.1 us -> 3.05 us
  starting transfers between devices: 25.7 us -> 0.96 us
  local copies, waits for them, and re-layouts: 7.86 us -> 0.9 us
    all_to_all x1 -> x3, blocking collectives: 26.6 us -> 87.6 us  [shards(): lax.all_to_all(outgoing.reshape(peers, sent // peers, cols), 'dom', split...]
    all_to_all x2 -> x0, waiting for transfers between devices: 31.4 us -> none  [shards(): lax.all_to_all(outgoing.reshape(peers, sent // peers, cols), 'dom', split...]
    all_to_all x2 -> x0, starting transfers between devices: 24.6 us -> none  [shards(): lax.all_to_all(outgoing.reshape(peers, sent // peers, cols), 'dom', split...]
    unnamed x25 -> x9, local copies, waits for them, and re-layouts: 6.78 us -> 0.81 us
    all_to_all x2 -> x3, blocking collectives: 41 us -> 36.4 us  [exchange(): lax.all_to_all(blocks, 'dom', split_axis=0, concat_axis=0, tiled=True, ax...]
    pallas_call x1, Pallas kernels: 1.23 us -> 3.49 us  [densify(): pl.pallas_call(densify_kernel, out_shape=jax.ShapeDtypeStruct((out_blocks...]
    ppermute x1, waiting for transfers between devices: 1.73 us -> 0.01 us  [shards(): other_agg = lax.ppermute(aggregated, 'feat', SWAP)]
  transfers between devices with their start and end apart: 7 -> 5, of which waited for: 5 -> 2; matrix products, arithmetic and copies ran while one was open for 1% -> 2% of each run, Pallas kernels for 1% -> 3%
where the time goes in v2:
time: 142 us
  blocking collectives  124 us (87%)
  Pallas kernels  10.1 us (7%)
  waiting for transfers between devices  3.05 us (2%)
  between operations  1.44 us (1%)
    all_to_all x3, blocking collectives, shards(): lax.all_to_all(outgoing.reshape(peers, sent // peers, cols), 'dom', split...  87.6 us
    all_to_all x3, blocking collectives, exchange(): lax.all_to_all(blocks, 'dom', split_axis=0, concat_axis=0, tiled=True, ax...  36.4 us
    pallas_call x1, Pallas kernels, densify(): pl.pallas_call(densify_kernel, out_shape=jax.ShapeDtypeStruct((out_blocks...  3.49 us
    ppermute x3, waiting for transfers between devices, shards(): other = lax.ppermute(scaled, 'feat', SWAP)  3.05 us
  transfers between devices with their start and end apart: 5, of which 2 were waited for; matrix products, arithmetic and copies ran while one was open for 2% of the time, Pallas kernels for 3%

profile of v2, /device:TPU:8, one launch (start us, length us, event | category | flops | bytes accessed | tf_op | source)
XLA Modules:
  0.0 141.9 jit_solution(10519592607624948024)
XLA Ops:
  0.6 0.1 collective-permute-start.1
  0.7 1.2 multiply_subtract_fusion
  1.9 0.6 collective-permute-start
  2.5 0.1 collective-permute-start.2
  3.2 0.8 copy.11
  4.0 0.1 eq.15
  4.1 0.0 copy-start.2
  4.1 3.5 %densify.1.dense = bf16[512,1536]{1,0:T(8,128)(2,1)} custom-call(s32[1]{0:T(128)S(6)} %copy.12.count, s32[64]{0:T(128)} %inputs.1, s32[64]{0:T(128)} %outputs.1, bf16[64,128,128]{2,1,0:T(8,128)(2,1)} %tiles.1), custom_call_target="tpu_custom_call" | custom-call | flops 4194304 | bytes 4194304 | tf_op jit(solution)/shard_map/densify/pallas_call | solution.py:68
  7.6 0.0 copy-start
  7.6 0.0 copy-start.1
  7.6 0.2 fusion.pick
  7.9 0.0 collective-permute-done.1.other_w
  7.9 0.0 collective-permute-done.other
  7.9 0.9 mix.3
  8.8 0.0 collective-permute-done.2.other
  8.9 34.1 %all_to_all.30 = bf16[128,8,256]{2,1,0:T(8,128)(2,1)S(1)} all-to-all(bf16[128,8,256]{2,1,0:T(8,128)(2,1)S(1)} %bitcast.18), channel_id=1, replica_groups=mesh['dom'=128,'feat'=2] {'dom'}, dimensions={0} | all-to-all | bytes 1048576 | tf_op jit(solution)/shard_map/all_to_all | solution.py:227
  42.9 0.6 sweep.2.own
  43.5 0.1 collective-permute-start.3
  43.6 1.5 %collective-permute-done.3.other = bf16[512,256]{1,0:T(8,128)(2,1)S(1)} collective-permute-done((bf16[512,256]{1,0:T(8,128)(2,1)S(1)}, bf16[512,256]{1,0:T(8,128)(2,1)S(1)}, u32[]{:S(2)}, u32[]{:S(2)}) %collective-permute-start.3) | collective-permute-done | bytes 262176 | tf_op jit(solution)/shard_map/ppermute | solution.py:223
  45.1 0.9 mix.4
  46.1 26.8 %all_to_all.31 = bf16[128,8,256]{2,1,0:T(8,128)(2,1)S(1)} all-to-all(bf16[128,8,256]{2,1,0:T(8,128)(2,1)S(1)} %bitcast.20), channel_id=1, replica_groups=mesh['dom'=128,'feat'=2] {'dom'}, dimensions={0} | all-to-all | bytes 1048576 | tf_op jit(solution)/shard_map/all_to_all | solution.py:227
  72.9 0.6 sweep.3.own
  73.4 0.0 copy-start.3
  73.5 0.1 collective-permute-start.4
  73.6 1.5 %collective-permute-done.4.other = bf16[512,256]{1,0:T(8,128)(2,1)S(1)} collective-permute-done((bf16[512,256]{1,0:T(8,128)(2,1)S(1)}, bf16[512,256]{1,0:T(8,128)(2,1)S(1)}, u32[]{:S(2)}, u32[]{:S(2)}) %collective-permute-start.4) | collective-permute-done | bytes 262176 | tf_op jit(solution)/shard_map/ppermute | solution.py:223
  75.1 0.9 mix.5
  76.0 26.8 %all_to_all.32 = bf16[128,8,256]{2,1,0:T(8,128)(2,1)S(1)} all-to-all(bf16[128,8,256]{2,1,0:T(8,128)(2,1)S(1)} %bitcast.19), channel_id=1, replica_groups=mesh['dom'=128,'feat'=2] {'dom'}, dimensions={0} | all-to-all | bytes 1048576 | tf_op jit(solution)/shard_map/all_to_all | solution.py:227
  102.8 1.8 %last.1 = (bf16[512,256]{1,0:T(8,128)(2,1)}, bf16[128,8,128]{2,1,0:T(8,128)(2,1)S(1)}) custom-call(s32[1]{0:T(128)} %bitcast.half, bf16[512,1536]{1,0:T(8,128)(2,1)S(1)} %copy-done, bf16[512,256]{1,0:T(8,128)(2,1)S(1)} %get-tuple-element.19.mixed, bf16[1024,256]{1,0:T(8,128)(2,1)S(1)} %bitcast.11, f32[512,256]{1,0:T(8,128)S(1)} %get-tuple-element.24.slope, ...), custom_call_target="tpu_custom_call" | custom-call | tf_op jit(solution)/shard_map/last/pallas_call | solution.py:158
  104.6 13.0 %all_to_all.33 = bf16[128,8,128]{2,1,0:T(8,128)(2,1)S(1)} all-to-all(bf16[128,8,128]{2,1,0:T(8,128)(2,1)S(1)} %get-tuple-element.23), channel_id=1, replica_groups={{0,16,32,48,64,80,96,112,128,144,160,176,192,208,224,240},{2,18,34,50,6..., dimensions={0} | all-to-all | bytes 524288 | tf_op jit(solution)/shard_map/all_to_all | solution.py:238
  117.7 11.5 %all_to_all.34 = bf16[64,8,128]{2,1,0:T(8,128)(2,1)S(1)} all-to-all(bf16[64,8,128]{2,1,0:T(8,128)(2,1)S(1)} %bitcast.16), channel_id=1, replica_groups={{0,2,4,6,8,10,12,14},{16,18,20,22,24,26,28,30},{32,34,36,38,40,42,44,46..., dimensions={0} | all-to-all | bytes 262144 | tf_op jit(solution)/shard_map/all_to_all | solution.py:238
  129.2 11.9 %all_to_all.35.pieces = bf16[128,8,128]{2,1,0:T(8,128)(2,1)S(1)} all-to-all(bf16[128,8,128]{2,1,0:T(8,128)(2,1)S(1)} %bitcast.15), channel_id=1, replica_groups={{0,16,32,48,64,80,96,112,128,144,160,176,192,208,224,240},{2,18,34,50,6..., dimensions={0} | all-to-all | bytes 524288 | tf_op jit(solution)/shard_map/all_to_all | solution.py:238
  141.1 0.8 unpack.1
  (6 shorter events, 0.1 us)
Async XLA Ops:
  0.6 7.3 %collective-permute-start.1 = (bf16[512,256]{1,0:T(8,128)(2,1)}, bf16[512,256]{1,0:T(8,128)(2,1)S(1)}, u32[]{:S(2)}, u32[]{:S(2)}) collective-permute-start(bf16[512,256]{1,0:T(8,128)(2,1)} %own_w.5), channel_id=1, source_target_pairs={{0,1},{1,0},{2,3},{3,2},{4,5},{5,4},{6,7},{7,6},{8,9},{9,8},{10,11... | collective-permute-start | bytes 786440 | tf_op jit(solution)/shard_map/ppermute | solution.py:213
  1.9 6.0 %collective-permute-start = (bf16[512,256]{1,0:T(8,128)(2,1)S(1)}, bf16[512,256]{1,0:T(8,128)(2,1)S(1)}, u32[]{:S(2)}, u32[]{:S(2)}) collective-permute-start(bf16[512,256]{1,0:T(8,128)(2,1)S(1)} %get-tuple-element.25.own), channel_id=1, source_target_pairs={{0,1},{1,0},{2,3},{3,2},{4,5},{5,4},{6,7},{7,6},{8,9},{9,8},{10,11... | collective-permute-start | bytes 786440 | tf_op jit(solution)/shard_map/ppermute | solution.py:223
  2.5 6.4 %collective-permute-start.2 = (bf16[512,256]{1,0:T(8,128)(2,1)}, bf16[512,256]{1,0:T(8,128)(2,1)S(1)}, u32[]{:S(2)}, u32[]{:S(2)}) collective-permute-start(bf16[512,256]{1,0:T(8,128)(2,1)} %own.1), channel_id=1, source_target_pairs={{0,1},{1,0},{2,3},{3,2},{4,5},{5,4},{6,7},{7,6},{8,9},{9,8},{10,11... | collective-permute-start | bytes 786440 | tf_op jit(solution)/shard_map/ppermute | solution.py:214
  4.1 3.8 %copy-start.2 = (bf16[512,256]{1,0:T(8,128)(2,1)S(1)}, bf16[512,256]{1,0:T(8,128)(2,1)}, u32[]{:S(2)}) copy-start(bf16[512,256]{1,0:T(8,128)(2,1)} %own_w.5) | copy-start | bytes 786436
  7.6 35.3 %copy-start = (bf16[512,1536]{1,0:T(8,128)(2,1)S(1)}, bf16[512,1536]{1,0:T(8,128)(2,1)}, u32[]{:S(2)}) copy-start(bf16[512,1536]{1,0:T(8,128)(2,1)} %densify.1.dense) | copy-start | bytes 4718596
  7.6 35.3 %copy-start.1 = (bf16[512,256]{1,0:T(8,128)(2,1)S(1)}, bf16[512,256]{1,0:T(8,128)(2,1)}, u32[]{:S(2)}) copy-start(bf16[512,256]{1,0:T(8,128)(2,1)} %source.5) | copy-start | bytes 786436
  43.5 1.6 %collective-permute-start.3 = (bf16[512,256]{1,0:T(8,128)(2,1)S(1)}, bf16[512,256]{1,0:T(8,128)(2,1)S(1)}, u32[]{:S(2)}, u32[]{:S(2)}) collective-permute-start(bf16[512,256]{1,0:T(8,128)(2,1)S(1)} %sweep.2.own), channel_id=1, source_target_pairs={{0,1},{1,0},{2,3},{3,2},{4,5},{5,4},{6,7},{7,6},{8,9},{9,8},{10,11... | collective-permute-start | bytes 786440 | tf_op jit(solution)/shard_map/ppermute | solution.py:223
  73.4 29.4 %copy-start.3 = (bf16[512,256]{1,0:T(8,128)(2,1)S(1)}, bf16[512,256]{1,0:T(8,128)(2,1)}, u32[]{:S(2)}) copy-start(bf16[512,256]{1,0:T(8,128)(2,1)} %own.1) | copy-start | bytes 786436
  73.5 1.6 %collective-permute-start.4 = (bf16[512,256]{1,0:T(8,128)(2,1)S(1)}, bf16[512,256]{1,0:T(8,128)(2,1)S(1)}, u32[]{:S(2)}, u32[]{:S(2)}) collective-permute-start(bf16[512,256]{1,0:T(8,128)(2,1)S(1)} %sweep.3.own), channel_id=1, source_target_pairs={{0,1},{1,0},{2,3},{3,2},{4,5},{5,4},{6,7},{7,6},{8,9},{9,8},{10,11... | collective-permute-start | bytes 786440 | tf_op jit(solution)/shard_map/ppermute | solution.py:223

commit v3 on v2

--- a/solution.py
+++ b/solution.py
@@ -13,7 +13,6 @@
 F32 = jnp.float32
 VMEM = pl.BlockSpec(memory_space=pltpu.VMEM)
 SMEM = pl.BlockSpec(memory_space=pltpu.SMEM)
-HBM = pl.BlockSpec(memory_space=pltpu.HBM)
 SWAP = ((0, 1), (1, 0))
 
 
@@ -23,62 +22,6 @@
 
 def dot(a, b, dims=((1,), (0,))):
     return lax.dot_general(a, b, (dims, ((), ())), preferred_element_type=F32)
-
-
-def densify_kernel(count, inputs, outputs, tiles, dense, total, here, sems):
-    size = tiles.shape[1]
-    in_blocks = dense.shape[1] // size
-    out_blocks = dense.shape[0] // size
-    runs = here.shape[0]
-    run = here.shape[1]
-    fetches = [
-        pltpu.make_async_copy(tiles.at[pl.ds(part * run, run)], here.at[part], sems.at[part])
-        for part in range(runs)
-    ]
-    for part in range(runs):
-
-        @pl.when(part * run < count[0])
-        def _():
-            fetches[part].start()
-
-    total[...] = jnp.zeros_like(total)
-    for part in range(runs):
-
-        @pl.when(part * run < count[0])
-        def _():
-            fetches[part].wait()
-
-            def step(slot, carry):
-                place = outputs[part * run + slot] * in_blocks + inputs[part * run + slot]
-                total[place] += here[part, slot].astype(F32)
-                return carry
-
-            lax.fori_loop(0, jnp.minimum(count[0] - part * run, run), step, 0)
-
-    for out in range(out_blocks):
-        for inp in range(in_blocks):
-            dense[out * size:(out + 1) * size, inp * size:(inp + 1) * size] = total[
-                out * in_blocks + inp
-            ].astype(BF16)
-
-
-def densify(count, inputs, outputs, tiles, out_blocks, in_blocks):
-    size = tiles.shape[1]
-    runs = 8
-    return pl.pallas_call(
-        densify_kernel,
-        out_shape=jax.ShapeDtypeStruct((out_blocks * size, in_blocks * size), BF16),
-        in_specs=[SMEM, SMEM, SMEM, HBM],
-        out_specs=VMEM,
-        scratch_shapes=[
-            pltpu.VMEM((out_blocks * in_blocks, size, size), F32),
-            pltpu.VMEM((runs, tiles.shape[0] // runs, size, size), BF16),
-            pltpu.SemaphoreType.DMA((runs,)),
-        ],
-        compiler_params=params(60),
-        cost_estimate=pl.CostEstimate(flops=1 << 22, bytes_accessed=4 << 20, transcendentals=0),
-        name="densify",
-    )(count, inputs, outputs, tiles)
 
 
 def mix_kernel(half, own, other, own_w, other_w, pick, mixed, outgoing):
@@ -102,15 +45,59 @@
         in_specs=[SMEM] + [VMEM] * 5,
         out_specs=(VMEM, VMEM),
         compiler_params=params(16),
+        cost_estimate=pl.CostEstimate(
+            flops=8 * rows * cols * (2 * cols + pick.shape[0]), bytes_accessed=5 << 19, transcendentals=0
+        ),
         name="mix",
     )(half, own, other, own_w, other_w, pick)
 
 
-def sweep_kernel(dense, mixed, ghosts, slope, source, scaled):
+def new_state(dense, mixed, ghosts, source):
     rows = mixed.shape[0]
     state = dot(dense[:, :rows], mixed[...]) + dot(dense[:, rows:], ghosts[...])
-    state = state + source[...].astype(F32)
-    scaled[...] = (slope[...] * state).astype(BF16)
+    return state + source[...].astype(F32)
+
+
+def first_kernel(places, tiles, mixed, ghosts, slope, source, scaled, dense, total):
+    size = tiles.shape[1]
+    out_blocks = dense.shape[0] // size
+    in_blocks = dense.shape[1] // size
+    total[...] = jnp.zeros_like(total)
+
+    def step(slot, carry):
+        total[places[slot]] += tiles[slot].astype(F32)
+        return carry
+
+    lax.fori_loop(0, tiles.shape[0], step, 0)
+    for out in range(out_blocks):
+        for inp in range(in_blocks):
+            dense[out * size:(out + 1) * size, inp * size:(inp + 1) * size] = total[
+                out * in_blocks + inp
+            ].astype(BF16)
+    scaled[...] = (slope[...] * new_state(dense, mixed, ghosts, source)).astype(BF16)
+
+
+def first(places, tiles, mixed, ghosts, slope, source):
+    size = tiles.shape[1]
+    rows = mixed.shape[0]
+    across = rows + ghosts.shape[0]
+    pairs = rows * across // (size * size)
+    return pl.pallas_call(
+        first_kernel,
+        out_shape=(
+            jax.ShapeDtypeStruct(mixed.shape, BF16),
+            jax.ShapeDtypeStruct((rows, across), BF16),
+        ),
+        in_specs=[SMEM] + [VMEM] * 5,
+        out_specs=(VMEM, VMEM),
+        scratch_shapes=[pltpu.VMEM((pairs + 1, size, size), F32)],
+        compiler_params=params(24),
+        name="first",
+    )(places, tiles, mixed, ghosts, slope, source)
+
+
+def sweep_kernel(dense, mixed, ghosts, slope, source, scaled):
+    scaled[...] = (slope[...] * new_state(dense, mixed, ghosts, source)).astype(BF16)
 
 
 def sweep(dense, mixed, ghosts, slope, source):
@@ -124,27 +111,14 @@
     )(dense, mixed, ghosts, slope, source)
 
 
-def last_kernel(
-    half, dense, mixed, ghosts, slope, source, own, other, adjoint, pieces, own_here, other_here, sems
-):
-    rows, cols = mixed.shape
-    fetches = [
-        pltpu.make_async_copy(own, own_here, sems.at[0]),
-        pltpu.make_async_copy(other, other_here, sems.at[1]),
-    ]
-    for fetch in fetches:
-        fetch.start()
-    state = dot(dense[:, :rows], mixed[...]) + dot(dense[:, rows:], ghosts[...])
-    state = state + source[...].astype(F32)
+def last_kernel(half, dense, mixed, ghosts, slope, source, own, other, adjoint, pieces):
+    cols = mixed.shape[1]
+    state = new_state(dense, mixed, ghosts, source)
     adjoint[...] = state.astype(BF16)
     pre_grad = (slope[...] * state).astype(BF16)
     count = pieces.shape[0] // 2
     sides = cols // 128
-    for fetch, features, place in (
-        (fetches[0], own_here, half[0]),
-        (fetches[1], other_here, 1 - half[0]),
-    ):
-        fetch.wait()
+    for features, place in ((own, half[0]), (other, 1 - half[0])):
         part = dot(features[...], pre_grad, ((0,), (0,))).astype(BF16)
         for group in range(cols // 8):
             for side in range(sides):
@@ -161,13 +135,8 @@
             jax.ShapeDtypeStruct((rows, cols), BF16),
             jax.ShapeDtypeStruct((2 * cols * cols // 1024, 8, 128), BF16),
         ),
-        in_specs=[SMEM] + [VMEM] * 5 + [HBM] * 2,
+        in_specs=[SMEM] + [VMEM] * 7,
         out_specs=(VMEM, VMEM),
-        scratch_shapes=[
-            pltpu.VMEM(own.shape, BF16),
-            pltpu.VMEM(own.shape, BF16),
-            pltpu.SemaphoreType.DMA((2,)),
-        ],
         compiler_params=params(24),
         name="last",
     )(half, dense, mixed, ghosts, slope, source, own, other)
@@ -204,7 +173,6 @@
 
 def shards(grad_out, preact, aggregated, weight, tiles, in_block, out_block, tile_count, send_rows):
     rows, cols = grad_out.shape
-    tile_size = tiles.shape[1]
     peers = lax.axis_size("dom")
     sent_rows = send_rows[0].reshape(-1)
     sent = sent_rows.shape[0]
@@ -216,18 +184,21 @@
     hyperbolic = jnp.tanh(preact.astype(F32))
     slope = 1.0 - hyperbolic * hyperbolic
     scaled = (slope * grad_out.astype(F32)).astype(BF16)
-    dense = densify(
-        tile_count, in_block, out_block, tiles, rows // tile_size, (rows + sent) // tile_size
-    )
+    in_blocks = (rows + sent) // tiles.shape[1]
+    pairs = rows // tiles.shape[1] * in_blocks
+    slots = jnp.arange(tiles.shape[0], dtype=jnp.int32)
+    places = jnp.where(slots < tile_count[0], out_block * in_blocks + in_block, pairs)
     for iteration in range(ITERS):
         other = lax.ppermute(scaled, "feat", SWAP)
         mixed, outgoing = mix(half, scaled, other, weight, other_weight, pick)
         if iteration == 0:
-            outgoing, dense, other_agg = lax.optimization_barrier((outgoing, dense, other_agg))
+            outgoing, other_agg, places = lax.optimization_barrier((outgoing, other_agg, places))
         ghosts = lax.all_to_all(
             outgoing.reshape(peers, sent // peers, cols), "dom", split_axis=0, concat_axis=0, tiled=True
         ).reshape(sent, cols)
-        if iteration < ITERS - 1:
+        if iteration == 0:
+            scaled, dense = first(places, tiles, mixed, ghosts, slope, grad_out)
+        elif iteration < ITERS - 1:
             scaled = sweep(dense, mixed, ghosts, slope, grad_out)
     adjoint, pieces = last(half, dense, mixed, ghosts, slope, grad_out, aggregated, other_agg)
     lines = peers // RING

time: 142 us -> 140 us (0.986)
  Pallas kernels: 10.1 us -> 7.72 us
    pallas_call x1, Pallas kernels: 3.49 us -> 2.04 us  [first(): pl.pallas_call(first_kernel, out_shape=(jax.ShapeDtypeStruct(mixed.shape,...]
  transfers between devices with their start and end apart: 5 -> 5, of which waited for: 2 -> 2; matrix products, arithmetic and copies ran while one was open for 2% -> 2% of each run, Pallas kernels for 3% -> 1%
where the time goes in v3:
time: 140 us; the launch traced here: 139 us
  blocking collectives  124 us (89%)
  Pallas kernels  7.72 us (6%)
  waiting for transfers between devices  3.05 us (2%)
  between operations  1.47 us (1%)
    all_to_all x3, blocking collectives, shards(): lax.all_to_all(outgoing.reshape(peers, sent // peers, cols), 'dom', split...  87.3 us
    all_to_all x3, blocking collectives, exchange(): lax.all_to_all(blocks, 'dom', split_axis=0, concat_axis=0, tiled=True, ax...  36.4 us
    ppermute x3, waiting for transfers between devices, shards(): other = lax.ppermute(scaled, 'feat', SWAP)  3.05 us
  transfers between devices with their start and end apart: 5, of which 2 were waited for; matrix products, arithmetic and copies ran while one was open for 2% of the time, Pallas kernels for 1%

profile of v3, /device:TPU:8, one launch (start us, length us, event | category | flops | bytes accessed | tf_op | source)
XLA Modules:
  0.0 139.3 jit_solution(2046707654434037650)
XLA Ops:
  0.6 0.0 copy-start.3
  0.7 0.1 collective-permute-start.2
  0.8 0.5 collective-permute-start.1
  1.3 1.1 multiply_subtract_fusion
  2.4 0.2 collective-permute-start
  2.6 0.8 copy.11
  3.4 0.1 eq.15
  3.5 0.2 fusion.pick
  4.4 0.0 collective-permute-done.1.other_w
  4.4 0.0 collective-permute-done.other
  4.4 0.0 copy-start
  4.5 0.0 copy-start.1
  4.5 0.9 mix.3
  5.4 0.0 collective-permute-done.2.other
  5.4 33.8 %all_to_all.30 = bf16[128,8,256]{2,1,0:T(8,128)(2,1)S(1)} all-to-all(bf16[128,8,256]{2,1,0:T(8,128)(2,1)S(1)} %bitcast.20), channel_id=1, replica_groups=mesh['dom'=128,'feat'=2] {'dom'}, dimensions={0} | all-to-all | bytes 1048576 | tf_op jit(solution)/shard_map/all_to_all | solution.py:196
  39.2 2.0 %first.1 = (bf16[512,256]{1,0:T(8,128)(2,1)S(1)}, bf16[512,1536]{1,0:T(8,128)(2,1)S(1)}) custom-call(s32[64]{0:T(128)S(1)} %compare_select_fusion.places, bf16[64,128,128]{2,1,0:T(8,128)(2,1)S(1)} %copy-done.1, bf16[512,256]{1,0:T(8,128)(2,1)S(1)} %get-tuple-element.17.mixed, bf16[1024,256]{1,0:T(8,128)(2,1)S(1)} %bitcast.14, ...), custom_call_target="tpu_custom_call" | custom-call | tf_op jit(solution)/shard_map/first/pallas_call | solution.py:85
  41.2 0.1 collective-permute-start.3
  41.3 1.5 %collective-permute-done.3.other = bf16[512,256]{1,0:T(8,128)(2,1)S(1)} collective-permute-done((bf16[512,256]{1,0:T(8,128)(2,1)S(1)}, bf16[512,256]{1,0:T(8,128)(2,1)S(1)}, u32[]{:S(2)}, u32[]{:S(2)}) %collective-permute-start.3) | collective-permute-done | bytes 262176 | tf_op jit(solution)/shard_map/ppermute | solution.py:192
  42.9 0.9 mix.4
  43.8 26.8 %all_to_all.31 = bf16[128,8,256]{2,1,0:T(8,128)(2,1)S(1)} all-to-all(bf16[128,8,256]{2,1,0:T(8,128)(2,1)S(1)} %bitcast.22), channel_id=1, replica_groups=mesh['dom'=128,'feat'=2] {'dom'}, dimensions={0} | all-to-all | bytes 1048576 | tf_op jit(solution)/shard_map/all_to_all | solution.py:196
  70.6 0.6 sweep.1.own
  71.1 0.0 copy-start.2
  71.2 0.1 collective-permute-start.4
  71.3 1.5 %collective-permute-done.4.other = bf16[512,256]{1,0:T(8,128)(2,1)S(1)} collective-permute-done((bf16[512,256]{1,0:T(8,128)(2,1)S(1)}, bf16[512,256]{1,0:T(8,128)(2,1)S(1)}, u32[]{:S(2)}, u32[]{:S(2)}) %collective-permute-start.4) | collective-permute-done | bytes 262176 | tf_op jit(solution)/shard_map/ppermute | solution.py:192
  72.8 0.9 mix.5
  73.7 26.8 %all_to_all.32 = bf16[128,8,256]{2,1,0:T(8,128)(2,1)S(1)} all-to-all(bf16[128,8,256]{2,1,0:T(8,128)(2,1)S(1)} %bitcast.21), channel_id=1, replica_groups=mesh['dom'=128,'feat'=2] {'dom'}, dimensions={0} | all-to-all | bytes 1048576 | tf_op jit(solution)/shard_map/all_to_all | solution.py:196
  100.5 0.0 copy-done.2
  100.5 1.4 %last.1 = (bf16[512,256]{1,0:T(8,128)(2,1)}, bf16[128,8,128]{2,1,0:T(8,128)(2,1)S(1)}) custom-call(s32[1]{0:T(128)} %bitcast.half, bf16[512,1536]{1,0:T(8,128)(2,1)S(1)} %get-tuple-element.19.dense, bf16[512,256]{1,0:T(8,128)(2,1)S(1)} %get-tuple-element.23.mixed, bf16[1024,256]{1,0:T(8,128)(2,1)S(1)} %bitcast.13, f32[512,256]{1,0:T(8,128)S(1)} %get-tuple-element.28.slope, ...), custom_call_target="tpu_custom_call" | custom-call | tf_op jit(solution)/shard_map/last/pallas_call | solution.py:132
  101.9 13.0 %all_to_all.33 = bf16[128,8,128]{2,1,0:T(8,128)(2,1)S(1)} all-to-all(bf16[128,8,128]{2,1,0:T(8,128)(2,1)S(1)} %get-tuple-element.27), channel_id=1, replica_groups={{0,16,32,48,64,80,96,112,128,144,160,176,192,208,224,240},{2,18,34,50,6..., dimensions={0} | all-to-all | bytes 524288 | tf_op jit(solution)/shard_map/all_to_all | solution.py:209
  115.0 11.5 %all_to_all.34 = bf16[64,8,128]{2,1,0:T(8,128)(2,1)S(1)} all-to-all(bf16[64,8,128]{2,1,0:T(8,128)(2,1)S(1)} %bitcast.18), channel_id=1, replica_groups={{0,2,4,6,8,10,12,14},{16,18,20,22,24,26,28,30},{32,34,36,38,40,42,44,46..., dimensions={0} | all-to-all | bytes 262144 | tf_op jit(solution)/shard_map/all_to_all | solution.py:209
  126.5 11.9 %all_to_all.35.pieces = bf16[128,8,128]{2,1,0:T(8,128)(2,1)S(1)} all-to-all(bf16[128,8,128]{2,1,0:T(8,128)(2,1)S(1)} %bitcast.17), channel_id=1, replica_groups={{0,16,32,48,64,80,96,112,128,144,160,176,192,208,224,240},{2,18,34,50,6..., dimensions={0} | all-to-all | bytes 524288 | tf_op jit(solution)/shard_map/all_to_all | solution.py:209
  138.4 0.8 unpack.1
  (10 shorter events, 0.1 us)
Async XLA Ops:
  0.6 3.8 %copy-start.3 = (bf16[512,256]{1,0:T(8,128)(2,1)S(1)}, bf16[512,256]{1,0:T(8,128)(2,1)}, u32[]{:S(2)}) copy-start(bf16[512,256]{1,0:T(8,128)(2,1)} %own_w.5) | copy-start | bytes 786436
  0.6 3.7 %copy-start.5 = (s32[64]{0:T(128)S(1)}, s32[64]{0:T(128)}, u32[]{:S(2)}) copy-start(s32[64]{0:T(128)} %param.15) | copy-start | bytes 772
  0.7 3.7 %copy-start.4 = (s32[64]{0:T(128)S(1)}, s32[64]{0:T(128)}, u32[]{:S(2)}) copy-start(s32[64]{0:T(128)} %param.14) | copy-start | bytes 772
  0.7 4.7 %collective-permute-start.2 = (bf16[512,256]{1,0:T(8,128)(2,1)}, bf16[512,256]{1,0:T(8,128)(2,1)S(1)}, u32[]{:S(2)}, u32[]{:S(2)}) collective-permute-start(bf16[512,256]{1,0:T(8,128)(2,1)} %own.1), channel_id=1, source_target_pairs={{0,1},{1,0},{2,3},{3,2},{4,5},{5,4},{6,7},{7,6},{8,9},{9,8},{10,11... | collective-permute-start | bytes 786440 | tf_op jit(solution)/shard_map/ppermute | solution.py:182
  0.8 3.6 %collective-permute-start.1 = (bf16[512,256]{1,0:T(8,128)(2,1)}, bf16[512,256]{1,0:T(8,128)(2,1)S(1)}, u32[]{:S(2)}, u32[]{:S(2)}) collective-permute-start(bf16[512,256]{1,0:T(8,128)(2,1)} %own_w.5), channel_id=1, source_target_pairs={{0,1},{1,0},{2,3},{3,2},{4,5},{5,4},{6,7},{7,6},{8,9},{9,8},{10,11... | collective-permute-start | bytes 786440 | tf_op jit(solution)/shard_map/ppermute | solution.py:181
  2.4 2.0 %collective-permute-start = (bf16[512,256]{1,0:T(8,128)(2,1)S(1)}, bf16[512,256]{1,0:T(8,128)(2,1)S(1)}, u32[]{:S(2)}, u32[]{:S(2)}) collective-permute-start(bf16[512,256]{1,0:T(8,128)(2,1)S(1)} %get-tuple-element.29.own), channel_id=1, source_target_pairs={{0,1},{1,0},{2,3},{3,2},{4,5},{5,4},{6,7},{7,6},{8,9},{9,8},{10,11... | collective-permute-start | bytes 786440 | tf_op jit(solution)/shard_map/ppermute | solution.py:192
  4.4 34.7 %copy-start = (bf16[512,256]{1,0:T(8,128)(2,1)S(1)}, bf16[512,256]{1,0:T(8,128)(2,1)}, u32[]{:S(2)}) copy-start(bf16[512,256]{1,0:T(8,128)(2,1)} %source.5) | copy-start | bytes 786436
  4.5 34.7 %copy-start.1 = (bf16[64,128,128]{2,1,0:T(8,128)(2,1)S(1)}, bf16[64,128,128]{2,1,0:T(8,128)(2,1)}, u32[]{:S(2)}) copy-start(bf16[64,128,128]{2,1,0:T(8,128)(2,1)} %tiles.1) | copy-start | bytes 6291460
  41.2 1.6 %collective-permute-start.3 = (bf16[512,256]{1,0:T(8,128)(2,1)S(1)}, bf16[512,256]{1,0:T(8,128)(2,1)S(1)}, u32[]{:S(2)}, u32[]{:S(2)}) collective-permute-start(bf16[512,256]{1,0:T(8,128)(2,1)S(1)} %get-tuple-element.20.own), channel_id=1, source_target_pairs={{0,1},{1,0},{2,3},{3,2},{4,5},{5,4},{6,7},{7,6},{8,9},{9,8},{10,11... | collective-permute-start | bytes 786440 | tf_op jit(solution)/shard_map/ppermute | solution.py:192
  71.1 29.4 %copy-start.2 = (bf16[512,256]{1,0:T(8,128)(2,1)S(1)}, bf16[512,256]{1,0:T(8,128)(2,1)}, u32[]{:S(2)}) copy-start(bf16[512,256]{1,0:T(8,128)(2,1)} %own.1) | copy-start | bytes 786436
  71.2 1.6 %collective-permute-start.4 = (bf16[512,256]{1,0:T(8,128)(2,1)S(1)}, bf16[512,256]{1,0:T(8,128)(2,1)S(1)}, u32[]{:S(2)}, u32[]{:S(2)}) collective-permute-start(bf16[512,256]{1,0:T(8,128)(2,1)S(1)} %sweep.1.own), channel_id=1, source_target_pairs={{0,1},{1,0},{2,3},{3,2},{4,5},{5,4},{6,7},{7,6},{8,9},{9,8},{10,11... | collective-permute-start | bytes 786440 | tf_op jit(solution)/shard_map/ppermute | solution.py:192

commit v4 on v3

--- a/solution.py
+++ b/solution.py
@@ -13,6 +13,7 @@
 F32 = jnp.float32
 VMEM = pl.BlockSpec(memory_space=pltpu.VMEM)
 SMEM = pl.BlockSpec(memory_space=pltpu.SMEM)
+PARTS = 4
 SWAP = ((0, 1), (1, 0))
 
 
@@ -58,22 +59,26 @@
     return state + source[...].astype(F32)
 
 
-def first_kernel(places, tiles, mixed, ghosts, slope, source, scaled, dense, total):
+def first_kernel(places, tiles, mixed, ghosts, slope, source, scaled, dense, total, seen):
     size = tiles.shape[1]
     out_blocks = dense.shape[0] // size
     in_blocks = dense.shape[1] // size
-    total[...] = jnp.zeros_like(total)
+    for pair in range(total.shape[0]):
+        seen[pair] = 0
 
     def step(slot, carry):
-        total[places[slot]] += tiles[slot].astype(F32)
+        place = places[slot]
+        before = jnp.where(seen[place] == 1, total[place], 0.0)
+        total[place] = before + tiles[slot].astype(F32)
+        seen[place] = 1
         return carry
 
-    lax.fori_loop(0, tiles.shape[0], step, 0)
+    lax.fori_loop(0, tiles.shape[0], step, 0, unroll=4)
     for out in range(out_blocks):
         for inp in range(in_blocks):
-            dense[out * size:(out + 1) * size, inp * size:(inp + 1) * size] = total[
-                out * in_blocks + inp
-            ].astype(BF16)
+            pair = out * in_blocks + inp
+            value = jnp.where(seen[pair] == 1, total[pair], 0.0)
+            dense[out * size:(out + 1) * size, inp * size:(inp + 1) * size] = value.astype(BF16)
     scaled[...] = (slope[...] * new_state(dense, mixed, ghosts, source)).astype(BF16)
 
 
@@ -90,7 +95,7 @@
         ),
         in_specs=[SMEM] + [VMEM] * 5,
         out_specs=(VMEM, VMEM),
-        scratch_shapes=[pltpu.VMEM((pairs + 1, size, size), F32)],
+        scratch_shapes=[pltpu.VMEM((pairs + 1, size, size), F32), pltpu.SMEM((pairs + 1,), jnp.int32)],
         compiler_params=params(24),
         name="first",
     )(places, tiles, mixed, ghosts, slope, source)
@@ -111,10 +116,14 @@
     )(dense, mixed, ghosts, slope, source)
 
 
-def last_kernel(half, dense, mixed, ghosts, slope, source, own, other, adjoint, pieces):
+def last_kernel(
+    half, dense, mixed, ghosts, slope, source, own, other, adjoint, pieces, rounded, sem
+):
     cols = mixed.shape[1]
     state = new_state(dense, mixed, ghosts, source)
-    adjoint[...] = state.astype(BF16)
+    rounded[...] = state.astype(BF16)
+    leave = pltpu.make_async_copy(rounded, adjoint, sem)
+    leave.start()
     pre_grad = (slope[...] * state).astype(BF16)
     count = pieces.shape[0] // 2
     sides = cols // 128
@@ -125,6 +134,7 @@
                 pieces[place * count + group * sides + side] = part[
                     group * 8:group * 8 + 8, side * 128:side * 128 + 128
                 ]
+    leave.wait()
 
 
 def last(half, dense, mixed, ghosts, slope, source, own, other):
@@ -136,7 +146,8 @@
             jax.ShapeDtypeStruct((2 * cols * cols // 1024, 8, 128), BF16),
         ),
         in_specs=[SMEM] + [VMEM] * 7,
-        out_specs=(VMEM, VMEM),
+        out_specs=(pl.BlockSpec(memory_space=pl.ANY), VMEM),
+        scratch_shapes=[pltpu.VMEM((rows, cols), BF16), pltpu.SemaphoreType.DMA],
         compiler_params=params(24),
         name="last",
     )(half, dense, mixed, ghosts, slope, source, own, other)
@@ -179,7 +190,6 @@
     half = lax.axis_index("feat")
     half = half.reshape(1)
     other_weight = lax.ppermute(weight, "feat", SWAP)
-    other_agg = lax.ppermute(aggregated, "feat", SWAP)
     pick = (sent_rows[:, None] == jnp.arange(rows, dtype=jnp.int32)[None, :]).astype(BF16)
     hyperbolic = jnp.tanh(preact.astype(F32))
     slope = 1.0 - hyperbolic * hyperbolic
@@ -192,12 +202,16 @@
         other = lax.ppermute(scaled, "feat", SWAP)
         mixed, outgoing = mix(half, scaled, other, weight, other_weight, pick)
         if iteration == 0:
-            outgoing, other_agg, places = lax.optimization_barrier((outgoing, other_agg, places))
+            outgoing, places = lax.optimization_barrier((outgoing, places))
+        if iteration == 1:
+            outgoing, other_agg = lax.optimization_barrier((outgoing, other_agg))
         ghosts = lax.all_to_all(
             outgoing.reshape(peers, sent // peers, cols), "dom", split_axis=0, concat_axis=0, tiled=True
         ).reshape(sent, cols)
         if iteration == 0:
             scaled, dense = first(places, tiles, mixed, ghosts, slope, grad_out)
+            scaled, aggregated = lax.optimization_barrier((scaled, aggregated))
+            other_agg = lax.ppermute(aggregated, "feat", SWAP)
         elif iteration < ITERS - 1:
             scaled = sweep(dense, mixed, ghosts, slope, grad_out)
     adjoint, pieces = last(half, dense, mixed, ghosts, slope, grad_out, aggregated, other_agg)
@@ -216,8 +230,9 @@
     grad_weight = pl.pallas_call(
         unpack_kernel,
         out_shape=jax.ShapeDtypeStruct((2 * cols, cols), F32),
-        in_specs=[VMEM],
-        out_specs=VMEM,
+        grid=(PARTS,),
+        in_specs=[pl.BlockSpec((gathered.shape[0] // PARTS, 8, 128), lambda part: (part, 0, 0))],
+        out_specs=pl.BlockSpec((2 * cols // PARTS, cols), lambda part: (part, 0)),
         compiler_params=params(16),
         name="unpack",
     )(gathered)

time: 140 us -> 140 us (level)
  no operation moved by 1% of the time
where the time goes in v4:
time: 140 us
  blocking collectives  123 us (88%)
  Pallas kernels  8.3 us (6%)
  waiting for transfers between devices  2.55 us (2%)
  other arithmetic  2.07 us (1%)
  between operations  1.44 us (1%)
    all_to_all x3, blocking collectives, shards(): lax.all_to_all(outgoing.reshape(peers, sent // peers, cols), 'dom', split...  87 us
    all_to_all x3, blocking collectives, exchange(): lax.all_to_all(blocks, 'dom', split_axis=0, concat_axis=0, tiled=True, ax...  36.4 us
  transfers between devices with their start and end apart: 5, of which 2 were waited for; matrix products, arithmetic and copies ran while one was open for 2% of the time, Pallas kernels for 1%

profile of v4, /device:TPU:8, one launch (start us, length us, event | category | flops | bytes accessed | tf_op | source)
XLA Modules:
  0.0 140.0 jit_solution(12158421372161267314)
XLA Ops:
  0.6 0.1 collective-permute-start.1
  0.7 1.2 multiply_subtract_fusion
  1.9 0.6 collective-permute-start
  3.1 0.7 compare_select_fusion.places
  3.8 0.8 copy.11
  4.6 0.1 eq.15
  4.7 0.2 fusion.pick
  4.9 0.0 collective-permute-done.1.other_w
  4.9 0.0 collective-permute-done.other
  5.0 0.0 copy-done.3
  5.0 0.0 copy-start
  5.0 0.0 copy-start.1
  5.0 0.9 mix.3
  5.9 33.7 %all_to_all.30 = bf16[128,8,256]{2,1,0:T(8,128)(2,1)S(1)} all-to-all(bf16[128,8,256]{2,1,0:T(8,128)(2,1)S(1)} %bitcast.22), channel_id=1, replica_groups=mesh['dom'=128,'feat'=2] {'dom'}, dimensions={0} | all-to-all | bytes 1048576 | tf_op jit(solution)/shard_map/all_to_all | solution.py:208
  39.6 0.0 copy-done
  39.6 2.1 %first.1 = (bf16[512,256]{1,0:T(8,128)(2,1)S(1)}, bf16[512,1536]{1,0:T(8,128)(2,1)S(1)}) custom-call(s32[64]{0:T(128)S(1)} %compare_select_fusion.places, bf16[64,128,128]{2,1,0:T(8,128)(2,1)S(1)} %copy-done.1, bf16[512,256]{1,0:T(8,128)(2,1)S(1)} %get-tuple-element.20.mixed, bf16[1024,256]{1,0:T(8,128)(2,1)S(1)} %bitcast.14, ...), custom_call_target="tpu_custom_call" | custom-call | tf_op jit(solution)/shard_map/first/pallas_call | solution.py:90
  41.7 0.1 collective-permute-start.2
  41.8 0.5 collective-permute-start.3
  42.3 1.0 collective-permute-done.2.other
  43.3 0.9 mix.4
  44.2 0.0 collective-permute-done.3.other
  44.2 26.5 %all_to_all.31 = bf16[128,8,256]{2,1,0:T(8,128)(2,1)S(1)} all-to-all(bf16[128,8,256]{2,1,0:T(8,128)(2,1)S(1)} %bitcast.20), channel_id=1, replica_groups=mesh['dom'=128,'feat'=2] {'dom'}, dimensions={0} | all-to-all | bytes 1048576 | tf_op jit(solution)/shard_map/all_to_all | solution.py:208
  70.7 0.6 sweep.1.own
  71.3 0.1 collective-permute-start.4
  71.4 1.5 %collective-permute-done.4.other = bf16[512,256]{1,0:T(8,128)(2,1)S(1)} collective-permute-done((bf16[512,256]{1,0:T(8,128)(2,1)S(1)}, bf16[512,256]{1,0:T(8,128)(2,1)S(1)}, u32[]{:S(2)}, u32[]{:S(2)}) %collective-permute-start.4) | collective-permute-done | bytes 262176 | tf_op jit(solution)/shard_map/ppermute | solution.py:202
  72.9 0.9 mix.5
  73.9 26.8 %all_to_all.32 = bf16[128,8,256]{2,1,0:T(8,128)(2,1)S(1)} all-to-all(bf16[128,8,256]{2,1,0:T(8,128)(2,1)S(1)} %bitcast.21), channel_id=1, replica_groups=mesh['dom'=128,'feat'=2] {'dom'}, dimensions={0} | all-to-all | bytes 1048576 | tf_op jit(solution)/shard_map/all_to_all | solution.py:208
  100.7 1.4 %last.1 = (bf16[512,256]{1,0:T(8,128)(2,1)}, bf16[128,8,128]{2,1,0:T(8,128)(2,1)S(1)}) custom-call(s32[1]{0:T(128)} %bitcast.half, bf16[512,1536]{1,0:T(8,128)(2,1)S(1)} %get-tuple-element.22.dense, bf16[512,256]{1,0:T(8,128)(2,1)S(1)} %get-tuple-element.29.mixed, bf16[1024,256]{1,0:T(8,128)(2,1)S(1)} %bitcast.13, f32[512,256]{1,0:T(8,128)S(1)} %get-tuple-element.34.slope, ...), custom_call_target="tpu_custom_call" | custom-call | tf_op jit(solution)/shard_map/last/pallas_call | solution.py:142
  102.1 13.0 %all_to_all.33 = bf16[128,8,128]{2,1,0:T(8,128)(2,1)S(1)} all-to-all(bf16[128,8,128]{2,1,0:T(8,128)(2,1)S(1)} %get-tuple-element.33), channel_id=1, replica_groups={{0,16,32,48,64,80,96,112,128,144,160,176,192,208,224,240},{2,18,34,50,6..., dimensions={0} | all-to-all | bytes 524288 | tf_op jit(solution)/shard_map/all_to_all | solution.py:223
  115.2 11.5 %all_to_all.34 = bf16[64,8,128]{2,1,0:T(8,128)(2,1)S(1)} all-to-all(bf16[64,8,128]{2,1,0:T(8,128)(2,1)S(1)} %bitcast.18), channel_id=1, replica_groups={{0,2,4,6,8,10,12,14},{16,18,20,22,24,26,28,30},{32,34,36,38,40,42,44,46..., dimensions={0} | all-to-all | bytes 262144 | tf_op jit(solution)/shard_map/all_to_all | solution.py:223
  126.7 11.9 %all_to_all.35.pieces = bf16[128,8,128]{2,1,0:T(8,128)(2,1)S(1)} all-to-all(bf16[128,8,128]{2,1,0:T(8,128)(2,1)S(1)} %bitcast.17), channel_id=1, replica_groups={{0,16,32,48,64,80,96,112,128,144,160,176,192,208,224,240},{2,18,34,50,6..., dimensions={0} | all-to-all | bytes 524288 | tf_op jit(solution)/shard_map/all_to_all | solution.py:223
  138.6 1.4 unpack.1
  (6 shorter events, 0.1 us)
Async XLA Ops:
  0.6 4.3 %copy-start.3 = (bf16[512,256]{1,0:T(8,128)(2,1)S(1)}, bf16[512,256]{1,0:T(8,128)(2,1)}, u32[]{:S(2)}) copy-start(bf16[512,256]{1,0:T(8,128)(2,1)} %own_w.5) | copy-start | bytes 786436
  0.6 4.3 %collective-permute-start.1 = (bf16[512,256]{1,0:T(8,128)(2,1)}, bf16[512,256]{1,0:T(8,128)(2,1)S(1)}, u32[]{:S(2)}, u32[]{:S(2)}) collective-permute-start(bf16[512,256]{1,0:T(8,128)(2,1)} %own_w.5), channel_id=1, source_target_pairs={{0,1},{1,0},{2,3},{3,2},{4,5},{5,4},{6,7},{7,6},{8,9},{9,8},{10,11... | collective-permute-start | bytes 786440 | tf_op jit(solution)/shard_map/ppermute | solution.py:192
  1.9 3.0 %collective-permute-start = (bf16[512,256]{1,0:T(8,128)(2,1)S(1)}, bf16[512,256]{1,0:T(8,128)(2,1)S(1)}, u32[]{:S(2)}, u32[]{:S(2)}) collective-permute-start(bf16[512,256]{1,0:T(8,128)(2,1)S(1)} %get-tuple-element.35.own), channel_id=1, source_target_pairs={{0,1},{1,0},{2,3},{3,2},{4,5},{5,4},{6,7},{7,6},{8,9},{9,8},{10,11... | collective-permute-start | bytes 786440 | tf_op jit(solution)/shard_map/ppermute | solution.py:202
  5.0 34.6 %copy-start = (bf16[512,256]{1,0:T(8,128)(2,1)S(1)}, bf16[512,256]{1,0:T(8,128)(2,1)}, u32[]{:S(2)}) copy-start(bf16[512,256]{1,0:T(8,128)(2,1)} %source.5) | copy-start | bytes 786436
  5.0 34.6 %copy-start.1 = (bf16[64,128,128]{2,1,0:T(8,128)(2,1)S(1)}, bf16[64,128,128]{2,1,0:T(8,128)(2,1)}, u32[]{:S(2)}) copy-start(bf16[64,128,128]{2,1,0:T(8,128)(2,1)} %tiles.1) | copy-start | bytes 6291460
  39.6 2.2 %copy-start.2 = (bf16[512,256]{1,0:T(8,128)(2,1)S(1)}, bf16[512,256]{1,0:T(8,128)(2,1)}, u32[]{:S(2)}) copy-start(bf16[512,256]{1,0:T(8,128)(2,1)} %own) | copy-start | bytes 786436
  41.7 1.6 %collective-permute-start.2 = (bf16[512,256]{1,0:T(8,128)(2,1)S(1)}, bf16[512,256]{1,0:T(8,128)(2,1)S(1)}, u32[]{:S(2)}, u32[]{:S(2)}) collective-permute-start(bf16[512,256]{1,0:T(8,128)(2,1)S(1)} %get-tuple-element.24.own), channel_id=1, source_target_pairs={{0,1},{1,0},{2,3},{3,2},{4,5},{5,4},{6,7},{7,6},{8,9},{9,8},{10,11... | collective-permute-start | bytes 786440 | tf_op jit(solution)/shard_map/ppermute | solution.py:202
  41.8 2.4 %collective-permute-start.3 = (bf16[512,256]{1,0:T(8,128)(2,1)S(1)}, bf16[512,256]{1,0:T(8,128)(2,1)S(1)}, u32[]{:S(2)}, u32[]{:S(2)}) collective-permute-start(bf16[512,256]{1,0:T(8,128)(2,1)S(1)} %copy-done.2), channel_id=1, source_target_pairs={{0,1},{1,0},{2,3},{3,2},{4,5},{5,4},{6,7},{7,6},{8,9},{9,8},{10,11... | collective-permute-start | bytes 786440 | tf_op jit(solution)/shard_map/ppermute | solution.py:214
  71.3 1.6 %collective-permute-start.4 = (bf16[512,256]{1,0:T(8,128)(2,1)S(1)}, bf16[512,256]{1,0:T(8,128)(2,1)S(1)}, u32[]{:S(2)}, u32[]{:S(2)}) collective-permute-start(bf16[512,256]{1,0:T(8,128)(2,1)S(1)} %sweep.1.own), channel_id=1, source_target_pairs={{0,1},{1,0},{2,3},{3,2},{4,5},{5,4},{6,7},{7,6},{8,9},{9,8},{10,11... | collective-permute-start | bytes 786440 | tf_op jit(solution)/shard_map/ppermute | solution.py:202

commit v5 on v3

--- a/solution.py
+++ b/solution.py
@@ -24,7 +24,28 @@
     return lax.dot_general(a, b, (dims, ((), ())), preferred_element_type=F32)
 
 
-def mix_kernel(half, own, other, own_w, other_w, pick, mixed, outgoing):
+def choose_kernel(wanted, pick):
+    step, rows = 2 * wanted.shape[0], pick.shape[1]
+    row = lax.broadcasted_iota(jnp.int32, (wanted.shape[0], rows), 1)
+    for pair in range(wanted.shape[1] // 2):
+        parts = [
+            (wanted[:, peer:peer + 1] == row).astype(F32) for peer in (2 * pair, 2 * pair + 1)
+        ]
+        pick[pair * step:pair * step + step, :] = jnp.concatenate(parts, axis=0).astype(BF16)
+
+
+def choose(wanted, rows):
+    return pl.pallas_call(
+        choose_kernel,
+        out_shape=jax.ShapeDtypeStruct((wanted.shape[0] * wanted.shape[1], rows), BF16),
+        in_specs=[VMEM],
+        out_specs=VMEM,
+        compiler_params=params(16),
+        name="choose",
+    )(wanted)
+
+
+def mix_kernel(half, count, own, other, own_w, other_w, pick, mixed, outgoing):
     cols = own.shape[1]
     mine = pl.ds(pl.multiple_of(half[0] * cols, cols), cols)
     value = dot(own[...], own_w[mine, :], ((1,), (1,)))
@@ -34,7 +55,7 @@
     outgoing[...] = dot(pick[...], value).astype(BF16)
 
 
-def mix(half, own, other, own_w, other_w, pick):
+def mix(half, count, own, other, own_w, other_w, pick):
     rows, cols = own.shape
     return pl.pallas_call(
         mix_kernel,
@@ -42,14 +63,14 @@
             jax.ShapeDtypeStruct((rows, cols), BF16),
             jax.ShapeDtypeStruct((pick.shape[0], cols), BF16),
         ),
-        in_specs=[SMEM] + [VMEM] * 5,
+        in_specs=[SMEM] * 2 + [VMEM] * 5,
         out_specs=(VMEM, VMEM),
         compiler_params=params(16),
         cost_estimate=pl.CostEstimate(
             flops=8 * rows * cols * (2 * cols + pick.shape[0]), bytes_accessed=5 << 19, transcendentals=0
         ),
         name="mix",
-    )(half, own, other, own_w, other_w, pick)
+    )(half, count, own, other, own_w, other_w, pick)
 
 
 def new_state(dense, mixed, ghosts, source):
@@ -58,17 +79,19 @@
     return state + source[...].astype(F32)
 
 
-def first_kernel(places, tiles, mixed, ghosts, slope, source, scaled, dense, total):
+def first_kernel(
+    count, inputs, outputs, tiles, mixed, ghosts, slope, source, scaled, dense, total
+):
     size = tiles.shape[1]
     out_blocks = dense.shape[0] // size
     in_blocks = dense.shape[1] // size
     total[...] = jnp.zeros_like(total)
 
     def step(slot, carry):
-        total[places[slot]] += tiles[slot].astype(F32)
+        total[outputs[slot] * in_blocks + inputs[slot]] += tiles[slot].astype(F32)
         return carry
 
-    lax.fori_loop(0, tiles.shape[0], step, 0)
+    lax.fori_loop(0, count[0], step, 0)
     for out in range(out_blocks):
         for inp in range(in_blocks):
             dense[out * size:(out + 1) * size, inp * size:(inp + 1) * size] = total[
@@ -77,7 +100,7 @@
     scaled[...] = (slope[...] * new_state(dense, mixed, ghosts, source)).astype(BF16)
 
 
-def first(places, tiles, mixed, ghosts, slope, source):
+def first(count, inputs, outputs, tiles, mixed, ghosts, slope, source):
     size = tiles.shape[1]
     rows = mixed.shape[0]
     across = rows + ghosts.shape[0]
@@ -88,12 +111,12 @@
             jax.ShapeDtypeStruct(mixed.shape, BF16),
             jax.ShapeDtypeStruct((rows, across), BF16),
         ),
-        in_specs=[SMEM] + [VMEM] * 5,
+        in_specs=[SMEM] * 3 + [VMEM] * 5,
         out_specs=(VMEM, VMEM),
-        scratch_shapes=[pltpu.VMEM((pairs + 1, size, size), F32)],
+        scratch_shapes=[pltpu.VMEM((pairs, size, size), F32)],
         compiler_params=params(24),
         name="first",
-    )(places, tiles, mixed, ghosts, slope, source)
+    )(count, inputs, outputs, tiles, mixed, ghosts, slope, source)
 
 
 def sweep_kernel(dense, mixed, ghosts, slope, source, scaled):
@@ -174,30 +197,28 @@
 def shards(grad_out, preact, aggregated, weight, tiles, in_block, out_block, tile_count, send_rows):
     rows, cols = grad_out.shape
     peers = lax.axis_size("dom")
-    sent_rows = send_rows[0].reshape(-1)
-    sent = sent_rows.shape[0]
+    sent = send_rows.shape[1] * send_rows.shape[2]
     half = lax.axis_index("feat")
     half = half.reshape(1)
     other_weight = lax.ppermute(weight, "feat", SWAP)
-    other_agg = lax.ppermute(aggregated, "feat", SWAP)
-    pick = (sent_rows[:, None] == jnp.arange(rows, dtype=jnp.int32)[None, :]).astype(BF16)
+    pick = choose(send_rows[0].T, rows)
     hyperbolic = jnp.tanh(preact.astype(F32))
     slope = 1.0 - hyperbolic * hyperbolic
     scaled = (slope * grad_out.astype(F32)).astype(BF16)
-    in_blocks = (rows + sent) // tiles.shape[1]
-    pairs = rows // tiles.shape[1] * in_blocks
-    slots = jnp.arange(tiles.shape[0], dtype=jnp.int32)
-    places = jnp.where(slots < tile_count[0], out_block * in_blocks + in_block, pairs)
     for iteration in range(ITERS):
         other = lax.ppermute(scaled, "feat", SWAP)
-        mixed, outgoing = mix(half, scaled, other, weight, other_weight, pick)
-        if iteration == 0:
-            outgoing, other_agg, places = lax.optimization_barrier((outgoing, other_agg, places))
+        mixed, outgoing = mix(half, tile_count, scaled, other, weight, other_weight, pick)
+        if iteration == 1:
+            outgoing, other_agg = lax.optimization_barrier((outgoing, other_agg))
         ghosts = lax.all_to_all(
             outgoing.reshape(peers, sent // peers, cols), "dom", split_axis=0, concat_axis=0, tiled=True
         ).reshape(sent, cols)
         if iteration == 0:
-            scaled, dense = first(places, tiles, mixed, ghosts, slope, grad_out)
+            scaled, dense = first(
+                tile_count, in_block, out_block, tiles, mixed, ghosts, slope, grad_out
+            )
+            scaled, aggregated = lax.optimization_barrier((scaled, aggregated))
+            other_agg = lax.ppermute(aggregated, "feat", SWAP)
         elif iteration < ITERS - 1:
             scaled = sweep(dense, mixed, ghosts, slope, grad_out)
     adjoint, pieces = last(half, dense, mixed, ghosts, slope, grad_out, aggregated, other_agg)

time: 140 us -> 139 us (level)
  transfers between devices with their start and end apart: 5 -> 5, of which waited for: 2 -> 2; matrix products, arithmetic and copies ran while one was open for 2% -> 1% of each run, Pallas kernels for 1% -> 1%
where the time goes in v5:
time: 139 us; the launch traced here: 138 us
  blocking collectives  123 us (88%)
  Pallas kernels  7.71 us (6%)
  waiting for transfers between devices  2.55 us (2%)
  between operations  1.46 us (1%)
    all_to_all x3, blocking collectives, shards(): lax.all_to_all(outgoing.reshape(peers, sent // peers, cols), 'dom', split...  86.8 us
    all_to_all x3, blocking collectives, exchange(): lax.all_to_all(blocks, 'dom', split_axis=0, concat_axis=0, tiled=True, ax...  36.4 us
    pallas_call x3, Pallas kernels, mix(): pl.pallas_call(mix_kernel, out_shape=(jax.ShapeDtypeStruct((rows, cols),...  2.78 us
  transfers between devices with their start and end apart: 5, of which 2 were waited for; matrix products, arithmetic and copies ran while one was open for 1% of the time, Pallas kernels for 1%

profile of v5, /device:TPU:8, one launch (start us, length us, event | category | flops | bytes accessed | tf_op | source)
XLA Modules:
  0.0 138.2 jit_solution(2947016475258441352)
XLA Ops:
  0.6 0.1 collective-permute-start.1
  0.7 1.2 multiply_subtract_fusion
  1.9 0.6 collective-permute-start
  3.1 0.0 copy-start.3
  3.1 0.7 copy-done.3
  3.8 0.3 choose.1.pick
  4.1 0.0 collective-permute-done.1.other_w
  4.1 0.0 collective-permute-done.other
  4.1 0.0 copy-done.6
  4.1 0.0 copy-start
  4.2 0.0 copy-start.1
  4.2 0.0 copy-start.4
  4.2 0.0 copy-start.5
  4.2 0.9 mix.3
  5.1 33.7 %all_to_all.30 = bf16[128,8,256]{2,1,0:T(8,128)(2,1)S(1)} all-to-all(bf16[128,8,256]{2,1,0:T(8,128)(2,1)S(1)} %bitcast.23), channel_id=1, replica_groups=mesh['dom'=128,'feat'=2] {'dom'}, dimensions={0} | all-to-all | bytes 1048576 | tf_op jit(solution)/shard_map/all_to_all | solution.py:213
  38.8 1.7 %first.1 = (bf16[512,256]{1,0:T(8,128)(2,1)S(1)}, bf16[512,1536]{1,0:T(8,128)(2,1)S(1)}) custom-call(s32[1]{0:T(128)S(6)} %copy.11.count, s32[64]{0:T(128)S(1)} %copy-done.4, s32[64]{0:T(128)S(1)} %copy-done.5, bf16[64,128,128]{2,1,0:T(8,128)(2,1)S(1)} %copy-done.1, bf16[512,256]{1,0:T(8,128)(2,1)S(1)} %get-tuple-element.16.mixed, ...), custom_call_target="tpu_custom_call" | custom-call | tf_op jit(solution)/shard_map/first/pallas_call | solution.py:108
  40.5 0.1 collective-permute-start.2
  40.6 0.5 collective-permute-start.3
  41.1 1.0 collective-permute-done.2.other
  42.2 0.9 mix.4
  43.1 0.0 collective-permute-done.3.other
  43.1 26.4 %all_to_all.31 = bf16[128,8,256]{2,1,0:T(8,128)(2,1)S(1)} all-to-all(bf16[128,8,256]{2,1,0:T(8,128)(2,1)S(1)} %bitcast.21), channel_id=1, replica_groups=mesh['dom'=128,'feat'=2] {'dom'}, dimensions={0} | all-to-all | bytes 1048576 | tf_op jit(solution)/shard_map/all_to_all | solution.py:213
  69.5 0.6 sweep.1.own
  70.1 0.1 collective-permute-start.4
  70.2 1.5 %collective-permute-done.4.other = bf16[512,256]{1,0:T(8,128)(2,1)S(1)} collective-permute-done((bf16[512,256]{1,0:T(8,128)(2,1)S(1)}, bf16[512,256]{1,0:T(8,128)(2,1)S(1)}, u32[]{:S(2)}, u32[]{:S(2)}) %collective-permute-start.4) | collective-permute-done | bytes 262176 | tf_op jit(solution)/shard_map/ppermute | solution.py:209
  71.7 0.9 mix.5
  72.7 26.7 %all_to_all.32 = bf16[128,8,256]{2,1,0:T(8,128)(2,1)S(1)} all-to-all(bf16[128,8,256]{2,1,0:T(8,128)(2,1)S(1)} %bitcast.22), channel_id=1, replica_groups=mesh['dom'=128,'feat'=2] {'dom'}, dimensions={0} | all-to-all | bytes 1048576 | tf_op jit(solution)/shard_map/all_to_all | solution.py:213
  99.4 1.4 %last.1 = (bf16[512,256]{1,0:T(8,128)(2,1)}, bf16[128,8,128]{2,1,0:T(8,128)(2,1)S(1)}) custom-call(s32[1]{0:T(128)} %bitcast.half, bf16[512,1536]{1,0:T(8,128)(2,1)S(1)} %get-tuple-element.18.dense, bf16[512,256]{1,0:T(8,128)(2,1)S(1)} %get-tuple-element.25.mixed, bf16[1024,256]{1,0:T(8,128)(2,1)S(1)} %bitcast.14, f32[512,256]{1,0:T(8,128)S(1)} %get-tuple-element.30.slope, ...), custom_call_target="tpu_custom_call" | custom-call | tf_op jit(solution)/shard_map/last/pallas_call | solution.py:155
  100.8 13.0 %all_to_all.33 = bf16[128,8,128]{2,1,0:T(8,128)(2,1)S(1)} all-to-all(bf16[128,8,128]{2,1,0:T(8,128)(2,1)S(1)} %get-tuple-element.29), channel_id=1, replica_groups={{0,16,32,48,64,80,96,112,128,144,160,176,192,208,224,240},{2,18,34,50,6..., dimensions={0} | all-to-all | bytes 524288 | tf_op jit(solution)/shard_map/all_to_all | solution.py:230
  113.9 11.5 %all_to_all.34 = bf16[64,8,128]{2,1,0:T(8,128)(2,1)S(1)} all-to-all(bf16[64,8,128]{2,1,0:T(8,128)(2,1)S(1)} %bitcast.19), channel_id=1, replica_groups={{0,2,4,6,8,10,12,14},{16,18,20,22,24,26,28,30},{32,34,36,38,40,42,44,46..., dimensions={0} | all-to-all | bytes 262144 | tf_op jit(solution)/shard_map/all_to_all | solution.py:230
  125.4 11.9 %all_to_all.35.pieces = bf16[128,8,128]{2,1,0:T(8,128)(2,1)S(1)} all-to-all(bf16[128,8,128]{2,1,0:T(8,128)(2,1)S(1)} %bitcast.18), channel_id=1, replica_groups={{0,16,32,48,64,80,96,112,128,144,160,176,192,208,224,240},{2,18,34,50,6..., dimensions={0} | all-to-all | bytes 524288 | tf_op jit(solution)/shard_map/all_to_all | solution.py:230
  137.3 0.8 unpack.1
  (9 shorter events, 0.1 us)
Async XLA Ops:
  0.6 3.5 %copy-start.6 = (bf16[512,256]{1,0:T(8,128)(2,1)S(1)}, bf16[512,256]{1,0:T(8,128)(2,1)}, u32[]{:S(2)}) copy-start(bf16[512,256]{1,0:T(8,128)(2,1)} %own_w.5) | copy-start | bytes 786436
  0.6 3.5 %collective-permute-start.1 = (bf16[512,256]{1,0:T(8,128)(2,1)}, bf16[512,256]{1,0:T(8,128)(2,1)S(1)}, u32[]{:S(2)}, u32[]{:S(2)}) collective-permute-start(bf16[512,256]{1,0:T(8,128)(2,1)} %own_w.5), channel_id=1, source_target_pairs={{0,1},{1,0},{2,3},{3,2},{4,5},{5,4},{6,7},{7,6},{8,9},{9,8},{10,11... | collective-permute-start | bytes 786440 | tf_op jit(solution)/shard_map/ppermute | solution.py:203
  1.9 2.2 %collective-permute-start = (bf16[512,256]{1,0:T(8,128)(2,1)S(1)}, bf16[512,256]{1,0:T(8,128)(2,1)S(1)}, u32[]{:S(2)}, u32[]{:S(2)}) collective-permute-start(bf16[512,256]{1,0:T(8,128)(2,1)S(1)} %get-tuple-element.31.own), channel_id=1, source_target_pairs={{0,1},{1,0},{2,3},{3,2},{4,5},{5,4},{6,7},{7,6},{8,9},{9,8},{10,11... | collective-permute-start | bytes 786440 | tf_op jit(solution)/shard_map/ppermute | solution.py:209
  3.1 0.7 copy-start.3
  4.1 34.6 %copy-start = (bf16[512,256]{1,0:T(8,128)(2,1)S(1)}, bf16[512,256]{1,0:T(8,128)(2,1)}, u32[]{:S(2)}) copy-start(bf16[512,256]{1,0:T(8,128)(2,1)} %source.5) | copy-start | bytes 786436
  4.2 34.6 %copy-start.1 = (bf16[64,128,128]{2,1,0:T(8,128)(2,1)S(1)}, bf16[64,128,128]{2,1,0:T(8,128)(2,1)}, u32[]{:S(2)}) copy-start(bf16[64,128,128]{2,1,0:T(8,128)(2,1)} %tiles.1) | copy-start | bytes 6291460
  4.2 34.6 %copy-start.4 = (s32[64]{0:T(128)S(1)}, s32[64]{0:T(128)}, u32[]{:S(2)}) copy-start(s32[64]{0:T(128)} %inputs.1) | copy-start | bytes 772
  4.2 34.6 %copy-start.5 = (s32[64]{0:T(128)S(1)}, s32[64]{0:T(128)}, u32[]{:S(2)}) copy-start(s32[64]{0:T(128)} %outputs.1) | copy-start | bytes 772
  38.8 1.9 %copy-start.2 = (bf16[512,256]{1,0:T(8,128)(2,1)S(1)}, bf16[512,256]{1,0:T(8,128)(2,1)}, u32[]{:S(2)}) copy-start(bf16[512,256]{1,0:T(8,128)(2,1)} %own) | copy-start | bytes 786436
  40.5 1.6 %collective-permute-start.2 = (bf16[512,256]{1,0:T(8,128)(2,1)S(1)}, bf16[512,256]{1,0:T(8,128)(2,1)S(1)}, u32[]{:S(2)}, u32[]{:S(2)}) collective-permute-start(bf16[512,256]{1,0:T(8,128)(2,1)S(1)} %get-tuple-element.20.own), channel_id=1, source_target_pairs={{0,1},{1,0},{2,3},{3,2},{4,5},{5,4},{6,7},{7,6},{8,9},{9,8},{10,11... | collective-permute-start | bytes 786440 | tf_op jit(solution)/shard_map/ppermute | solution.py:209
  40.6 2.4 %collective-permute-start.3 = (bf16[512,256]{1,0:T(8,128)(2,1)S(1)}, bf16[512,256]{1,0:T(8,128)(2,1)S(1)}, u32[]{:S(2)}, u32[]{:S(2)}) collective-permute-start(bf16[512,256]{1,0:T(8,128)(2,1)S(1)} %copy-done.2), channel_id=1, source_target_pairs={{0,1},{1,0},{2,3},{3,2},{4,5},{5,4},{6,7},{7,6},{8,9},{9,8},{10,11... | collective-permute-start | bytes 786440 | tf_op jit(solution)/shard_map/ppermute | solution.py:221
  70.1 1.6 %collective-permute-start.4 = (bf16[512,256]{1,0:T(8,128)(2,1)S(1)}, bf16[512,256]{1,0:T(8,128)(2,1)S(1)}, u32[]{:S(2)}, u32[]{:S(2)}) collective-permute-start(bf16[512,256]{1,0:T(8,128)(2,1)S(1)} %sweep.1.own), channel_id=1, source_target_pairs={{0,1},{1,0},{2,3},{3,2},{4,5},{5,4},{6,7},{7,6},{8,9},{9,8},{10,11... | collective-permute-start | bytes 786440 | tf_op jit(solution)/shard_map/ppermute | solution.py:209

commit v6 on v5

--- a/solution.py
+++ b/solution.py
@@ -22,6 +22,10 @@
 
 def dot(a, b, dims=((1,), (0,))):
     return lax.dot_general(a, b, (dims, ((), ())), preferred_element_type=F32)
+
+
+def split(size):
+    return slice(0, size // 2), slice(size // 2, size)
 
 
 def choose_kernel(wanted, pick):
@@ -48,11 +52,15 @@
 def mix_kernel(half, count, own, other, own_w, other_w, pick, mixed, outgoing):
     cols = own.shape[1]
     mine = pl.ds(pl.multiple_of(half[0] * cols, cols), cols)
-    value = dot(own[...], own_w[mine, :], ((1,), (1,)))
-    value = value + dot(other[...], other_w[mine, :], ((1,), (1,)))
-    value = value.astype(BF16)
-    mixed[...] = value
-    outgoing[...] = dot(pick[...], value).astype(BF16)
+    ends = []
+    for part in split(own.shape[0]):
+        value = dot(own[part, :], own_w[mine, :], ((1,), (1,)))
+        value = value + dot(other[part, :], other_w[mine, :], ((1,), (1,)))
+        ends.append(value.astype(BF16))
+        mixed[part, :] = ends[-1]
+    value = jnp.concatenate(ends, axis=0)
+    for part in split(pick.shape[0]):
+        outgoing[part, :] = dot(pick[part, :], value).astype(BF16)
 
 
 def mix(half, count, own, other, own_w, other_w, pick):
@@ -187,11 +195,21 @@
     return out.reshape((copies * blocks,) + terms.shape[1:])
 
 
-def unpack_kernel(pieces, grad):
+def unpack_kernel(pieces, grad, wide, sems):
     sides = grad.shape[1] // 128
-    for piece in range(pieces.shape[0]):
-        group, side = divmod(piece, sides)
-        grad[group * 8:group * 8 + 8, side * 128:side * 128 + 128] = pieces[piece].astype(F32)
+    parts = sems.shape[0]
+    run = pieces.shape[0] // parts
+    lines = grad.shape[0] // parts
+    leaves = []
+    for part in range(parts):
+        for piece in range(part * run, part * run + run):
+            group, side = divmod(piece, sides)
+            wide[group * 8:group * 8 + 8, side * 128:side * 128 + 128] = pieces[piece].astype(F32)
+        here = pl.ds(part * lines, lines)
+        leaves.append(pltpu.make_async_copy(wide.at[here], grad.at[here], sems.at[part]))
+        leaves[-1].start()
+    for leave in leaves:
+        leave.wait()
 
 
 def shards(grad_out, preact, aggregated, weight, tiles, in_block, out_block, tile_count, send_rows):
@@ -238,7 +256,11 @@
         unpack_kernel,
         out_shape=jax.ShapeDtypeStruct((2 * cols, cols), F32),
         in_specs=[VMEM],
-        out_specs=VMEM,
+        out_specs=pl.BlockSpec(memory_space=pl.ANY),
+        scratch_shapes=[
+            pltpu.VMEM((2 * cols, cols), F32),
+            pltpu.SemaphoreType.DMA((4,)),
+        ],
         compiler_params=params(16),
         name="unpack",
     )(gathered)

time: 139 us -> 138 us (level)
  no operation moved by 1% of the time
where the time goes in v6:
time: 138 us; the launch traced here: 137 us
  blocking collectives  123 us (89%)
  Pallas kernels  6.85 us (5%)
  waiting for transfers between devices  2.55 us (2%)
  between operations  1.46 us (1%)
    all_to_all x3, blocking collectives, shards(): lax.all_to_all(outgoing.reshape(peers, sent // peers, cols), 'dom', split...  87 us
    all_to_all x3, blocking collectives, exchange(): lax.all_to_all(blocks, 'dom', split_axis=0, concat_axis=0, tiled=True, ax...  36.4 us
  transfers between devices with their start and end apart: 5, of which 2 were waited for; matrix products, arithmetic and copies ran while one was open for 1% of the time, Pallas kernels for 1%

profile of v6, /device:TPU:8, one launch (start us, length us, event | category | flops | bytes accessed | tf_op | source)
XLA Modules:
  0.0 137.5 jit_solution(18044343940598116513)
XLA Ops:
  0.6 0.1 collective-permute-start.1
  0.7 1.2 multiply_subtract_fusion
  1.9 0.6 collective-permute-start
  3.1 0.0 copy-start.3
  3.1 0.7 copy-done.3
  3.8 0.3 choose.1.pick
  4.1 0.0 collective-permute-done.1.other_w
  4.1 0.0 collective-permute-done.other
  4.1 0.0 copy-start
  4.2 0.0 copy-start.1
  4.2 0.0 copy-start.4
  4.2 0.0 copy-start.5
  4.2 0.7 mix.3
  4.9 33.7 %all_to_all.30 = bf16[128,8,256]{2,1,0:T(8,128)(2,1)S(1)} all-to-all(bf16[128,8,256]{2,1,0:T(8,128)(2,1)S(1)} %bitcast.23), channel_id=1, replica_groups=mesh['dom'=128,'feat'=2] {'dom'}, dimensions={0} | all-to-all | bytes 1048576 | tf_op jit(solution)/shard_map/all_to_all | solution.py:231
  38.6 0.0 copy-done.1
  38.6 1.4 %first.1 = (bf16[512,256]{1,0:T(8,128)(2,1)S(1)}, bf16[512,1536]{1,0:T(8,128)(2,1)S(1)}) custom-call(s32[1]{0:T(128)S(6)} %copy.11.count, s32[64]{0:T(128)S(1)} %copy-done.4, s32[64]{0:T(128)S(1)} %copy-done.5, bf16[64,128,128]{2,1,0:T(8,128)(2,1)S(1)} %copy-done.1, bf16[512,256]{1,0:T(8,128)(2,1)S(1)} %get-tuple-element.16.mixed, ...), custom_call_target="tpu_custom_call" | custom-call | tf_op jit(solution)/shard_map/first/pallas_call | solution.py:116
  40.1 0.1 collective-permute-start.2
  40.2 0.5 collective-permute-start.3
  40.7 1.0 collective-permute-done.2.other
  41.7 0.7 mix.4
  42.4 0.0 collective-permute-done.3.other
  42.5 26.8 %all_to_all.31 = bf16[128,8,256]{2,1,0:T(8,128)(2,1)S(1)} all-to-all(bf16[128,8,256]{2,1,0:T(8,128)(2,1)S(1)} %bitcast.21), channel_id=1, replica_groups=mesh['dom'=128,'feat'=2] {'dom'}, dimensions={0} | all-to-all | bytes 1048576 | tf_op jit(solution)/shard_map/all_to_all | solution.py:231
  69.2 0.6 sweep.1.own
  69.8 0.1 collective-permute-start.4
  69.9 1.5 %collective-permute-done.4.other = bf16[512,256]{1,0:T(8,128)(2,1)S(1)} collective-permute-done((bf16[512,256]{1,0:T(8,128)(2,1)S(1)}, bf16[512,256]{1,0:T(8,128)(2,1)S(1)}, u32[]{:S(2)}, u32[]{:S(2)}) %collective-permute-start.4) | collective-permute-done | bytes 262176 | tf_op jit(solution)/shard_map/ppermute | solution.py:227
  71.5 0.7 mix.5
  72.2 26.5 %all_to_all.32 = bf16[128,8,256]{2,1,0:T(8,128)(2,1)S(1)} all-to-all(bf16[128,8,256]{2,1,0:T(8,128)(2,1)S(1)} %bitcast.22), channel_id=1, replica_groups=mesh['dom'=128,'feat'=2] {'dom'}, dimensions={0} | all-to-all | bytes 1048576 | tf_op jit(solution)/shard_map/all_to_all | solution.py:231
  98.7 1.4 %last.1 = (bf16[512,256]{1,0:T(8,128)(2,1)}, bf16[128,8,128]{2,1,0:T(8,128)(2,1)S(1)}) custom-call(s32[1]{0:T(128)} %bitcast.half, bf16[512,1536]{1,0:T(8,128)(2,1)S(1)} %get-tuple-element.18.dense, bf16[512,256]{1,0:T(8,128)(2,1)S(1)} %get-tuple-element.25.mixed, bf16[1024,256]{1,0:T(8,128)(2,1)S(1)} %bitcast.14, f32[512,256]{1,0:T(8,128)S(1)} %get-tuple-element.30.slope, ...), custom_call_target="tpu_custom_call" | custom-call | tf_op jit(solution)/shard_map/last/pallas_call | solution.py:163
  100.1 13.0 %all_to_all.33 = bf16[128,8,128]{2,1,0:T(8,128)(2,1)S(1)} all-to-all(bf16[128,8,128]{2,1,0:T(8,128)(2,1)S(1)} %get-tuple-element.29), channel_id=1, replica_groups={{0,16,32,48,64,80,96,112,128,144,160,176,192,208,224,240},{2,18,34,50,6..., dimensions={0} | all-to-all | bytes 524288 | tf_op jit(solution)/shard_map/all_to_all | solution.py:248
  113.2 11.5 %all_to_all.34 = bf16[64,8,128]{2,1,0:T(8,128)(2,1)S(1)} all-to-all(bf16[64,8,128]{2,1,0:T(8,128)(2,1)S(1)} %bitcast.19), channel_id=1, replica_groups={{0,2,4,6,8,10,12,14},{16,18,20,22,24,26,28,30},{32,34,36,38,40,42,44,46..., dimensions={0} | all-to-all | bytes 262144 | tf_op jit(solution)/shard_map/all_to_all | solution.py:248
  124.7 11.9 %all_to_all.35.pieces = bf16[128,8,128]{2,1,0:T(8,128)(2,1)S(1)} all-to-all(bf16[128,8,128]{2,1,0:T(8,128)(2,1)S(1)} %bitcast.18), channel_id=1, replica_groups={{0,16,32,48,64,80,96,112,128,144,160,176,192,208,224,240},{2,18,34,50,6..., dimensions={0} | all-to-all | bytes 524288 | tf_op jit(solution)/shard_map/all_to_all | solution.py:248
  136.6 0.8 unpack.1
  (9 shorter events, 0.1 us)
Async XLA Ops:
  0.6 3.5 %copy-start.6 = (bf16[512,256]{1,0:T(8,128)(2,1)S(1)}, bf16[512,256]{1,0:T(8,128)(2,1)}, u32[]{:S(2)}) copy-start(bf16[512,256]{1,0:T(8,128)(2,1)} %own_w.5) | copy-start | bytes 786436
  0.6 3.5 %collective-permute-start.1 = (bf16[512,256]{1,0:T(8,128)(2,1)}, bf16[512,256]{1,0:T(8,128)(2,1)S(1)}, u32[]{:S(2)}, u32[]{:S(2)}) collective-permute-start(bf16[512,256]{1,0:T(8,128)(2,1)} %own_w.5), channel_id=1, source_target_pairs={{0,1},{1,0},{2,3},{3,2},{4,5},{5,4},{6,7},{7,6},{8,9},{9,8},{10,11... | collective-permute-start | bytes 786440 | tf_op jit(solution)/shard_map/ppermute | solution.py:221
  1.9 2.2 %collective-permute-start = (bf16[512,256]{1,0:T(8,128)(2,1)S(1)}, bf16[512,256]{1,0:T(8,128)(2,1)S(1)}, u32[]{:S(2)}, u32[]{:S(2)}) collective-permute-start(bf16[512,256]{1,0:T(8,128)(2,1)S(1)} %get-tuple-element.31.own), channel_id=1, source_target_pairs={{0,1},{1,0},{2,3},{3,2},{4,5},{5,4},{6,7},{7,6},{8,9},{9,8},{10,11... | collective-permute-start | bytes 786440 | tf_op jit(solution)/shard_map/ppermute | solution.py:227
  3.1 0.7 copy-start.3
  4.1 34.5 %copy-start = (bf16[512,256]{1,0:T(8,128)(2,1)S(1)}, bf16[512,256]{1,0:T(8,128)(2,1)}, u32[]{:S(2)}) copy-start(bf16[512,256]{1,0:T(8,128)(2,1)} %source.5) | copy-start | bytes 786436
  4.2 34.4 %copy-start.1 = (bf16[64,128,128]{2,1,0:T(8,128)(2,1)S(1)}, bf16[64,128,128]{2,1,0:T(8,128)(2,1)}, u32[]{:S(2)}) copy-start(bf16[64,128,128]{2,1,0:T(8,128)(2,1)} %tiles.1) | copy-start | bytes 6291460
  4.2 34.4 %copy-start.4 = (s32[64]{0:T(128)S(1)}, s32[64]{0:T(128)}, u32[]{:S(2)}) copy-start(s32[64]{0:T(128)} %inputs.1) | copy-start | bytes 772
  4.2 34.4 %copy-start.5 = (s32[64]{0:T(128)S(1)}, s32[64]{0:T(128)}, u32[]{:S(2)}) copy-start(s32[64]{0:T(128)} %outputs.1) | copy-start | bytes 772
  38.6 1.6 %copy-start.2 = (bf16[512,256]{1,0:T(8,128)(2,1)S(1)}, bf16[512,256]{1,0:T(8,128)(2,1)}, u32[]{:S(2)}) copy-start(bf16[512,256]{1,0:T(8,128)(2,1)} %own) | copy-start | bytes 786436
  40.1 1.6 %collective-permute-start.2 = (bf16[512,256]{1,0:T(8,128)(2,1)S(1)}, bf16[512,256]{1,0:T(8,128)(2,1)S(1)}, u32[]{:S(2)}, u32[]{:S(2)}) collective-permute-start(bf16[512,256]{1,0:T(8,128)(2,1)S(1)} %get-tuple-element.20.own), channel_id=1, source_target_pairs={{0,1},{1,0},{2,3},{3,2},{4,5},{5,4},{6,7},{7,6},{8,9},{9,8},{10,11... | collective-permute-start | bytes 786440 | tf_op jit(solution)/shard_map/ppermute | solution.py:227
  40.2 2.3 %collective-permute-start.3 = (bf16[512,256]{1,0:T(8,128)(2,1)S(1)}, bf16[512,256]{1,0:T(8,128)(2,1)S(1)}, u32[]{:S(2)}, u32[]{:S(2)}) collective-permute-start(bf16[512,256]{1,0:T(8,128)(2,1)S(1)} %copy-done.2), channel_id=1, source_target_pairs={{0,1},{1,0},{2,3},{3,2},{4,5},{5,4},{6,7},{7,6},{8,9},{9,8},{10,11... | collective-permute-start | bytes 786440 | tf_op jit(solution)/shard_map/ppermute | solution.py:239
  69.8 1.6 %collective-permute-start.4 = (bf16[512,256]{1,0:T(8,128)(2,1)S(1)}, bf16[512,256]{1,0:T(8,128)(2,1)S(1)}, u32[]{:S(2)}, u32[]{:S(2)}) collective-permute-start(bf16[512,256]{1,0:T(8,128)(2,1)S(1)} %sweep.1.own), channel_id=1, source_target_pairs={{0,1},{1,0},{2,3},{3,2},{4,5},{5,4},{6,7},{7,6},{8,9},{9,8},{10,11... | collective-permute-start | bytes 786440 | tf_op jit(solution)/shard_map/ppermute | solution.py:227

commit v7 on v6

--- a/solution.py
+++ b/solution.py
@@ -49,7 +49,7 @@
     )(wanted)
 
 
-def mix_kernel(half, count, own, other, own_w, other_w, pick, mixed, outgoing):
+def mix_kernel(half, own, other, own_w, other_w, pick, mixed, outgoing):
     cols = own.shape[1]
     mine = pl.ds(pl.multiple_of(half[0] * cols, cols), cols)
     ends = []
@@ -63,7 +63,7 @@
         outgoing[part, :] = dot(pick[part, :], value).astype(BF16)
 
 
-def mix(half, count, own, other, own_w, other_w, pick):
+def mix(half, own, other, own_w, other_w, pick):
     rows, cols = own.shape
     return pl.pallas_call(
         mix_kernel,
@@ -71,14 +71,14 @@
             jax.ShapeDtypeStruct((rows, cols), BF16),
             jax.ShapeDtypeStruct((pick.shape[0], cols), BF16),
         ),
-        in_specs=[SMEM] * 2 + [VMEM] * 5,
+        in_specs=[SMEM] + [VMEM] * 5,
         out_specs=(VMEM, VMEM),
         compiler_params=params(16),
         cost_estimate=pl.CostEstimate(
             flops=8 * rows * cols * (2 * cols + pick.shape[0]), bytes_accessed=5 << 19, transcendentals=0
         ),
         name="mix",
-    )(half, count, own, other, own_w, other_w, pick)
+    )(half, own, other, own_w, other_w, pick)
 
 
 def new_state(dense, mixed, ghosts, source):
@@ -87,9 +87,7 @@
     return state + source[...].astype(F32)
 
 
-def first_kernel(
-    count, inputs, outputs, tiles, mixed, ghosts, slope, source, scaled, dense, total
-):
+def densify_kernel(count, inputs, outputs, tiles, dense, total):
     size = tiles.shape[1]
     out_blocks = dense.shape[0] // size
     in_blocks = dense.shape[1] // size
@@ -105,26 +103,21 @@
             dense[out * size:(out + 1) * size, inp * size:(inp + 1) * size] = total[
                 out * in_blocks + inp
             ].astype(BF16)
-    scaled[...] = (slope[...] * new_state(dense, mixed, ghosts, source)).astype(BF16)
-
-
-def first(count, inputs, outputs, tiles, mixed, ghosts, slope, source):
+
+
+def densify(count, inputs, outputs, tiles, rows, across):
     size = tiles.shape[1]
-    rows = mixed.shape[0]
-    across = rows + ghosts.shape[0]
     pairs = rows * across // (size * size)
     return pl.pallas_call(
-        first_kernel,
-        out_shape=(
-            jax.ShapeDtypeStruct(mixed.shape, BF16),
-            jax.ShapeDtypeStruct((rows, across), BF16),
-        ),
-        in_specs=[SMEM] * 3 + [VMEM] * 5,
-        out_specs=(VMEM, VMEM),
+        densify_kernel,
+        out_shape=jax.ShapeDtypeStruct((rows, across), BF16),
+        in_specs=[SMEM] * 3 + [VMEM],
+        out_specs=VMEM,
         scratch_shapes=[pltpu.VMEM((pairs, size, size), F32)],
-        compiler_params=params(24),
-        name="first",
-    )(count, inputs, outputs, tiles, mixed, ghosts, slope, source)
+        compiler_params=params(8),
+        cost_estimate=pl.CostEstimate(flops=1 << 22, bytes_accessed=4 << 20, transcendentals=0),
+        name="densify",
+    )(count, inputs, outputs, tiles)
 
 
 def sweep_kernel(dense, mixed, ghosts, slope, source, scaled):
@@ -225,16 +218,17 @@
     scaled = (slope * grad_out.astype(F32)).astype(BF16)
     for iteration in range(ITERS):
         other = lax.ppermute(scaled, "feat", SWAP)
-        mixed, outgoing = mix(half, tile_count, scaled, other, weight, other_weight, pick)
+        mixed, outgoing = mix(half, scaled, other, weight, other_weight, pick)
         if iteration == 1:
             outgoing, other_agg = lax.optimization_barrier((outgoing, other_agg))
         ghosts = lax.all_to_all(
             outgoing.reshape(peers, sent // peers, cols), "dom", split_axis=0, concat_axis=0, tiled=True
         ).reshape(sent, cols)
         if iteration == 0:
-            scaled, dense = first(
-                tile_count, in_block, out_block, tiles, mixed, ghosts, slope, grad_out
-            )
+            dense = densify(tile_count, in_block, out_block, tiles, rows, rows + sent)
+            mixed = pltpu.with_memory_space_constraint(mixed, pltpu.VMEM)
+            ghosts = pltpu.with_memory_space_constraint(ghosts, pltpu.VMEM)
+            scaled = sweep(dense, mixed, ghosts, slope, grad_out)
             scaled, aggregated = lax.optimization_barrier((scaled, aggregated))
             other_agg = lax.ppermute(aggregated, "feat", SWAP)
         elif iteration < ITERS - 1:

time: 138 us -> 138 us (level)
  blocking collectives: 123 us -> 90 us
  starting transfers between devices: 1.35 us -> 16.7 us
  waiting for transfers between devices: 2.55 us -> 17.9 us
  local copies, waits for them, and re-layouts: 0.72 us -> 2.32 us
    all_to_all x3 -> x2, blocking collectives: 87 us -> 53.5 us  [shards(): lax.all_to_all(outgoing.reshape(peers, sent // peers, cols), 'dom', split...]
    all_to_all x0 -> x1, starting transfers between devices: none -> 15.3 us  [shards(): lax.all_to_all(outgoing.reshape(peers, sent // peers, cols), 'dom', split...]
    all_to_all x0 -> x1, waiting for transfers between devices: none -> 15.2 us  [shards(): lax.all_to_all(outgoing.reshape(peers, sent // peers, cols), 'dom', split...]
    unnamed x14 -> x24, local copies, waits for them, and re-layouts: 0.72 us -> 2.32 us
  transfers between devices with their start and end apart: 5 -> 6, of which waited for: 2 -> 4; matrix products, arithmetic and copies ran while one was open for 1% -> 1% of each run, Pallas kernels for 1% -> 2%
where the time goes in v7:
time: 138 us; the launch traced here: 137 us
  blocking collectives  90 us (65%)
  waiting for transfers between devices  17.9 us (13%)
  starting transfers between devices  16.7 us (12%)
  Pallas kernels  7.85 us (6%)
  local copies, waits for them, and re-layouts  2.32 us (2%)
  between operations  1.51 us (1%)
    all_to_all x2, blocking collectives, shards(): lax.all_to_all(outgoing.reshape(peers, sent // peers, cols), 'dom', split...  53.5 us
    all_to_all x3, blocking collectives, exchange(): lax.all_to_all(blocks, 'dom', split_axis=0, concat_axis=0, tiled=True, ax...  36.4 us
    all_to_all x1, starting transfers between devices, shards(): lax.all_to_all(outgoing.reshape(peers, sent // peers, cols), 'dom', split...  15.3 us
    all_to_all x1, waiting for transfers between devices, shards(): lax.all_to_all(outgoing.reshape(peers, sent // peers, cols), 'dom', split...  15.2 us
    pallas_call x3, Pallas kernels, mix(): pl.pallas_call(mix_kernel, out_shape=(jax.ShapeDtypeStruct((rows, cols),...  3.01 us
  transfers between devices with their start and end apart: 6, of which 4 were waited for; matrix products, arithmetic and copies ran while one was open for 1% of the time, Pallas kernels for 2%

profile of v7, /device:TPU:8, one launch (start us, length us, event | category | flops | bytes accessed | tf_op | source)
XLA Modules:
  0.0 137.4 jit_solution(2077739128513076657)
XLA Ops:
  0.6 0.0 copy-start.8
  0.6 0.1 collective-permute-start.1
  0.7 1.2 multiply_subtract_fusion
  1.9 0.6 collective-permute-start
  2.5 0.7 copy-done.5
  3.2 0.3 choose.1.pick
  3.5 0.0 copy-start.10
  3.5 0.1 collective-permute-done.other
  3.6 1.5 %mix.3 = (bf16[512,256]{1,0:T(8,128)(2,1)S(1)}, bf16[1024,256]{1,0:T(8,128)(2,1)}) custom-call(s32[1]{0:T(128)} %bitcast.half, bf16[512,256]{1,0:T(8,128)(2,1)S(1)} %get-tuple-element.27.own, bf16[512,256]{1,0:T(8,128)(2,1)S(1)} %collective-permute-done.other, bf16[512,256]{1,0:T(8,128)(2,1)S(1)} %copy-done.8, ...), custom_call_target="tpu_custom_call" | custom-call | flops 1610612736 | bytes 2621440 | tf_op jit(solution)/shard_map/mix/pallas_call | solution.py:68
  5.2 15.3 %all-to-all-start = ((bf16[128,8,256]{2,1,0:T(8,128)(2,1)}), bf16[128,8,256]{2,1,0:T(8,128)(2,1)S(1)}, u32[]{:S(2)}, u32[]{:S(2)}) async-start(bf16[128,8,256]{2,1,0:T(8,128)(2,1)} %bitcast.3), calls=%async_computation | async-start | bytes 1048576 | tf_op jit(solution)/shard_map/all_to_all | solution.py:224
  20.5 0.0 copy-start
  21.3 0.0 copy-start.1
  21.3 1.6 %copy-done.1 = bf16[64,128,128]{2,1,0:T(8,128)(2,1)S(1)} copy-done((bf16[64,128,128]{2,1,0:T(8,128)(2,1)S(1)}, bf16[64,128,128]{2,1,0:T(8,128)(2,1)}, u32[]{:S(2)}) %copy-start.1) | copy-done | bytes 2097176
  22.9 1.1 densify.1.dense
  24.0 0.0 copy-start.4
  24.0 15.2 %all-to-all-done = bf16[128,8,256]{2,1,0:T(8,128)(2,1)S(1)} async-done(((bf16[128,8,256]{2,1,0:T(8,128)(2,1)}), bf16[128,8,256]{2,1,0:T(8,128)(2,1)S(1)}, u32[]{:S(2)}, u32[]{:S(2)}) %all-to-all-start) | async-done | bytes 524320 | tf_op jit(solution)/shard_map/all_to_all | solution.py:224
  39.2 0.6 sweep.2.own
  39.8 0.1 collective-permute-start.2
  39.9 0.5 collective-permute-start.3
  40.4 1.0 collective-permute-done.2.other
  41.4 0.7 mix.4
  42.1 26.8 %all_to_all.30 = bf16[128,8,256]{2,1,0:T(8,128)(2,1)S(1)} all-to-all(bf16[128,8,256]{2,1,0:T(8,128)(2,1)S(1)} %bitcast.21), channel_id=1, replica_groups=mesh['dom'=128,'feat'=2] {'dom'}, dimensions={0} | all-to-all | bytes 1048576 | tf_op jit(solution)/shard_map/all_to_all | solution.py:224
  68.9 0.6 sweep.3.own
  69.5 0.1 collective-permute-start.4
  69.6 1.5 %collective-permute-done.4.other = bf16[512,256]{1,0:T(8,128)(2,1)S(1)} collective-permute-done((bf16[512,256]{1,0:T(8,128)(2,1)S(1)}, bf16[512,256]{1,0:T(8,128)(2,1)S(1)}, u32[]{:S(2)}, u32[]{:S(2)}) %collective-permute-start.4) | collective-permute-done | bytes 262176 | tf_op jit(solution)/shard_map/ppermute | solution.py:220
  71.1 0.7 mix.5
  71.8 26.8 %all_to_all.31 = bf16[128,8,256]{2,1,0:T(8,128)(2,1)S(1)} all-to-all(bf16[128,8,256]{2,1,0:T(8,128)(2,1)S(1)} %bitcast.22), channel_id=1, replica_groups=mesh['dom'=128,'feat'=2] {'dom'}, dimensions={0} | all-to-all | bytes 1048576 | tf_op jit(solution)/shard_map/all_to_all | solution.py:224
  98.6 1.4 %last.1 = (bf16[512,256]{1,0:T(8,128)(2,1)}, bf16[128,8,128]{2,1,0:T(8,128)(2,1)S(1)}) custom-call(s32[1]{0:T(128)} %bitcast.half, bf16[512,1536]{1,0:T(8,128)(2,1)S(1)} %densify.1.dense, bf16[512,256]{1,0:T(8,128)(2,1)S(1)} %get-tuple-element.21.mixed, bf16[1024,256]{1,0:T(8,128)(2,1)S(1)} %bitcast.15, f32[512,256]{1,0:T(8,128)S(1)} %get-tuple-element.26.slope, ...), custom_call_target="tpu_custom_call" | custom-call | tf_op jit(solution)/shard_map/last/pallas_call | solution.py:156
  100.1 13.0 %all_to_all.32 = bf16[128,8,128]{2,1,0:T(8,128)(2,1)S(1)} all-to-all(bf16[128,8,128]{2,1,0:T(8,128)(2,1)S(1)} %get-tuple-element.25), channel_id=1, replica_groups={{0,16,32,48,64,80,96,112,128,144,160,176,192,208,224,240},{2,18,34,50,6..., dimensions={0} | all-to-all | bytes 524288 | tf_op jit(solution)/shard_map/all_to_all | solution.py:242
  113.1 11.5 %all_to_all.33 = bf16[64,8,128]{2,1,0:T(8,128)(2,1)S(1)} all-to-all(bf16[64,8,128]{2,1,0:T(8,128)(2,1)S(1)} %bitcast.19), channel_id=1, replica_groups={{0,2,4,6,8,10,12,14},{16,18,20,22,24,26,28,30},{32,34,36,38,40,42,44,46..., dimensions={0} | all-to-all | bytes 262144 | tf_op jit(solution)/shard_map/all_to_all | solution.py:242
  124.6 11.9 %all_to_all.34.pieces = bf16[128,8,128]{2,1,0:T(8,128)(2,1)S(1)} all-to-all(bf16[128,8,128]{2,1,0:T(8,128)(2,1)S(1)} %bitcast.18), channel_id=1, replica_groups={{0,16,32,48,64,80,96,112,128,144,160,176,192,208,224,240},{2,18,34,50,6..., dimensions={0} | all-to-all | bytes 524288 | tf_op jit(solution)/shard_map/all_to_all | solution.py:242
  136.6 0.8 unpack.1
  (21 shorter events, 0.1 us)
Async XLA Ops:
  0.6 3.0 %copy-start.8 = (bf16[512,256]{1,0:T(8,128)(2,1)S(1)}, bf16[512,256]{1,0:T(8,128)(2,1)}, u32[]{:S(2)}) copy-start(bf16[512,256]{1,0:T(8,128)(2,1)} %own_w.5) | copy-start | bytes 786436
  0.6 2.8 %collective-permute-start.1 = (bf16[512,256]{1,0:T(8,128)(2,1)}, bf16[512,256]{1,0:T(8,128)(2,1)S(1)}, u32[]{:S(2)}, u32[]{:S(2)}) collective-permute-start(bf16[512,256]{1,0:T(8,128)(2,1)} %own_w.5), channel_id=1, source_target_pairs={{0,1},{1,0},{2,3},{3,2},{4,5},{5,4},{6,7},{7,6},{8,9},{9,8},{10,11... | collective-permute-start | bytes 786440 | tf_op jit(solution)/shard_map/ppermute | solution.py:214
  1.9 1.7 %collective-permute-start = (bf16[512,256]{1,0:T(8,128)(2,1)S(1)}, bf16[512,256]{1,0:T(8,128)(2,1)S(1)}, u32[]{:S(2)}, u32[]{:S(2)}) collective-permute-start(bf16[512,256]{1,0:T(8,128)(2,1)S(1)} %get-tuple-element.27.own), channel_id=1, source_target_pairs={{0,1},{1,0},{2,3},{3,2},{4,5},{5,4},{6,7},{7,6},{8,9},{9,8},{10,11... | collective-permute-start | bytes 786440 | tf_op jit(solution)/shard_map/ppermute | solution.py:220
  2.5 0.7 copy-start.5
  3.5 1.7 %copy-start.2 = (bf16[1024,512]{1,0:T(8,128)(2,1)}, bf16[1024,512]{1,0:T(8,128)(2,1)S(1)}, u32[]{:S(2)}) copy-start(bf16[1024,512]{1,0:T(8,128)(2,1)S(1)} %choose.1.pick) | copy-start | bytes 3145732
  3.5 1.7 %copy-start.10 = (bf16[512,256]{1,0:T(8,128)(2,1)}, bf16[512,256]{1,0:T(8,128)(2,1)S(1)}, u32[]{:S(2)}) copy-start(bf16[512,256]{1,0:T(8,128)(2,1)S(1)} %collective-permute-done.1.other_w) | copy-start | bytes 786436
  3.6 17.6 %copy-start.6 = (s32[64]{0:T(128)S(1)}, s32[64]{0:T(128)}, u32[]{:S(2)}) copy-start(s32[64]{0:T(128)} %inputs.1) | copy-start | bytes 772
  3.6 17.6 %copy-start.7 = (s32[64]{0:T(128)S(1)}, s32[64]{0:T(128)}, u32[]{:S(2)}) copy-start(s32[64]{0:T(128)} %outputs.1) | copy-start | bytes 772
  5.2 34.0 %all-to-all-start = ((bf16[128,8,256]{2,1,0:T(8,128)(2,1)}), bf16[128,8,256]{2,1,0:T(8,128)(2,1)S(1)}, u32[]{:S(2)}, u32[]{:S(2)}) async-start(bf16[128,8,256]{2,1,0:T(8,128)(2,1)} %bitcast.3), calls=%async_computation | async-start | bytes 1048576 | tf_op jit(solution)/shard_map/all_to_all | solution.py:224
  20.5 18.6 %copy-start = (bf16[512,256]{1,0:T(8,128)(2,1)S(1)}, bf16[512,256]{1,0:T(8,128)(2,1)}, u32[]{:S(2)}) copy-start(bf16[512,256]{1,0:T(8,128)(2,1)} %source.5) | copy-start | bytes 786436
  21.3 1.6 %copy-start.1 = (bf16[64,128,128]{2,1,0:T(8,128)(2,1)S(1)}, bf16[64,128,128]{2,1,0:T(8,128)(2,1)}, u32[]{:S(2)}) copy-start(bf16[64,128,128]{2,1,0:T(8,128)(2,1)} %tiles.1) | copy-start | bytes 6291460
  24.0 15.9 %copy-start.4 = (bf16[512,256]{1,0:T(8,128)(2,1)S(1)}, bf16[512,256]{1,0:T(8,128)(2,1)}, u32[]{:S(2)}) copy-start(bf16[512,256]{1,0:T(8,128)(2,1)} %own) | copy-start | bytes 786436
  39.2 2.2 %copy-start.3 = (bf16[1024,512]{1,0:T(8,128)(2,1)S(1)}, bf16[1024,512]{1,0:T(8,128)(2,1)}, u32[]{:S(2)}) copy-start(bf16[1024,512]{1,0:T(8,128)(2,1)} %copy-done.2) | copy-start | bytes 3145732
  39.2 2.2 %copy-start.9 = (bf16[512,256]{1,0:T(8,128)(2,1)S(1)}, bf16[512,256]{1,0:T(8,128)(2,1)}, u32[]{:S(2)}) copy-start(bf16[512,256]{1,0:T(8,128)(2,1)} %own_w.5) | copy-start | bytes 786436
  39.2 2.2 %copy-start.11 = (bf16[512,256]{1,0:T(8,128)(2,1)S(1)}, bf16[512,256]{1,0:T(8,128)(2,1)}, u32[]{:S(2)}) copy-start(bf16[512,256]{1,0:T(8,128)(2,1)} %copy-done.10) | copy-start | bytes 786436
  39.8 1.6 %collective-permute-start.2 = (bf16[512,256]{1,0:T(8,128)(2,1)S(1)}, bf16[512,256]{1,0:T(8,128)(2,1)S(1)}, u32[]{:S(2)}, u32[]{:S(2)}) collective-permute-start(bf16[512,256]{1,0:T(8,128)(2,1)S(1)} %sweep.2.own), channel_id=1, source_target_pairs={{0,1},{1,0},{2,3},{3,2},{4,5},{5,4},{6,7},{7,6},{8,9},{9,8},{10,11... | collective-permute-start | bytes 786440 | tf_op jit(solution)/shard_map/ppermute | solution.py:220
  39.9 2.3 %collective-permute-start.3 = (bf16[512,256]{1,0:T(8,128)(2,1)S(1)}, bf16[512,256]{1,0:T(8,128)(2,1)S(1)}, u32[]{:S(2)}, u32[]{:S(2)}) collective-permute-start(bf16[512,256]{1,0:T(8,128)(2,1)S(1)} %copy-done.4), channel_id=1, source_target_pairs={{0,1},{1,0},{2,3},{3,2},{4,5},{5,4},{6,7},{7,6},{8,9},{9,8},{10,11... | collective-permute-start | bytes 786440 | tf_op jit(solution)/shard_map/ppermute | solution.py:233
  69.5 1.6 %collective-permute-start.4 = (bf16[512,256]{1,0:T(8,128)(2,1)S(1)}, bf16[512,256]{1,0:T(8,128)(2,1)S(1)}, u32[]{:S(2)}, u32[]{:S(2)}) collective-permute-start(bf16[512,256]{1,0:T(8,128)(2,1)S(1)} %sweep.3.own), channel_id=1, source_target_pairs={{0,1},{1,0},{2,3},{3,2},{4,5},{5,4},{6,7},{7,6},{8,9},{9,8},{10,11... | collective-permute-start | bytes 786440 | tf_op jit(solution)/shard_map/ppermute | solution.py:220

commit v8 on v7

--- a/solution.py
+++ b/solution.py
@@ -49,7 +49,7 @@
     )(wanted)
 
 
-def mix_kernel(half, own, other, own_w, other_w, pick, mixed, outgoing):
+def mix_kernel(half, own, other, own_w, other_w, pick, mixed, outgoing, *stage):
     cols = own.shape[1]
     mine = pl.ds(pl.multiple_of(half[0] * cols, cols), cols)
     ends = []
@@ -59,12 +59,25 @@
         ends.append(value.astype(BF16))
         mixed[part, :] = ends[-1]
     value = jnp.concatenate(ends, axis=0)
-    for part in split(pick.shape[0]):
-        outgoing[part, :] = dot(pick[part, :], value).astype(BF16)
-
-
-def mix(half, own, other, own_w, other_w, pick):
+    if not stage:
+        for part in split(pick.shape[0]):
+            outgoing[part, :] = dot(pick[part, :], value).astype(BF16)
+        return
+    staged, sems = stage
+    run = pick.shape[0] // sems.shape[0]
+    leaves = []
+    for index in range(sems.shape[0]):
+        here = pl.ds(index * run, run)
+        staged[here, :] = dot(pick[here, :], value).astype(BF16)
+        leaves.append(pltpu.make_async_copy(staged.at[here], outgoing.at[here], sems.at[index]))
+        leaves[-1].start()
+    for leave in leaves:
+        leave.wait()
+
+
+def mix(half, own, other, own_w, other_w, pick, away):
     rows, cols = own.shape
+    sent = pick.shape[0]
     return pl.pallas_call(
         mix_kernel,
         out_shape=(
@@ -72,7 +85,11 @@
             jax.ShapeDtypeStruct((pick.shape[0], cols), BF16),
         ),
         in_specs=[SMEM] + [VMEM] * 5,
-        out_specs=(VMEM, VMEM),
+        out_specs=(VMEM, pl.BlockSpec(memory_space=pl.ANY) if away else VMEM),
+        scratch_shapes=[
+            pltpu.VMEM((sent, cols), BF16),
+            pltpu.SemaphoreType.DMA((4,)),
+        ] if away else [],
         compiler_params=params(16),
         cost_estimate=pl.CostEstimate(
             flops=8 * rows * cols * (2 * cols + pick.shape[0]), bytes_accessed=5 << 19, transcendentals=0
@@ -218,7 +235,7 @@
     scaled = (slope * grad_out.astype(F32)).astype(BF16)
     for iteration in range(ITERS):
         other = lax.ppermute(scaled, "feat", SWAP)
-        mixed, outgoing = mix(half, scaled, other, weight, other_weight, pick)
+        mixed, outgoing = mix(half, scaled, other, weight, other_weight, pick, iteration == 0)
         if iteration == 1:
             outgoing, other_agg = lax.optimization_barrier((outgoing, other_agg))
         ghosts = lax.all_to_all(

time: 138 us -> 138 us (level)
  no operation moved by 1% of the time
where the time goes in v8:
time: 138 us; the launch traced here: 137 us
  blocking collectives  90 us (65%)
  waiting for transfers between devices  17.4 us (13%)
  starting transfers between devices  16.7 us (12%)
  Pallas kernels  8.26 us (6%)
  local copies, waits for them, and re-layouts  2.32 us (2%)
  between operations  1.53 us (1%)
    all_to_all x2, blocking collectives, shards(): lax.all_to_all(outgoing.reshape(peers, sent // peers, cols), 'dom', split...  53.5 us
    all_to_all x3, blocking collectives, exchange(): lax.all_to_all(blocks, 'dom', split_axis=0, concat_axis=0, tiled=True, ax...  36.4 us
    all_to_all x1, starting transfers between devices, shards(): lax.all_to_all(outgoing.reshape(peers, sent // peers, cols), 'dom', split...  15.4 us
    all_to_all x1, waiting for transfers between devices, shards(): lax.all_to_all(outgoing.reshape(peers, sent // peers, cols), 'dom', split...  14.7 us
    pallas_call x3, Pallas kernels, mix(): pl.pallas_call(mix_kernel, out_shape=(jax.ShapeDtypeStruct((rows, cols),...  2.95 us
  transfers between devices with their start and end apart: 6, of which 4 were waited for; matrix products, arithmetic and copies ran while one was open for 1% of the time, Pallas kernels for 2%

profile of v8, /device:TPU:8, one launch (start us, length us, event | category | flops | bytes accessed | tf_op | source)
XLA Modules:
  0.0 137.4 jit_solution(10063692180661702614)
XLA Ops:
  0.6 0.0 copy-start.8
  0.6 0.1 collective-permute-start.1
  0.7 1.2 multiply_subtract_fusion
  1.9 0.6 collective-permute-start
  2.5 0.7 copy-done.5
  3.2 0.3 choose.1.pick
  3.5 0.0 copy-start.10
  3.5 0.1 collective-permute-done.other
  3.6 1.5 %mix.3 = (bf16[512,256]{1,0:T(8,128)(2,1)S(1)}, bf16[1024,256]{1,0:T(8,128)(2,1)}) custom-call(s32[1]{0:T(128)} %bitcast.half, bf16[512,256]{1,0:T(8,128)(2,1)S(1)} %get-tuple-element.27.own, bf16[512,256]{1,0:T(8,128)(2,1)S(1)} %collective-permute-done.other, bf16[512,256]{1,0:T(8,128)(2,1)S(1)} %copy-done.8, ...), custom_call_target="tpu_custom_call" | custom-call | flops 1610612736 | bytes 2621440 | tf_op jit(solution)/shard_map/mix/pallas_call | solution.py:81
  5.2 15.4 %all-to-all-start = ((bf16[128,8,256]{2,1,0:T(8,128)(2,1)}), bf16[128,8,256]{2,1,0:T(8,128)(2,1)S(1)}, u32[]{:S(2)}, u32[]{:S(2)}) async-start(bf16[128,8,256]{2,1,0:T(8,128)(2,1)} %bitcast.3), calls=%async_computation | async-start | bytes 1048576 | tf_op jit(solution)/shard_map/all_to_all | solution.py:241
  20.5 0.0 copy-start
  21.2 0.0 copy-start.1
  21.3 1.6 %copy-done.1 = bf16[64,128,128]{2,1,0:T(8,128)(2,1)S(1)} copy-done((bf16[64,128,128]{2,1,0:T(8,128)(2,1)S(1)}, bf16[64,128,128]{2,1,0:T(8,128)(2,1)}, u32[]{:S(2)}) %copy-start.1) | copy-done | bytes 2097176
  22.8 1.6 %densify.1.dense = bf16[512,1536]{1,0:T(8,128)(2,1)S(1)} custom-call(s32[1]{0:T(128)S(6)} %copy.11.count, s32[64]{0:T(128)S(1)} %copy-done.6, s32[64]{0:T(128)S(1)} %copy-done.7, bf16[64,128,128]{2,1,0:T(8,128)(2,1)S(1)} %copy-done.1), custom_call_target="tpu_custom_call" | custom-call | flops 4194304 | bytes 4194304 | tf_op jit(solution)/shard_map/densify/pallas_call | solution.py:128
  24.4 0.0 copy-start.4
  24.4 14.7 %all-to-all-done = bf16[128,8,256]{2,1,0:T(8,128)(2,1)S(1)} async-done(((bf16[128,8,256]{2,1,0:T(8,128)(2,1)}), bf16[128,8,256]{2,1,0:T(8,128)(2,1)S(1)}, u32[]{:S(2)}, u32[]{:S(2)}) %all-to-all-start) | async-done | bytes 524320 | tf_op jit(solution)/shard_map/all_to_all | solution.py:241
  39.2 0.6 sweep.2.own
  39.7 0.1 collective-permute-start.2
  39.9 0.5 collective-permute-start.3
  40.3 1.0 collective-permute-done.2.other
  41.4 0.7 mix.4
  42.1 26.7 %all_to_all.30 = bf16[128,8,256]{2,1,0:T(8,128)(2,1)S(1)} all-to-all(bf16[128,8,256]{2,1,0:T(8,128)(2,1)S(1)} %bitcast.21), channel_id=1, replica_groups=mesh['dom'=128,'feat'=2] {'dom'}, dimensions={0} | all-to-all | bytes 1048576 | tf_op jit(solution)/shard_map/all_to_all | solution.py:241
  68.9 0.6 sweep.3.own
  69.5 0.1 collective-permute-start.4
  69.6 1.5 %collective-permute-done.4.other = bf16[512,256]{1,0:T(8,128)(2,1)S(1)} collective-permute-done((bf16[512,256]{1,0:T(8,128)(2,1)S(1)}, bf16[512,256]{1,0:T(8,128)(2,1)S(1)}, u32[]{:S(2)}, u32[]{:S(2)}) %collective-permute-start.4) | collective-permute-done | bytes 262176 | tf_op jit(solution)/shard_map/ppermute | solution.py:237
  71.1 0.7 mix.5
  71.8 26.8 %all_to_all.31 = bf16[128,8,256]{2,1,0:T(8,128)(2,1)S(1)} all-to-all(bf16[128,8,256]{2,1,0:T(8,128)(2,1)S(1)} %bitcast.22), channel_id=1, replica_groups=mesh['dom'=128,'feat'=2] {'dom'}, dimensions={0} | all-to-all | bytes 1048576 | tf_op jit(solution)/shard_map/all_to_all | solution.py:241
  98.6 1.4 %last.1 = (bf16[512,256]{1,0:T(8,128)(2,1)}, bf16[128,8,128]{2,1,0:T(8,128)(2,1)S(1)}) custom-call(s32[1]{0:T(128)} %bitcast.half, bf16[512,1536]{1,0:T(8,128)(2,1)S(1)} %densify.1.dense, bf16[512,256]{1,0:T(8,128)(2,1)S(1)} %get-tuple-element.21.mixed, bf16[1024,256]{1,0:T(8,128)(2,1)S(1)} %bitcast.15, f32[512,256]{1,0:T(8,128)S(1)} %get-tuple-element.26.slope, ...), custom_call_target="tpu_custom_call" | custom-call | tf_op jit(solution)/shard_map/last/pallas_call | solution.py:173
  100.0 13.0 %all_to_all.32 = bf16[128,8,128]{2,1,0:T(8,128)(2,1)S(1)} all-to-all(bf16[128,8,128]{2,1,0:T(8,128)(2,1)S(1)} %get-tuple-element.25), channel_id=1, replica_groups={{0,16,32,48,64,80,96,112,128,144,160,176,192,208,224,240},{2,18,34,50,6..., dimensions={0} | all-to-all | bytes 524288 | tf_op jit(solution)/shard_map/all_to_all | solution.py:259
  113.1 11.5 %all_to_all.33 = bf16[64,8,128]{2,1,0:T(8,128)(2,1)S(1)} all-to-all(bf16[64,8,128]{2,1,0:T(8,128)(2,1)S(1)} %bitcast.19), channel_id=1, replica_groups={{0,2,4,6,8,10,12,14},{16,18,20,22,24,26,28,30},{32,34,36,38,40,42,44,46..., dimensions={0} | all-to-all | bytes 262144 | tf_op jit(solution)/shard_map/all_to_all | solution.py:259
  124.6 11.9 %all_to_all.34.pieces = bf16[128,8,128]{2,1,0:T(8,128)(2,1)S(1)} all-to-all(bf16[128,8,128]{2,1,0:T(8,128)(2,1)S(1)} %bitcast.18), channel_id=1, replica_groups={{0,16,32,48,64,80,96,112,128,144,160,176,192,208,224,240},{2,18,34,50,6..., dimensions={0} | all-to-all | bytes 524288 | tf_op jit(solution)/shard_map/all_to_all | solution.py:259
  136.5 0.8 unpack.1
  (21 shorter events, 0.1 us)
Async XLA Ops:
  0.6 3.0 %copy-start.8 = (bf16[512,256]{1,0:T(8,128)(2,1)S(1)}, bf16[512,256]{1,0:T(8,128)(2,1)}, u32[]{:S(2)}) copy-start(bf16[512,256]{1,0:T(8,128)(2,1)} %own_w.5) | copy-start | bytes 786436
  0.6 2.8 %collective-permute-start.1 = (bf16[512,256]{1,0:T(8,128)(2,1)}, bf16[512,256]{1,0:T(8,128)(2,1)S(1)}, u32[]{:S(2)}, u32[]{:S(2)}) collective-permute-start(bf16[512,256]{1,0:T(8,128)(2,1)} %own_w.5), channel_id=1, source_target_pairs={{0,1},{1,0},{2,3},{3,2},{4,5},{5,4},{6,7},{7,6},{8,9},{9,8},{10,11... | collective-permute-start | bytes 786440 | tf_op jit(solution)/shard_map/ppermute | solution.py:231
  1.9 1.7 %collective-permute-start = (bf16[512,256]{1,0:T(8,128)(2,1)S(1)}, bf16[512,256]{1,0:T(8,128)(2,1)S(1)}, u32[]{:S(2)}, u32[]{:S(2)}) collective-permute-start(bf16[512,256]{1,0:T(8,128)(2,1)S(1)} %get-tuple-element.27.own), channel_id=1, source_target_pairs={{0,1},{1,0},{2,3},{3,2},{4,5},{5,4},{6,7},{7,6},{8,9},{9,8},{10,11... | collective-permute-start | bytes 786440 | tf_op jit(solution)/shard_map/ppermute | solution.py:237
  2.5 0.7 copy-start.5
  3.5 1.7 %copy-start.2 = (bf16[1024,512]{1,0:T(8,128)(2,1)}, bf16[1024,512]{1,0:T(8,128)(2,1)S(1)}, u32[]{:S(2)}) copy-start(bf16[1024,512]{1,0:T(8,128)(2,1)S(1)} %choose.1.pick) | copy-start | bytes 3145732
  3.5 1.7 %copy-start.10 = (bf16[512,256]{1,0:T(8,128)(2,1)}, bf16[512,256]{1,0:T(8,128)(2,1)S(1)}, u32[]{:S(2)}) copy-start(bf16[512,256]{1,0:T(8,128)(2,1)S(1)} %collective-permute-done.1.other_w) | copy-start | bytes 786436
  3.6 17.6 %copy-start.6 = (s32[64]{0:T(128)S(1)}, s32[64]{0:T(128)}, u32[]{:S(2)}) copy-start(s32[64]{0:T(128)} %inputs.1) | copy-start | bytes 772
  3.6 17.6 %copy-start.7 = (s32[64]{0:T(128)S(1)}, s32[64]{0:T(128)}, u32[]{:S(2)}) copy-start(s32[64]{0:T(128)} %outputs.1) | copy-start | bytes 772
  5.2 34.0 %all-to-all-start = ((bf16[128,8,256]{2,1,0:T(8,128)(2,1)}), bf16[128,8,256]{2,1,0:T(8,128)(2,1)S(1)}, u32[]{:S(2)}, u32[]{:S(2)}) async-start(bf16[128,8,256]{2,1,0:T(8,128)(2,1)} %bitcast.3), calls=%async_computation | async-start | bytes 1048576 | tf_op jit(solution)/shard_map/all_to_all | solution.py:241
  20.5 18.6 %copy-start = (bf16[512,256]{1,0:T(8,128)(2,1)S(1)}, bf16[512,256]{1,0:T(8,128)(2,1)}, u32[]{:S(2)}) copy-start(bf16[512,256]{1,0:T(8,128)(2,1)} %source.5) | copy-start | bytes 786436
  21.2 1.6 %copy-start.1 = (bf16[64,128,128]{2,1,0:T(8,128)(2,1)S(1)}, bf16[64,128,128]{2,1,0:T(8,128)(2,1)}, u32[]{:S(2)}) copy-start(bf16[64,128,128]{2,1,0:T(8,128)(2,1)} %tiles.1) | copy-start | bytes 6291460
  24.4 15.4 %copy-start.4 = (bf16[512,256]{1,0:T(8,128)(2,1)S(1)}, bf16[512,256]{1,0:T(8,128)(2,1)}, u32[]{:S(2)}) copy-start(bf16[512,256]{1,0:T(8,128)(2,1)} %own) | copy-start | bytes 786436
  39.1 2.2 %copy-start.3 = (bf16[1024,512]{1,0:T(8,128)(2,1)S(1)}, bf16[1024,512]{1,0:T(8,128)(2,1)}, u32[]{:S(2)}) copy-start(bf16[1024,512]{1,0:T(8,128)(2,1)} %copy-done.2) | copy-start | bytes 3145732
  39.1 2.2 %copy-start.9 = (bf16[512,256]{1,0:T(8,128)(2,1)S(1)}, bf16[512,256]{1,0:T(8,128)(2,1)}, u32[]{:S(2)}) copy-start(bf16[512,256]{1,0:T(8,128)(2,1)} %own_w.5) | copy-start | bytes 786436
  39.1 2.2 %copy-start.11 = (bf16[512,256]{1,0:T(8,128)(2,1)S(1)}, bf16[512,256]{1,0:T(8,128)(2,1)}, u32[]{:S(2)}) copy-start(bf16[512,256]{1,0:T(8,128)(2,1)} %copy-done.10) | copy-start | bytes 786436
  39.7 1.6 %collective-permute-start.2 = (bf16[512,256]{1,0:T(8,128)(2,1)S(1)}, bf16[512,256]{1,0:T(8,128)(2,1)S(1)}, u32[]{:S(2)}, u32[]{:S(2)}) collective-permute-start(bf16[512,256]{1,0:T(8,128)(2,1)S(1)} %sweep.2.own), channel_id=1, source_target_pairs={{0,1},{1,0},{2,3},{3,2},{4,5},{5,4},{6,7},{7,6},{8,9},{9,8},{10,11... | collective-permute-start | bytes 786440 | tf_op jit(solution)/shard_map/ppermute | solution.py:237
  39.9 2.3 %collective-permute-start.3 = (bf16[512,256]{1,0:T(8,128)(2,1)S(1)}, bf16[512,256]{1,0:T(8,128)(2,1)S(1)}, u32[]{:S(2)}, u32[]{:S(2)}) collective-permute-start(bf16[512,256]{1,0:T(8,128)(2,1)S(1)} %copy-done.4), channel_id=1, source_target_pairs={{0,1},{1,0},{2,3},{3,2},{4,5},{5,4},{6,7},{7,6},{8,9},{9,8},{10,11... | collective-permute-start | bytes 786440 | tf_op jit(solution)/shard_map/ppermute | solution.py:250
  69.5 1.6 %collective-permute-start.4 = (bf16[512,256]{1,0:T(8,128)(2,1)S(1)}, bf16[512,256]{1,0:T(8,128)(2,1)S(1)}, u32[]{:S(2)}, u32[]{:S(2)}) collective-permute-start(bf16[512,256]{1,0:T(8,128)(2,1)S(1)} %sweep.3.own), channel_id=1, source_target_pairs={{0,1},{1,0},{2,3},{3,2},{4,5},{5,4},{6,7},{7,6},{8,9},{9,8},{10,11... | collective-permute-start | bytes 786440 | tf_op jit(solution)/shard_map/ppermute | solution.py:237

commit v9 on v7

--- a/solution.py
+++ b/solution.py
@@ -212,7 +212,8 @@
     half = lax.axis_index("feat")
     half = half.reshape(1)
     other_weight = lax.ppermute(weight, "feat", SWAP)
-    pick = choose(send_rows[0].T, rows)
+    wanted = send_rows[0].T
+    pick = choose(wanted, rows)
     hyperbolic = jnp.tanh(preact.astype(F32))
     slope = 1.0 - hyperbolic * hyperbolic
     scaled = (slope * grad_out.astype(F32)).astype(BF16)
@@ -221,10 +222,13 @@
         mixed, outgoing = mix(half, scaled, other, weight, other_weight, pick)
         if iteration == 1:
             outgoing, other_agg = lax.optimization_barrier((outgoing, other_agg))
+        if iteration == 0:
+            outgoing, again = lax.optimization_barrier((outgoing, wanted))
         ghosts = lax.all_to_all(
             outgoing.reshape(peers, sent // peers, cols), "dom", split_axis=0, concat_axis=0, tiled=True
         ).reshape(sent, cols)
         if iteration == 0:
+            pick = choose(again, rows)
             dense = densify(tile_count, in_block, out_block, tiles, rows, rows + sent)
             mixed = pltpu.with_memory_space_constraint(mixed, pltpu.VMEM)
             ghosts = pltpu.with_memory_space_constraint(ghosts, pltpu.VMEM)

time: 138 us -> 138 us (level)
  no operation moved by 1% of the time
where the time goes in v9:
time: 138 us; the launch traced here: 137 us
  blocking collectives  90 us (65%)
  waiting for transfers between devices  17.3 us (13%)
  starting transfers between devices  16.7 us (12%)
  Pallas kernels  8.42 us (6%)
  local copies, waits for them, and re-layouts  2.32 us (2%)
  between operations  1.51 us (1%)
    all_to_all x2, blocking collectives, shards(): lax.all_to_all(outgoing.reshape(peers, sent // peers, cols), 'dom', split...  53.5 us
    all_to_all x3, blocking collectives, exchange(): lax.all_to_all(blocks, 'dom', split_axis=0, concat_axis=0, tiled=True, ax...  36.4 us
    all_to_all x1, starting transfers between devices, shards(): lax.all_to_all(outgoing.reshape(peers, sent // peers, cols), 'dom', split...  15.3 us
    all_to_all x1, waiting for transfers between devices, shards(): lax.all_to_all(outgoing.reshape(peers, sent // peers, cols), 'dom', split...  14.9 us
    pallas_call x3, Pallas kernels, mix(): pl.pallas_call(mix_kernel, out_shape=(jax.ShapeDtypeStruct((rows, cols),...  3.01 us
  transfers between devices with their start and end apart: 6, of which 4 were waited for; matrix products, arithmetic and copies ran while one was open for 1% of the time, Pallas kernels for 2%

profile of v9, /device:TPU:8, one launch (start us, length us, event | category | flops | bytes accessed | tf_op | source)
XLA Modules:
  0.0 137.4 jit_solution(4048474890102097681)
XLA Ops:
  0.6 0.0 copy-start.7
  0.6 0.1 collective-permute-start.1
  0.7 1.2 multiply_subtract_fusion
  1.9 0.6 collective-permute-start
  2.5 0.7 copy-done.3
  3.2 0.3 choose.2.pick
  3.5 0.0 copy-start.9
  3.5 0.2 collective-permute-done.other
  3.6 1.5 %mix.3 = (bf16[512,256]{1,0:T(8,128)(2,1)S(1)}, bf16[1024,256]{1,0:T(8,128)(2,1)}) custom-call(s32[1]{0:T(128)} %bitcast.half, bf16[512,256]{1,0:T(8,128)(2,1)S(1)} %get-tuple-element.31.own, bf16[512,256]{1,0:T(8,128)(2,1)S(1)} %collective-permute-done.other, bf16[512,256]{1,0:T(8,128)(2,1)S(1)} %copy-done.7, ...), custom_call_target="tpu_custom_call" | custom-call | flops 1610612736 | bytes 2621440 | tf_op jit(solution)/shard_map/mix/pallas_call | solution.py:68
  5.2 15.3 %all-to-all-start = ((bf16[128,8,256]{2,1,0:T(8,128)(2,1)}), bf16[128,8,256]{2,1,0:T(8,128)(2,1)S(1)}, u32[]{:S(2)}, u32[]{:S(2)}) async-start(bf16[128,8,256]{2,1,0:T(8,128)(2,1)} %bitcast.4), calls=%async_computation | async-start | bytes 1048576 | tf_op jit(solution)/shard_map/all_to_all | solution.py:227
  20.5 0.0 copy-start
  21.3 1.6 %copy-done.1 = bf16[64,128,128]{2,1,0:T(8,128)(2,1)S(1)} copy-done((bf16[64,128,128]{2,1,0:T(8,128)(2,1)S(1)}, bf16[64,128,128]{2,1,0:T(8,128)(2,1)}, u32[]{:S(2)}) %copy-start.1) | copy-done | bytes 2097176
  22.9 1.4 densify.1.dense
  24.2 0.0 copy-start.4
  24.3 14.9 %all-to-all-done = bf16[128,8,256]{2,1,0:T(8,128)(2,1)S(1)} async-done(((bf16[128,8,256]{2,1,0:T(8,128)(2,1)}), bf16[128,8,256]{2,1,0:T(8,128)(2,1)S(1)}, u32[]{:S(2)}, u32[]{:S(2)}) %all-to-all-start) | async-done | bytes 524320 | tf_op jit(solution)/shard_map/all_to_all | solution.py:227
  39.2 0.6 sweep.2.own
  39.7 0.1 collective-permute-start.2
  39.9 0.5 collective-permute-start.3
  40.3 0.3 choose.3.pick
  40.6 0.7 collective-permute-done.2.other
  41.4 0.7 mix.4
  42.1 26.7 %all_to_all.30 = bf16[128,8,256]{2,1,0:T(8,128)(2,1)S(1)} all-to-all(bf16[128,8,256]{2,1,0:T(8,128)(2,1)S(1)} %bitcast.21), channel_id=1, replica_groups=mesh['dom'=128,'feat'=2] {'dom'}, dimensions={0} | all-to-all | bytes 1048576 | tf_op jit(solution)/shard_map/all_to_all | solution.py:227
  68.9 0.6 sweep.3.own
  69.5 0.1 collective-permute-start.4
  69.6 1.5 %collective-permute-done.4.other = bf16[512,256]{1,0:T(8,128)(2,1)S(1)} collective-permute-done((bf16[512,256]{1,0:T(8,128)(2,1)S(1)}, bf16[512,256]{1,0:T(8,128)(2,1)S(1)}, u32[]{:S(2)}, u32[]{:S(2)}) %collective-permute-start.4) | collective-permute-done | bytes 262176 | tf_op jit(solution)/shard_map/ppermute | solution.py:221
  71.1 0.7 mix.5
  71.8 26.8 %all_to_all.31 = bf16[128,8,256]{2,1,0:T(8,128)(2,1)S(1)} all-to-all(bf16[128,8,256]{2,1,0:T(8,128)(2,1)S(1)} %bitcast.22), channel_id=1, replica_groups=mesh['dom'=128,'feat'=2] {'dom'}, dimensions={0} | all-to-all | bytes 1048576 | tf_op jit(solution)/shard_map/all_to_all | solution.py:227
  98.6 1.4 %last.1 = (bf16[512,256]{1,0:T(8,128)(2,1)}, bf16[128,8,128]{2,1,0:T(8,128)(2,1)S(1)}) custom-call(s32[1]{0:T(128)} %bitcast.half, bf16[512,1536]{1,0:T(8,128)(2,1)S(1)} %densify.1.dense, bf16[512,256]{1,0:T(8,128)(2,1)S(1)} %get-tuple-element.25.mixed, bf16[1024,256]{1,0:T(8,128)(2,1)S(1)} %bitcast.15, f32[512,256]{1,0:T(8,128)S(1)} %get-tuple-element.30.slope, ...), custom_call_target="tpu_custom_call" | custom-call | tf_op jit(solution)/shard_map/last/pallas_call | solution.py:156
  100.0 13.0 %all_to_all.32 = bf16[128,8,128]{2,1,0:T(8,128)(2,1)S(1)} all-to-all(bf16[128,8,128]{2,1,0:T(8,128)(2,1)S(1)} %get-tuple-element.29), channel_id=1, replica_groups={{0,16,32,48,64,80,96,112,128,144,160,176,192,208,224,240},{2,18,34,50,6..., dimensions={0} | all-to-all | bytes 524288 | tf_op jit(solution)/shard_map/all_to_all | solution.py:246
  113.1 11.5 %all_to_all.33 = bf16[64,8,128]{2,1,0:T(8,128)(2,1)S(1)} all-to-all(bf16[64,8,128]{2,1,0:T(8,128)(2,1)S(1)} %bitcast.19), channel_id=1, replica_groups={{0,2,4,6,8,10,12,14},{16,18,20,22,24,26,28,30},{32,34,36,38,40,42,44,46..., dimensions={0} | all-to-all | bytes 262144 | tf_op jit(solution)/shard_map/all_to_all | solution.py:246
  124.6 11.9 %all_to_all.34.pieces = bf16[128,8,128]{2,1,0:T(8,128)(2,1)S(1)} all-to-all(bf16[128,8,128]{2,1,0:T(8,128)(2,1)S(1)} %bitcast.18), channel_id=1, replica_groups={{0,16,32,48,64,80,96,112,128,144,160,176,192,208,224,240},{2,18,34,50,6..., dimensions={0} | all-to-all | bytes 524288 | tf_op jit(solution)/shard_map/all_to_all | solution.py:246
  136.5 0.8 unpack.1
  (20 shorter events, 0.1 us)
Async XLA Ops:
  0.6 3.0 %copy-start.7 = (bf16[512,256]{1,0:T(8,128)(2,1)S(1)}, bf16[512,256]{1,0:T(8,128)(2,1)}, u32[]{:S(2)}) copy-start(bf16[512,256]{1,0:T(8,128)(2,1)} %own_w.5) | copy-start | bytes 786436
  0.6 2.8 %collective-permute-start.1 = (bf16[512,256]{1,0:T(8,128)(2,1)}, bf16[512,256]{1,0:T(8,128)(2,1)S(1)}, u32[]{:S(2)}, u32[]{:S(2)}) collective-permute-start(bf16[512,256]{1,0:T(8,128)(2,1)} %own_w.5), channel_id=1, source_target_pairs={{0,1},{1,0},{2,3},{3,2},{4,5},{5,4},{6,7},{7,6},{8,9},{9,8},{10,11... | collective-permute-start | bytes 786440 | tf_op jit(solution)/shard_map/ppermute | solution.py:214
  1.9 1.7 %collective-permute-start = (bf16[512,256]{1,0:T(8,128)(2,1)S(1)}, bf16[512,256]{1,0:T(8,128)(2,1)S(1)}, u32[]{:S(2)}, u32[]{:S(2)}) collective-permute-start(bf16[512,256]{1,0:T(8,128)(2,1)S(1)} %get-tuple-element.31.own), channel_id=1, source_target_pairs={{0,1},{1,0},{2,3},{3,2},{4,5},{5,4},{6,7},{7,6},{8,9},{9,8},{10,11... | collective-permute-start | bytes 786440 | tf_op jit(solution)/shard_map/ppermute | solution.py:221
  2.5 0.7 copy-start.3
  3.5 1.7 %copy-start.9 = (bf16[512,256]{1,0:T(8,128)(2,1)}, bf16[512,256]{1,0:T(8,128)(2,1)S(1)}, u32[]{:S(2)}) copy-start(bf16[512,256]{1,0:T(8,128)(2,1)S(1)} %collective-permute-done.1.other_w) | copy-start | bytes 786436
  3.6 17.6 %copy-start.5 = (s32[64]{0:T(128)S(1)}, s32[64]{0:T(128)}, u32[]{:S(2)}) copy-start(s32[64]{0:T(128)} %inputs.1) | copy-start | bytes 772
  3.6 17.6 %copy-start.6 = (s32[64]{0:T(128)S(1)}, s32[64]{0:T(128)}, u32[]{:S(2)}) copy-start(s32[64]{0:T(128)} %outputs.1) | copy-start | bytes 772
  5.2 34.0 %all-to-all-start = ((bf16[128,8,256]{2,1,0:T(8,128)(2,1)}), bf16[128,8,256]{2,1,0:T(8,128)(2,1)S(1)}, u32[]{:S(2)}, u32[]{:S(2)}) async-start(bf16[128,8,256]{2,1,0:T(8,128)(2,1)} %bitcast.4), calls=%async_computation | async-start | bytes 1048576 | tf_op jit(solution)/shard_map/all_to_all | solution.py:227
  20.5 18.6 %copy-start = (bf16[512,256]{1,0:T(8,128)(2,1)S(1)}, bf16[512,256]{1,0:T(8,128)(2,1)}, u32[]{:S(2)}) copy-start(bf16[512,256]{1,0:T(8,128)(2,1)} %source.5) | copy-start | bytes 786436
  21.3 1.6 %copy-start.1 = (bf16[64,128,128]{2,1,0:T(8,128)(2,1)S(1)}, bf16[64,128,128]{2,1,0:T(8,128)(2,1)}, u32[]{:S(2)}) copy-start(bf16[64,128,128]{2,1,0:T(8,128)(2,1)} %tiles.1) | copy-start | bytes 6291460
  24.2 15.6 %copy-start.2 = (bf16[512,256]{1,0:T(8,128)(2,1)S(1)}, bf16[512,256]{1,0:T(8,128)(2,1)}, u32[]{:S(2)}) copy-start(bf16[512,256]{1,0:T(8,128)(2,1)} %own) | copy-start | bytes 786436
  24.2 16.1 %copy-start.4 = (s32[1,128,8]{1,2,0:T(8,128)S(1)}, s32[1,128,8]{1,2,0:T(8,128)}, u32[]{:S(2)}) copy-start(s32[1,128,8]{1,2,0:T(8,128)} %param.17) | copy-start | bytes 12292
  39.2 2.2 %copy-start.8 = (bf16[512,256]{1,0:T(8,128)(2,1)S(1)}, bf16[512,256]{1,0:T(8,128)(2,1)}, u32[]{:S(2)}) copy-start(bf16[512,256]{1,0:T(8,128)(2,1)} %own_w.5) | copy-start | bytes 786436
  39.2 2.2 %copy-start.10 = (bf16[512,256]{1,0:T(8,128)(2,1)S(1)}, bf16[512,256]{1,0:T(8,128)(2,1)}, u32[]{:S(2)}) copy-start(bf16[512,256]{1,0:T(8,128)(2,1)} %copy-done.9) | copy-start | bytes 786436
  39.7 1.6 %collective-permute-start.2 = (bf16[512,256]{1,0:T(8,128)(2,1)S(1)}, bf16[512,256]{1,0:T(8,128)(2,1)S(1)}, u32[]{:S(2)}, u32[]{:S(2)}) collective-permute-start(bf16[512,256]{1,0:T(8,128)(2,1)S(1)} %sweep.2.own), channel_id=1, source_target_pairs={{0,1},{1,0},{2,3},{3,2},{4,5},{5,4},{6,7},{7,6},{8,9},{9,8},{10,11... | collective-permute-start | bytes 786440 | tf_op jit(solution)/shard_map/ppermute | solution.py:221
  39.9 2.3 %collective-permute-start.3 = (bf16[512,256]{1,0:T(8,128)(2,1)S(1)}, bf16[512,256]{1,0:T(8,128)(2,1)S(1)}, u32[]{:S(2)}, u32[]{:S(2)}) collective-permute-start(bf16[512,256]{1,0:T(8,128)(2,1)S(1)} %copy-done.2), channel_id=1, source_target_pairs={{0,1},{1,0},{2,3},{3,2},{4,5},{5,4},{6,7},{7,6},{8,9},{9,8},{10,11... | collective-permute-start | bytes 786440 | tf_op jit(solution)/shard_map/ppermute | solution.py:237
  69.5 1.6 %collective-permute-start.4 = (bf16[512,256]{1,0:T(8,128)(2,1)S(1)}, bf16[512,256]{1,0:T(8,128)(2,1)S(1)}, u32[]{:S(2)}, u32[]{:S(2)}) collective-permute-start(bf16[512,256]{1,0:T(8,128)(2,1)S(1)} %sweep.3.own), channel_id=1, source_target_pairs={{0,1},{1,0},{2,3},{3,2},{4,5},{5,4},{6,7},{7,6},{8,9},{9,8},{10,11... | collective-permute-start | bytes 786440 | tf_op jit(solution)/shard_map/ppermute | solution.py:221
